TPU v7x, 32 devices: a whole 2x2x4 slice. The times are simulated.
32 devices in a mesh: dp: 4 (over z), expert: 8 (over y, x, core).
Axes of the slice: x: 2, y: 2, z: 4, core: 2. Of those that a mesh axis runs over, the one named last changes fastest.
Arguments:
- layer_in: bfloat16 [12288, 1536], P(('dp', 'expert')), may hold values from -6 to 6
- grad_out: bfloat16 [12288, 1536], P(('dp', 'expert')), may hold values from -6 to 6
- attn_gain: bfloat16 [1536], P('dp'), may hold values from 0.5 to 1.5
- query_proj: bfloat16 [1536, 1536], P('dp'), may hold values from -0.625 to 0.625
- key_proj: bfloat16 [1536, 512], P('dp'), may hold values from -0.625 to 0.625
- value_proj: bfloat16 [1536, 512], P('dp'), may hold values from -0.15625 to 0.15625
- out_proj: bfloat16 [1536, 1536], P('dp'), may hold values from -2 to 2
- ffn_gain: bfloat16 [1536], P('dp'), may hold values from 0.5 to 1.5
- router_proj: bfloat16 [1536, 16], P('dp'), may hold values from -0.3125 to 0.3125
- gate_up: bfloat16 [16, 1536, 1024], P('expert'), may hold values from -0.15625 to 0.15625
- down_proj: bfloat16 [16, 512, 1536], P('expert'), may hold values from -3 to 3
- routes: int32 [12288, 8], P(('dp', 'expert')), may hold values from 0 to 15, all different within a row
- drop_rank: int32 [32, 3072], P(('dp', 'expert')), may hold values from 0 to 3071, each once within a row
Outputs:
- layer_out: bfloat16 [12288, 1536], P(('dp', 'expert'))
- input_grad: bfloat16 [12288, 1536], P(('dp', 'expert'))
- attngain_grad: float32 [1536], P('dp')
- query_grad: float32 [1536, 1536], P('dp')
- key_grad: float32 [1536, 512], P('dp')
- value_grad: float32 [1536, 512], P('dp')
- outproj_grad: float32 [1536, 1536], P('dp')
- ffngain_grad: float32 [1536], P('dp')
- router_grad: float32 [1536, 16], P('dp')
- gateup_grad: float32 [16, 1536, 1024], P('expert')
- down_grad: float32 [16, 512, 1536], P('expert')
Inputs may be any that keep to these rules, and one draw needn't show every extreme that they name: `routes`: each row names 8 different experts. `drop_rank`: each row is a permutation of the 3072 pairs of one block.
All inputs are finite; a program needn't handle non-finite values.
Results may differ from a plain program's by a relative error of at most 0.025.
Values may be sent and summed in bfloat16 or wider, within the bound.
A program may use at most 320 MiB of HBM per device.

v0:
```python
import jax
import jax.numpy as jnp
from jax import lax
from jax.sharding import PartitionSpec as P

HEADS = 24
KV_HEADS = 8
HEAD = 64
PROMPT_DEV = 128


EPSILON = 1e-06
ATTN_SCALE = 0.015625
RESIDUAL = 0.22
ROPE_BASE = 10000.0
MASKED = -1e30


def passed_along(value, axis, steps):
    count = lax.axis_size(axis)
    initial, last = (max(0, -steps), min(count, count - steps))
    return lax.ppermute(value, axis, [(source, source + steps) for source in range(initial, last)])


def norm_forward(inputs, gain_vec):
    inverse = lax.rsqrt(jnp.mean(inputs * inputs, axis=-1, keepdims=True) + EPSILON)
    return (inputs * inverse * gain_vec, inverse)


def norm_backward(inputs, inverse, gain_vec, upstream):
    scaled = upstream * gain_vec
    middle = jnp.mean(inputs * scaled, axis=-1, keepdims=True)
    row_grad = inverse * scaled - inputs * inverse * inverse * inverse * middle
    return (row_grad, jnp.sum(upstream * inputs * inverse, axis=0))


def rotary_tables(position, head_size):
    half_size = head_size // 2
    frequency = ROPE_BASE ** (-jnp.arange(half_size, dtype=jnp.float32) * 2.0 / head_size)
    angles = position.astype(jnp.float32)[:, None] * frequency[None, :]
    return (jnp.cos(angles)[:, None, :], jnp.sin(angles)[:, None, :])


def rotate(values, cosine, sine_part):
    half_size = values.shape[-1] // 2
    lower_half = values[..., :half_size]
    upper_half = values[..., half_size:]
    return jnp.concatenate(
        [
            lower_half * cosine - upper_half * sine_part,
            upper_half * cosine + lower_half * sine_part,
        ],
        axis=-1,
    )


def unrotate(values, cosine, sine_part):
    half_size = values.shape[-1] // 2
    lower_half = values[..., :half_size]
    upper_half = values[..., half_size:]
    return jnp.concatenate(
        [
            lower_half * cosine + upper_half * sine_part,
            upper_half * cosine - lower_half * sine_part,
        ],
        axis=-1,
    )


def expert_slots(route_rows, rank_rows, experts, capacity):
    tok_rows, top_count = route_rows.shape
    pair_count = tok_rows * top_count
    expert_flat = route_rows.reshape(pair_count)
    rank_flat = rank_rows.reshape(pair_count)
    by_rank = (
        jnp.zeros((pair_count,), jnp.int32)
        .at[rank_flat]
        .set(jnp.arange(pair_count, dtype=jnp.int32))
    )
    ranked_expert = expert_flat[by_rank]
    onehot = (ranked_expert[:, None] == jnp.arange(experts, dtype=jnp.int32)[None, :]).astype(
        jnp.int32
    )
    earlier = jnp.cumsum(onehot, axis=0) - onehot
    ranked_slot = jnp.sum(earlier * onehot, axis=1)
    slot_rank = ranked_slot[rank_flat]
    kept_flag = slot_rank < capacity
    target = jnp.where(kept_flag, expert_flat * capacity + slot_rank, experts * capacity)
    source_row = jnp.arange(pair_count, dtype=jnp.int32) // top_count
    source = (
        jnp.zeros((experts * capacity + 1,), jnp.int32)
        .at[target]
        .set(source_row)[: experts * capacity]
    )
    filled = (
        jnp.zeros((experts * capacity + 1,), jnp.bfloat16).at[target].set(1.0)[: experts * capacity]
    )
    picked = jnp.minimum(target, experts * capacity - 1)
    kept_mask = kept_flag.reshape(tok_rows, top_count).astype(jnp.float32)
    return (source, filled, picked, target, kept_mask)


def on_device(
    layer_in,
    grad_out,
    attn_gain,
    query_proj,
    key_proj,
    value_proj,
    out_proj,
    ffn_gain,
    router_proj,
    gate_up,
    down_proj,
    routes,
    drop_rank,
):
    tok_rows, width = layer_in.shape
    local_experts = gate_up.shape[0]
    hidden_units = down_proj.shape[1]
    top_count = routes.shape[1]
    owner_count = lax.axis_size("expert")
    owner_index = lax.axis_index("expert")
    expert_total = local_experts * owner_count
    capacity = 5 * tok_rows * top_count // (4 * expert_total)
    prompt_rows = PROMPT_DEV
    half_rows = tok_rows - prompt_rows
    prompt_total = prompt_rows * owner_count
    head_size = HEAD
    kv_heads = KV_HEADS
    per_group = HEADS // KV_HEADS
    kv_width = kv_heads * head_size
    key_block = min(512, prompt_total)
    block_count = prompt_total // key_block
    gain_one, full_query, full_key, full_value, full_out, gain_two, full_router = (
        lax.all_gather(attn_gain, "dp", axis=0, tiled=True),
        lax.all_gather(query_proj, "dp", axis=0, tiled=True),
        lax.all_gather(key_proj, "dp", axis=0, tiled=True),
        lax.all_gather(value_proj, "dp", axis=0, tiled=True),
        lax.all_gather(out_proj, "dp", axis=0, tiled=True),
        lax.all_gather(ffn_gain, "dp", axis=0, tiled=True),
        lax.all_gather(router_proj, "dp", axis=0, tiled=True),
    )
    gain_one = gain_one.astype(jnp.float32)
    gain_two = gain_two.astype(jnp.float32)
    inputs = layer_in.astype(jnp.float32)
    normed_full, inverse_one = norm_forward(inputs, gain_one)
    normed = normed_full.astype(jnp.bfloat16)
    queries = jnp.dot(normed, full_query, preferred_element_type=jnp.float32)
    key_raw = jnp.dot(normed, full_key, preferred_element_type=jnp.float32)
    value_low = jnp.dot(normed, full_value, preferred_element_type=jnp.float32).astype(jnp.bfloat16)
    row_index = jnp.arange(tok_rows, dtype=jnp.int32)
    in_prompt = row_index < prompt_rows
    cont_rows = jnp.logical_not(in_prompt)
    parity = owner_index % 2
    position = jnp.where(
        in_prompt,
        owner_index * prompt_rows + row_index,
        prompt_total + parity * half_rows + row_index - prompt_rows,
    )
    cosine, sine_part = rotary_tables(position, head_size)
    query_low = rotate(queries.reshape(tok_rows, HEADS, head_size), cosine, sine_part).astype(
        jnp.bfloat16
    )
    key_low = (
        rotate(key_raw.reshape(tok_rows, kv_heads, head_size), cosine, sine_part)
        .astype(jnp.bfloat16)
        .reshape(tok_rows, kv_width)
    )
    query_grouped = query_low.reshape(tok_rows, kv_heads, per_group, head_size)
    prompt_keys, prompt_values = (
        lax.all_gather(key_low[:prompt_rows], "expert", axis=0, tiled=True),
        lax.all_gather(value_low[:prompt_rows], "expert", axis=0, tiled=True),
    )
    partner_keys, partner_values = passed_along(
        (key_low[prompt_rows:], value_low[prompt_rows:]), "expert", 1
    )
    tail_keys = jnp.concatenate([partner_keys, key_low[prompt_rows:]], axis=0)
    tail_values = jnp.concatenate([partner_values, value_low[prompt_rows:]], axis=0)
    block_keys = prompt_keys.reshape(block_count, key_block, kv_width)
    block_values = prompt_values.reshape(block_count, key_block, kv_width)
    block_starts = jnp.arange(block_count, dtype=jnp.int32) * key_block
    tail_index = jnp.arange(2 * half_rows, dtype=jnp.int32)
    tail_allowed = cont_rows[:, None] & jnp.where(
        tail_index[None, :] < half_rows,
        parity == 1,
        tail_index[None, :] - half_rows <= row_index[:, None] - prompt_rows,
    )

    def prompt_allowed(block_start):
        key_position = block_start + jnp.arange(key_block, dtype=jnp.int32)
        return cont_rows[:, None] | (key_position[None, :] <= position[:, None])

    def score_block(key_rows):
        keyed = key_rows.reshape(key_rows.shape[0], kv_heads, head_size)
        return ATTN_SCALE * jnp.einsum(
            "tkgd,skd->kgts", query_grouped, keyed, preferred_element_type=jnp.float32
        )

    def stats_update(running, scores, allowed):
        run_max, run_sum = running
        masked = jnp.where(allowed[None, None], scores, MASKED)
        new_max = jnp.maximum(run_max, jnp.max(masked, axis=-1))
        new_sum = run_sum * jnp.exp(run_max - new_max) + jnp.sum(
            jnp.exp(masked - new_max[..., None]), axis=-1
        )
        return (new_max, new_sum)

    def stats_step(running, block_in):
        return (stats_update(running, score_block(block_in[0]), prompt_allowed(block_in[1])), None)

    start_stats = (
        jnp.full((kv_heads, per_group, tok_rows), MASKED, jnp.float32),
        jnp.zeros((kv_heads, per_group, tok_rows), jnp.float32),
    )
    running, unused = lax.scan(stats_step, start_stats, (block_keys, block_starts))
    run_max, run_sum = stats_update(running, score_block(tail_keys), tail_allowed)
    log_total = run_max + jnp.log(run_sum)

    def prob_block(key_rows, allowed):
        return jnp.where(
            allowed[None, None], jnp.exp(score_block(key_rows) - log_total[..., None]), 0.0
        )

    def output_part(key_rows, value_rows, allowed):
        weights_low = prob_block(key_rows, allowed).astype(jnp.bfloat16)
        valued = value_rows.reshape(value_rows.shape[0], kv_heads, head_size)
        return jnp.einsum("kgts,skd->tkgd", weights_low, valued, preferred_element_type=jnp.float32)

    def output_step(running_total, block_in):
        return (
            running_total + output_part(block_in[0], block_in[1], prompt_allowed(block_in[2])),
            None,
        )

    zero_heads = jnp.zeros((tok_rows, kv_heads, per_group, head_size), jnp.float32)
    attended, unused = lax.scan(output_step, zero_heads, (block_keys, block_values, block_starts))
    attended = attended + output_part(tail_keys, tail_values, tail_allowed)
    att_low = attended.reshape(tok_rows, HEADS * head_size).astype(jnp.bfloat16)
    attn_proj = jnp.dot(att_low, full_out, preferred_element_type=jnp.float32)
    mixed_rows = inputs + RESIDUAL * attn_proj
    ffn_full, inverse_two = norm_forward(mixed_rows, gain_two)
    ffn_low = ffn_full.astype(jnp.bfloat16)
    logits = jnp.dot(ffn_low, full_router, preferred_element_type=jnp.float32)
    chosen = jnp.take_along_axis(logits, routes, axis=1)
    gate_weight = jax.nn.softmax(chosen, axis=-1)
    source, filled, picked, target, kept_mask = expert_slots(
        routes, drop_rank.reshape(tok_rows, top_count), expert_total, capacity
    )
    send_rows = (jnp.take(ffn_low, source, axis=0) * filled[:, None]).reshape(
        owner_count, local_experts, capacity, width
    )
    received = lax.all_to_all(send_rows, "expert", split_axis=0, concat_axis=0, tiled=True)
    mixed_in = jnp.einsum("sexd,edf->sexf", received, gate_up, preferred_element_type=jnp.float32)
    acted = (jax.nn.silu(mixed_in[..., :hidden_units]) * mixed_in[..., hidden_units:]).astype(
        jnp.bfloat16
    )
    produced = jnp.einsum(
        "sexf,efd->sexd", acted, down_proj, preferred_element_type=jnp.float32
    ).astype(jnp.bfloat16)
    returned = lax.all_to_all(produced, "expert", split_axis=0, concat_axis=0, tiled=True)
    returned, received, mixed_in, acted = (returned, received, mixed_in, acted)
    produced_flat = returned.reshape(expert_total * capacity, width)
    taken = jnp.take(produced_flat, picked, axis=0).reshape(tok_rows, top_count, width)
    combine_weight = gate_weight * kept_mask
    moe_rows = jnp.sum(combine_weight[:, :, None] * taken, axis=1)
    layer_out = (mixed_rows + RESIDUAL * moe_rows).astype(jnp.bfloat16)
    upstream = grad_out.astype(jnp.float32)
    moe_grad = RESIDUAL * upstream
    slot_grad = (combine_weight[:, :, None] * moe_grad[:, None, :]).astype(jnp.bfloat16)
    grad_slots = (
        jnp.zeros((expert_total * capacity + 1, width), jnp.bfloat16)
        .at[target]
        .set(slot_grad.reshape(tok_rows * top_count, width))
    )
    grad_send = grad_slots[: expert_total * capacity].reshape(
        owner_count, local_experts, capacity, width
    )
    gate_grad = jnp.sum(taken * moe_grad[:, None, :], axis=-1) * kept_mask
    chosen_grad = gate_weight * (
        gate_grad - jnp.sum(gate_weight * gate_grad, axis=1, keepdims=True)
    )
    route_onehot = (
        routes[:, :, None] == jnp.arange(expert_total, dtype=jnp.int32)[None, None, :]
    ).astype(jnp.float32)
    logit_grad = jnp.sum(route_onehot * chosen_grad[:, :, None], axis=1).astype(jnp.bfloat16)
    received_grad = lax.all_to_all(grad_send, "expert", split_axis=0, concat_axis=0, tiled=True)
    acted_grad = jnp.einsum(
        "sexd,efd->sexf", received_grad, down_proj, preferred_element_type=jnp.float32
    )
    gate_part = mixed_in[..., :hidden_units]
    up_part = mixed_in[..., hidden_units:]
    sigma = jax.nn.sigmoid(gate_part)
    mixed_grad = jnp.concatenate(
        [
            acted_grad * up_part * sigma * (1.0 + gate_part * (1.0 - sigma)),
            acted_grad * gate_part * sigma,
        ],
        axis=-1,
    ).astype(jnp.bfloat16)
    down_local = jnp.einsum(
        "sexf,sexd->efd", acted, received_grad, preferred_element_type=jnp.float32
    )
    gateup_local = jnp.einsum(
        "sexd,sexf->edf", received, mixed_grad, preferred_element_type=jnp.float32
    )
    input_rows = jnp.einsum(
        "sexf,edf->sexd", mixed_grad, gate_up, preferred_element_type=jnp.float32
    ).astype(jnp.bfloat16)
    back_rows = lax.all_to_all(input_rows, "expert", split_axis=0, concat_axis=0, tiled=True)
    gateup_grad, down_grad = (
        lax.psum(gateup_local.astype(jnp.bfloat16), "dp").astype(jnp.float32),
        lax.psum(down_local.astype(jnp.bfloat16), "dp").astype(jnp.float32),
    )
    pair_rows = jnp.take(back_rows.reshape(expert_total * capacity, width), picked, axis=0).reshape(
        tok_rows, top_count, width
    )
    router_local = jnp.einsum("td,te->de", ffn_low, logit_grad, preferred_element_type=jnp.float32)
    ffn_grad = jnp.einsum("te,de->td", logit_grad, full_router, preferred_element_type=jnp.float32)
    ffn_grad = ffn_grad + jnp.sum(kept_mask[:, :, None] * pair_rows, axis=1)
    norm_part, gain_two_local = norm_backward(mixed_rows, inverse_two, gain_two, ffn_grad)
    mixed_grad_total = upstream + norm_part
    attn_grad_low = (RESIDUAL * mixed_grad_total).astype(jnp.bfloat16)
    outproj_local = jnp.einsum(
        "tc,td->cd", att_low, attn_grad_low, preferred_element_type=jnp.float32
    )
    attended_grad = jnp.einsum(
        "td,cd->tc", attn_grad_low, full_out, preferred_element_type=jnp.float32
    ).astype(jnp.bfloat16)
    out_grad_grouped = attended_grad.reshape(tok_rows, kv_heads, per_group, head_size)
    row_delta = jnp.einsum("tkgd,tkgd->kgt", out_grad_grouped.astype(jnp.float32), attended)

    def grad_block(key_rows, value_rows, allowed):
        weights_full = prob_block(key_rows, allowed)
        keyed = key_rows.reshape(key_rows.shape[0], kv_heads, head_size)
        valued = value_rows.reshape(value_rows.shape[0], kv_heads, head_size)
        prob_grad = jnp.einsum(
            "tkgd,skd->kgts", out_grad_grouped, valued, preferred_element_type=jnp.float32
        )
        score_grad = (weights_full * (prob_grad - row_delta[..., None])).astype(jnp.bfloat16)
        query_part = jnp.einsum(
            "kgts,skd->tkgd", score_grad, keyed, preferred_element_type=jnp.float32
        )
        key_part = jnp.einsum(
            "kgts,tkgd->skd", score_grad, query_grouped, preferred_element_type=jnp.float32
        )
        value_part = jnp.einsum(
            "kgts,tkgd->skd",
            weights_full.astype(jnp.bfloat16),
            out_grad_grouped,
            preferred_element_type=jnp.float32,
        )
        return (query_part, key_part, value_part)

    def grad_step(query_total, block_in):
        query_part, key_part, value_part = grad_block(
            block_in[0], block_in[1], prompt_allowed(block_in[2])
        )
        return (query_total + query_part, (key_part, value_part))

    query_total, prompt_parts = lax.scan(
        grad_step, zero_heads, (block_keys, block_values, block_starts)
    )
    prompt_key_grad, prompt_value_grad = (
        lax.psum_scatter(
            (ATTN_SCALE * prompt_parts[0].reshape(prompt_total, kv_width)).astype(jnp.bfloat16),
            "expert",
            scatter_dimension=0,
            tiled=True,
        ).astype(jnp.float32),
        lax.psum_scatter(
            prompt_parts[1].reshape(prompt_total, kv_width).astype(jnp.bfloat16),
            "expert",
            scatter_dimension=0,
            tiled=True,
        ).astype(jnp.float32),
    )
    tail_query, tail_key_part, tail_value_part = grad_block(tail_keys, tail_values, tail_allowed)
    query_total = query_total + tail_query
    tail_key_part = ATTN_SCALE * tail_key_part.reshape(2 * half_rows, kv_width)
    tail_value_part = tail_value_part.reshape(2 * half_rows, kv_width)
    back_keys, back_values = (
        passed_along(tail_key_part[:half_rows].astype(jnp.bfloat16), "expert", -1).astype(
            jnp.float32
        ),
        passed_along(tail_value_part[:half_rows].astype(jnp.bfloat16), "expert", -1).astype(
            jnp.float32
        ),
    )
    key_grad_rot = jnp.concatenate([prompt_key_grad, tail_key_part[half_rows:] + back_keys], axis=0)
    value_grad_all = jnp.concatenate(
        [prompt_value_grad, tail_value_part[half_rows:] + back_values], axis=0
    )
    query_grad_low = (
        unrotate((ATTN_SCALE * query_total).reshape(tok_rows, HEADS, head_size), cosine, sine_part)
        .reshape(tok_rows, HEADS * head_size)
        .astype(jnp.bfloat16)
    )
    key_grad_low = (
        unrotate(key_grad_rot.reshape(tok_rows, kv_heads, head_size), cosine, sine_part)
        .reshape(tok_rows, kv_width)
        .astype(jnp.bfloat16)
    )
    value_grad_low = value_grad_all.astype(jnp.bfloat16)
    query_local = jnp.einsum(
        "td,tc->dc", normed, query_grad_low, preferred_element_type=jnp.float32
    )
    key_local = jnp.einsum("td,tc->dc", normed, key_grad_low, preferred_element_type=jnp.float32)
    value_local = jnp.einsum(
        "td,tc->dc", normed, value_grad_low, preferred_element_type=jnp.float32
    )
    normed_grad = jnp.einsum(
        "tc,dc->td", query_grad_low, full_query, preferred_element_type=jnp.float32
    )
    normed_grad = normed_grad + jnp.einsum(
        "tc,dc->td", key_grad_low, full_key, preferred_element_type=jnp.float32
    )
    normed_grad = normed_grad + jnp.einsum(
        "tc,dc->td", value_grad_low, full_value, preferred_element_type=jnp.float32
    )
    input_part, gain_one_local = norm_backward(inputs, inverse_one, gain_one, normed_grad)
    input_grad = (mixed_grad_total + input_part).astype(jnp.bfloat16)
    dense_local = (
        gain_one_local,
        query_local,
        key_local,
        value_local,
        outproj_local,
        gain_two_local,
        router_local,
    )
    dense_pieces = (
        lax.psum_scatter(
            dense_local[0].astype(jnp.bfloat16), "dp", scatter_dimension=0, tiled=True
        ).astype(jnp.float32),
        lax.psum_scatter(
            dense_local[1].astype(jnp.bfloat16), "dp", scatter_dimension=0, tiled=True
        ).astype(jnp.float32),
        lax.psum_scatter(
            dense_local[2].astype(jnp.bfloat16), "dp", scatter_dimension=0, tiled=True
        ).astype(jnp.float32),
        lax.psum_scatter(
            dense_local[3].astype(jnp.bfloat16), "dp", scatter_dimension=0, tiled=True
        ).astype(jnp.float32),
        lax.psum_scatter(
            dense_local[4].astype(jnp.bfloat16), "dp", scatter_dimension=0, tiled=True
        ).astype(jnp.float32),
        lax.psum_scatter(
            dense_local[5].astype(jnp.bfloat16), "dp", scatter_dimension=0, tiled=True
        ).astype(jnp.float32),
        lax.psum_scatter(
            dense_local[6].astype(jnp.bfloat16), "dp", scatter_dimension=0, tiled=True
        ).astype(jnp.float32),
    )
    dense_grads = (
        lax.psum(dense_pieces[0].astype(jnp.bfloat16), "expert").astype(jnp.float32),
        lax.psum(dense_pieces[1].astype(jnp.bfloat16), "expert").astype(jnp.float32),
        lax.psum(dense_pieces[2].astype(jnp.bfloat16), "expert").astype(jnp.float32),
        lax.psum(dense_pieces[3].astype(jnp.bfloat16), "expert").astype(jnp.float32),
        lax.psum(dense_pieces[4].astype(jnp.bfloat16), "expert").astype(jnp.float32),
        lax.psum(dense_pieces[5].astype(jnp.bfloat16), "expert").astype(jnp.float32),
        lax.psum(dense_pieces[6].astype(jnp.bfloat16), "expert").astype(jnp.float32),
    )
    return (
        layer_out,
        input_grad,
        dense_grads[0],
        dense_grads[1],
        dense_grads[2],
        dense_grads[3],
        dense_grads[4],
        dense_grads[5],
        dense_grads[6],
        gateup_grad,
        down_grad,
    )


def solution(mesh):
    placed = (
        P(("dp", "expert"), None),
        P(("dp", "expert"), None),
        P("dp"),
        P("dp", None),
        P("dp", None),
        P("dp", None),
        P("dp", None),
        P("dp"),
        P("dp", None),
        P("expert", None, None),
        P("expert", None, None),
        P(("dp", "expert"), None),
        P(("dp", "expert"), None),
    )
    return jax.shard_map(
        on_device,
        mesh=mesh,
        in_specs=placed,
        out_specs=(
            P(("dp", "expert"), None),
            P(("dp", "expert"), None),
            P("dp"),
            P("dp", None),
            P("dp", None),
            P("dp", None),
            P("dp", None),
            P("dp"),
            P("dp", None),
            P("expert", None, None),
            P("expert", None, None),
        ),
        check_vma=False,
    )
```

profile of v0, /device:TPU:0, one launch (start us, length us, event | category | flops | bytes accessed | tf_op | source)
XLA Modules:
  0.0 1886.2 jit_solution(682612509050585246)
XLA Ops:
  9.4 13.5 all-gather
  24.9 24.5 %all-gather.13.cloned.1.call-done = bf16[1536,512]{1,0:T(8,128)(2,1)} async-done(((bf16[384,512]{1,0:T(8,128)(2,1)}), bf16[1536,512]{1,0:T(8,128)(2,1)}) %all-gather.13.cloned.1.call-update) | async-done | bytes 1572880 | tf_op jit(solution)/shard_map/all_gather | solution.py:138
  54.0 33.0 %all-gather.9.cloned.1.call-done = bf16[1536,512]{1,0:T(8,128)(2,1)} async-done(((bf16[384,512]{1,0:T(8,128)(2,1)}), bf16[1536,512]{1,0:T(8,128)(2,1)}) %all-gather.9.cloned.1.call-update) | async-done | bytes 1572880 | tf_op jit(solution)/shard_map/all_gather | solution.py:139
  92.4 11.9 all-gather.1
  104.5 11.8 scatter_custom_fusion
  116.3 17.4 gather_fusion
  134.4 8.2 reduce-window.6
  143.8 17.4 gather_fusion.1
  161.2 11.8 scatter_custom_fusion.1
  178.9 21.7 %scatter_custom_fusion.2 = bf16[3841]{0:T(1024)(128)(2,1)S(1)} fusion(s32[3072]{0:T(1024)} %bitcast.421, bf16[3072]{0:T(1024)(128)(2,1)S(1)} %broadcast.508, bf16[]{:T(256)} %constant.188.clone.1), kind=kCustom, calls=%fused_computation.244 | custom fusion | bytes 8194 | tf_op jit(solution)/shard_map/scatter | solution.py:96
  216.3 12.2 all-gather.17.cloned.1.call-done
  236.0 42.6 %while.39 = (s32[]{:T(128)}, f32[8,3,384]{2,1,0:T(4,128)S(1)}, f32[8,3,384]{2,1,0:T(4,128)S(1)}, s32[2]{0:T(128)S(1)}, bf16[2,512,512]{1,2,0:T(8,128)(2,1)}, /*i...) while((s32[]{:T(128)}, f32[8,3,384]{2,1,0:T(4,128)S(1)}, ...), condition=%wide.region_4.5_spmd.clone, body=%wide.region_1.4_spmd.clone.sunk | while | flops 637452416 | bytes 46296996 | solution.py:216
  238.7 8.1 fusion.222
  246.8 10.3 exponential_reduce_fusion.3
  259.8 8.1 fusion.222
  267.9 10.3 exponential_reduce_fusion.3
  278.7 10.7 fusion.55
  289.4 10.2 exponential_reduce_fusion.1
  300.3 24.6 %while.40 = (s32[]{:T(128)}, f32[384,8,3,64]{0,3,2,1:T(8,128)}, bf16[2,512,512]{1,2,0:T(8,128)(2,1)}, s32[2]{0:T(128)S(1)}, bf16[2,512,512]{1,2,0:T(8,128)(2,1)}...) while((s32[]{:T(128)}, f32[384,8,3,64]{0,3,2,1:T(8,128)}, ...), condition=%wide.region_8.9_spmd.clone, body=%wide.region_7.8_spmd.clone.sunk | while | flops 1228409984 | bytes 9482131 | solution.py:237
  304.2 8.1 bitcast_add_fusion.8
  316.0 8.9 bitcast_add_fusion.8
  324.9 12.7 fusion.147
  345.7 25.5 %gather_fusion.2 = bf16[3840,1536]{1,0:T(8,128)(2,1)} fusion(bf16[384,1536]{1,0:T(8,128)(2,1)} %multiply_convert_fusion.2, s32[4096]{0:T(1024)S(1)} %copy-done.70), kind=kCustom, calls=%fused_computation.4 | custom fusion | bytes 23608320 | tf_op jit(solution)/shard_map/jit(_take)/gather | solution.py:250
  371.2 10.5 select_multiply_fusion.1
  388.3 13.3 all_gather.35
  405.0 25.0 %gather_fusion.3 = f32[3072]{0:T(1024)S(1)} fusion(f32[384,16]{0,1:T(8,128)S(1)} %fusion.149, s32[3072]{0:T(1024)S(1)} %reshape.653), kind=kCustom, calls=%fused_computation.5 | custom fusion | bytes 49152 | tf_op jit(solution)/shard_map/jit(take_along_axis)/gather | solution.py:245
  431.1 22.9 %scatter_custom_fusion.3 = bf16[3841,1536]{1,0:T(8,128)(2,1)} fusion(s32[3072]{0:T(1024)} %bitcast.422, f32[3072]{0:T(1024)S(1)} %mul.519, f32[384,1536]{1,0:T(8,128)} %convert_multiply_fusion.5, bf16[]{:T(256)} %constant.188.clone.1), kind=kCustom, calls=%fused_computation.97 | custom fusion | flops 9437184 | bytes 14171648 | tf_op jit(solution)/shard_map/scatter | solution.py:274
  454.1 10.0 slice.143
  464.1 53.6 %all-to-all-done = bf16[8,2,240,1536]{3,2,1,0:T(8,128)(2,1)} async-done(((bf16[8,2,240,1536]{3,2,1,0:T(8,128)(2,1)}), bf16[8,2,240,1536]{3,2,1,0:T(8,128)(2,1)}, u32[]{:S(2)}, u32[]{:S(2)}) %all-to-all-start) | async-done | bytes 11796512 | tf_op jit(solution)/shard_map/all_to_all | solution.py:253
  523.0 19.0 %fusion.76 = f32[8,2,240,1024]{3,2,0,1:T(8,128)} fusion(bf16[2,1536,1024]{2,1,0:T(8,128)(2,1)} %param.30, bf16[8,2,240,1536]{3,2,1,0:T(8,128)(2,1)} %all-to-all-done), kind=kOutput, calls=%fused_computation.118 | convolution fusion | flops 12079595520 | bytes 33816576 | tf_op jit(solution)/shard_map/sexd,edf->sexf/dot_general | solution.py:254
  542.0 111.6 %all-to-all-done.2 = bf16[8,2,240,1536]{3,2,1,0:T(8,128)(2,1)} async-done(((bf16[8,2,240,1536]{3,2,1,0:T(8,128)(2,1)}), bf16[8,2,240,1536]{3,2,1,0:T(8,128)(2,1)}, u32[]{:S(2)}, u32[]{:S(2)}) %all-to-all-start.2) | async-done | bytes 11796512 | tf_op jit(solution)/shard_map/all_to_all | solution.py:287
  653.6 17.3 fusion.69
  670.9 8.6 convert_bitcast_fusion.2
  690.1 19.2 %convert_bitcast_fusion.1 = bf16[8,2,240,1536]{3,2,0,1:T(8,128)(2,1)} fusion(bf16[2,1536,1024]{2,1,0:T(8,128)(2,1)} %param.30, bf16[8,2,240,512]{3,2,0,1:T(8,128)(2,1)} %get-tuple-element.522, bf16[8,2,240,512]{3,2,0,1:T(8,128)(2,1)} %get-tuple-element.521), kind=kOutput, calls=%fused_computation.90 | convolution fusion | flops 12101222400 | bytes 25952256 | tf_op jit(solution)/shard_map/sexf,edf->sexd/dot_general | solution.py:307
  709.3 10.0 copy.178
  719.3 101.4 %all-to-all-done.1 = bf16[8,2,240,1536]{3,2,1,0:T(8,128)(2,1)} async-done(((bf16[8,2,240,1536]{3,2,1,0:T(8,128)(2,1)}), bf16[8,2,240,1536]{3,2,1,0:T(8,128)(2,1)}, u32[]{:S(2)}, u32[]{:S(2)}) %all-to-all-start.1) | async-done | bytes 11796512 | tf_op jit(solution)/shard_map/all_to_all | solution.py:261
  826.2 25.5 %gather_fusion.4 = bf16[3072,1536]{1,0:T(8,128)(2,1)} fusion(bf16[3840,1536]{1,0:T(8,128)(2,1)} %bitcast.33, s32[3072]{0:T(1024)S(1)} %broadcast_clamp_fusion), kind=kCustom, calls=%fused_computation.clone | custom fusion | bytes 18886656 | tf_op jit(solution)/shard_map/jit(_take)/gather | solution.py:264
  851.8 6.6 fusion.48
  858.7 97.9 %all-to-all-done.3 = bf16[8,2,240,1536]{3,2,1,0:T(8,128)(2,1)} async-done(((bf16[8,2,240,1536]{3,2,1,0:T(8,128)(2,1)}), bf16[8,2,240,1536]{3,2,1,0:T(8,128)(2,1)}, u32[]{:S(2)}, u32[]{:S(2)}) %all-to-all-start.3) | async-done | bytes 11796512 | tf_op jit(solution)/shard_map/all_to_all | solution.py:310
  956.6 25.2 %gather_fusion.5 = bf16[3072,1536]{1,0:T(8,128)(2,1)} fusion(bf16[3840,1536]{1,0:T(8,128)(2,1)} %bitcast.41, s32[3072]{0:T(1024)S(1)} %broadcast_clamp_fusion), kind=kCustom, calls=%fused_computation.1.clone | custom fusion | bytes 18886656 | tf_op jit(solution)/shard_map/jit(_take)/gather | solution.py:315
  981.8 37.9 %fusion.50 = (f32[384,1536]{1,0:T(8,128)S(1)}, f32[384,1536]{1,0:T(8,128)S(1)}) fusion(bf16[3072,1536]{1,0:T(8,128)(2,1)} %gather_fusion.5, f32[384,8]{1,0:T(8,128)S(1)} %convert_element_type.248, pred[3072]{0:T(1024)(128)(4,1)S(1)} %copy-done.85, bf16[3072,1536]{1,0:T(8,128)(2,1)} %gather_fusion.4, f32[384,8]{1,0:T(8,128)S(1)} %copy-done.31), kind=kLoop, calls=%fused_computation.76 | loop fusion | flops 36569088 | bytes 23620608 | tf_op jit(solution)/shard_map/reduce_sum | solution.py:320
  1030.8 91.8 %while.41 = (s32[]{:T(128)}, f32[384,8,3,64]{0,3,2,1:T(8,128)}, f32[2,512,8,64]{1,3,2,0:T(8,128)}, bf16[2,512,8,64]{1,3,2,0:T(8,128)(2,1)}, bf16[2,512,512]{1,2,...) while((s32[]{:T(128)}, f32[384,8,3,64]{0,3,2,1:T(8,128)}, ...), condition=%wide.region_26.28_spmd.clone, body=%wide.region_25.27_spmd.clone.sunk | while | flops 3068660736 | bytes 160092720 | solution.py:361
  1031.9 8.0 fusion.239
  1041.4 11.7 fusion.241
  1053.1 7.0 bitcast_add_fusion.9
  1065.3 11.1 fusion.243
  1077.5 8.0 fusion.239
  1087.0 11.7 fusion.241
  1098.7 7.7 bitcast_add_fusion.9
  1111.5 11.1 fusion.243
  1133.3 20.3 %bitcast_convert_fusion = bf16[2,1536,1024]{2,1,0:T(8,128)(2,1)} fusion(bf16[8,2,240,1536]{3,2,1,0:T(8,128)(2,1)} %all-to-all-done, bf16[8,2,240,512]{3,2,0,1:T(8,128)(2,1)} %get-tuple-element.522, bf16[8,2,240,512]{3,2,0,1:T(8,128)(2,1)} %get-tuple-element.521), kind=kOutput, calls=%fused_computation.87 | convolution fusion | flops 12098469888 | bytes 25952256 | tf_op jit(solution)/shard_map/sexd,sexf->edf/dot_general | solution.py:304
  1153.6 13.1 bitcast_convert_fusion.1
  1168.0 8.9 convolution_bitcast_fusion.1
  1185.3 10.0 fusion.52
  1209.3 5.9 convolution_convert_fusion
  1231.0 297.7 %all-reduce.11.cloned.1.call-done = (bf16[2,1536,1024]{2,1,0:T(8,128)(2,1)}, bf16[2,512,1536]{2,1,0:T(8,128)(2,1)}) async-done(((bf16[2,1536,1024]{2,1,0:T(8,128)(2,1)}, bf16[2,512,1536]{2,1,0:T(8,128)(2,1)}), (bf16[2,1536,1024]{2,1,0:T(8,128)(2,1)}, bf16[2,512,1536]{2,1,0:T(8,128)(2,1)})) %all-reduce.11.cloned.1.call-update) | async-done | bytes 9437200 | tf_op jit(solution)/shard_map/psum | solution.py:312
  1528.6 9.3 convert_element_type.284
  1551.3 35.1 %reduce-scatter.18.cloned.1.call-done = bf16[384,512]{1,0:T(8,128)(2,1)} async-done(((bf16[1536,512]{1,0:T(8,128)(2,1)}), bf16[384,512]{1,0:T(8,128)(2,1)}) %reduce-scatter.18.cloned.1.call-update) | async-done | bytes 393232 | tf_op jit(solution)/shard_map/reduce_scatter | solution.py:442
  1586.4 36.6 %reduce-scatter.16.cloned.1.call-done = bf16[384,512]{1,0:T(8,128)(2,1)} async-done(((bf16[1536,512]{1,0:T(8,128)(2,1)}), bf16[384,512]{1,0:T(8,128)(2,1)}) %reduce-scatter.16.cloned.1.call-update) | async-done | bytes 393232 | tf_op jit(solution)/shard_map/reduce_scatter | solution.py:439
  1622.9 86.7 %reduce-scatter.20.cloned.1.call-done = bf16[384,1536]{1,0:T(8,128)(2,1)} async-done(((bf16[1536,1536]{1,0:T(8,128)(2,1)}), bf16[384,1536]{1,0:T(8,128)(2,1)}) %reduce-scatter.20.cloned.1.call-update) | async-done | bytes 1179664 | tf_op jit(solution)/shard_map/reduce_scatter | solution.py:445
  1709.6 88.1 %reduce-scatter.14.cloned.1.call-done = bf16[384,1536]{1,0:T(8,128)(2,1)} async-done(((bf16[1536,1536]{1,0:T(8,128)(2,1)}), bf16[384,1536]{1,0:T(8,128)(2,1)}) %reduce-scatter.14.cloned.1.call-update) | async-done | bytes 1179664 | tf_op jit(solution)/shard_map/reduce_scatter | solution.py:436
  1803.5 11.1 all-reduce.4
  1814.8 22.8 %all-reduce.2 = (bf16[384]{0:T(512)(128)(2,1)S(1)}, bf16[384]{0:T(512)(128)(2,1)S(1)}, bf16[384,16]{0,1:T(8,128)(2,1)S(1)}) all-reduce(bf16[384]{0:T(512)(128)(2,1)S(1)} %dynamic-slice.1, bf16[384]{0:T(512)(128)(2,1)S(1)} %dynamic-slice.3, bf16[384,16]{0,1:T(8,128)(2,1)S(1)} %copy.226), channel_id=1, replica_groups=mesh['dp'=4,'expert'=8] {'expert'}, use_global_device_ids=true, to_apply=%region_32.34 | all-reduce | flops 6912 | bytes 27648 | tf_op jit(solution)/shard_map/psum | solution.py:456
  1843.6 28.9 %all-reduce.9.cloned.1.call-done = (bf16[384,1536]{1,0:T(8,128)(2,1)}, bf16[384,512]{1,0:T(8,128)(2,1)}, bf16[384,512]{1,0:T(8,128)(2,1)}, bf16[384,1536]{1,0:T(8,128)(2,1)}) async-done(((bf16[384,1536]{1,0:T(8,128)(2,1)}, bf16[384,512]{1,0:T(8,128)(2,1)}, bf16[384,512]{1,0:T(8,128)(2,1)}, bf16[384,1536]{1,0:T(8,128)(2,1)}), (bf16[384,1536]{1,0:T(8,128)(2,1)}, bf16[384,512]{1,0:T(8,128)(2,1)}, ...) | async-done | bytes 3145744 | tf_op jit(solution)/shard_map/psum | solution.py:457
  (442 shorter events, 206.4 us)
Async XLA Ops:
  7.2 646.4 %copy-start = (bf16[2,512,1536]{2,1,0:T(8,128)(2,1)S(1)}, bf16[2,512,1536]{2,1,0:T(8,128)(2,1)}, u32[]{:S(2)}) copy-start(bf16[2,512,1536]{2,1,0:T(8,128)(2,1)} %param.31) | copy-start | bytes 9437188
  7.2 42.2 %all-gather.13.cloned.1.call-start = ((), (), s32[]{:S(2)}) async-start(), calls=%async_computation.13 | async-start | bytes 1966080 | tf_op jit(solution)/shard_map/all_gather | solution.py:138
  7.9 79.1 %all-gather.9.cloned.1.call-start = ((), (), s32[]{:S(2)}) async-start(), calls=%async_computation.11 | async-start | bytes 1966080 | tf_op jit(solution)/shard_map/all_gather | solution.py:139
  8.7 203.1 %all-gather.15.cloned.1.call-start = ((), (), s32[]{:S(2)}) async-start(), calls=%async_computation.14 | async-start | bytes 1179648 | tf_op jit(solution)/shard_map/all_gather | solution.py:172
  23.0 205.6 %copy-start.68 = (f32[1536]{0:T(1024)}, f32[1536]{0:T(1024)S(1)}, u32[]{:S(2)}) copy-start(f32[1536]{0:T(1024)S(1)} %reshape.704) | copy-start | bytes 18436
  24.6 62.4 %copy-start.86 = (f32[384]{0:T(512)}, f32[384]{0:T(512)S(1)}, u32[]{:S(2)}) copy-start(f32[384]{0:T(512)S(1)} %add_rsqrt_fusion.1) | copy-start | bytes 4612
  24.9 27.5 %copy-start.38 = (f32[384,32]{0,1:T(8,128)}, f32[384,32]{0,1:T(8,128)S(1)}, u32[]{:S(2)}) copy-start(f32[384,32]{0,1:T(8,128)S(1)} %get-tuple-element.539) | copy-start | bytes 147460
  24.9 208.7 %copy-start.36 = (f32[384,32]{0,1:T(8,128)}, f32[384,32]{0,1:T(8,128)S(1)}, u32[]{:S(2)}) copy-start(f32[384,32]{0,1:T(8,128)S(1)} %get-tuple-element.538) | copy-start | bytes 147460
  54.0 160.1 %all-gather.11.cloned.1.call-start = ((), (), s32[]{:S(2)}) async-start(), calls=%async_computation.12 | async-start | bytes 1179648 | tf_op jit(solution)/shard_map/all_gather | solution.py:173
  90.3 14.1 copy-start.90
  91.0 137.5 %all-gather.17.cloned.1.call-start = ((), (), s32[]{:S(2)}) async-start(), calls=%async_computation.15 | async-start | bytes 5898240 | tf_op jit(solution)/shard_map/all_gather | solution.py:137
  91.6 246.0 %all-gather.19.cloned.1.call-start = ((), (), s32[]{:S(2)}) async-start(), calls=%async_computation.16 | async-start | bytes 5898240 | tf_op jit(solution)/shard_map/all_gather | solution.py:140
  104.5 29.3 %copy-start.2 = (s32[3072]{0:T(1024)}, s32[3072]{0:T(1024)S(1)}, u32[]{:S(2)}) copy-start(s32[3072]{0:T(1024)S(1)} %reshape.602) | copy-start | bytes 36868
  143.7 58.1 %copy-start.33 = (bf16[384,8,32]{0,2,1:T(8,128)(2,1)S(1)}, bf16[384,8,32]{0,2,1:T(8,128)(2,1)}, u32[]{:S(2)}) copy-start(bf16[384,8,32]{0,2,1:T(8,128)(2,1)} %copy-done.32) | copy-start | bytes 589828
  161.2 52.9 %copy-start.61 = (s32[3072]{0:T(1024)}, s32[3072]{0:T(1024)S(1)}, u32[]{:S(2)}) copy-start(s32[3072]{0:T(1024)S(1)} %gather_fusion.1) | copy-start | bytes 36868
  161.2 17.6 copy-start.91
  176.3 31.5 %collective-permute-start.1 = (bf16[256,512]{1,0:T(8,128)(2,1)}, bf16[256,512]{1,0:T(8,128)(2,1)}, u32[]{:S(2)}, u32[]{:S(2)}) collective-permute-start(bf16[256,512]{1,0:T(8,128)(2,1)} %slice.136), channel_id=1, source_target_pairs={{0,1},{1,2},{2,3},{3,4},{4,5},{5,6},{6,7},{8,9},{9,10},{10,11},{11... | collective-permute-start | bytes 786440 | tf_op jit(solution)/shard_map/ppermute | solution.py:22
  178.8 164.2 %copy-start.64 = (f32[1536]{0:T(1024)}, f32[1536]{0:T(1024)S(1)}, u32[]{:S(2)}) copy-start(f32[1536]{0:T(1024)S(1)} %reshape.705) | copy-start | bytes 18436
  203.5 75.1 %collective-permute-start = (bf16[256,512]{0,1:T(8,128)(2,1)}, bf16[256,512]{0,1:T(8,128)(2,1)}, u32[]{:S(2)}, u32[]{:S(2)}) collective-permute-start(bf16[256,512]{0,1:T(8,128)(2,1)} %bitcast.9), channel_id=1, source_target_pairs={{0,1},{1,2},{2,3},{3,4},{4,5},{5,6},{6,7},{8,9},{9,10},{10,11},{11... | collective-permute-start | bytes 786440 | tf_op jit(solution)/shard_map/ppermute | solution.py:22
  211.7 16.8 copy-start.87
  216.3 17.3 copy-start.39
  278.6 10.8 copy-start.44
  300.3 24.6 %copy-start.45 = (pred[384,512]{0,1:T(8,128)(4,1)S(1)}, pred[384,512]{0,1:T(8,128)(4,1)}, u32[]{:S(2)}) copy-start(pred[384,512]{0,1:T(8,128)(4,1)} %select_and_fusion) | copy-start | bytes 589828
  324.9 12.7 copy-start.97
  345.7 25.5 %copy-start.79 = (pred[8,2,240]{2,1,0:T(4,128)(4,1)S(1)}, pred[8,2,240]{2,1,0:T(4,128)(4,1)}, u32[]{:S(2)}) copy-start(pred[8,2,240]{2,1,0:T(4,128)(4,1)} %compare_and_fusion) | copy-start | bytes 11524
  345.7 25.5 %copy-start.80 = (bf16[8,2,240]{2,1,0:T(2,128)(2,1)S(1)}, bf16[8,2,240]{2,1,0:T(2,128)(2,1)}, u32[]{:S(2)}) copy-start(bf16[8,2,240]{2,1,0:T(2,128)(2,1)} %mul.501) | copy-start | bytes 23044
  381.7 136.0 %all-to-all-start = ((bf16[8,2,240,1536]{3,2,1,0:T(8,128)(2,1)}), bf16[8,2,240,1536]{3,2,1,0:T(8,128)(2,1)}, u32[]{:S(2)}, u32[]{:S(2)}) async-start(bf16[8,2,240,1536]{3,2,1,0:T(8,128)(2,1)} %select_multiply_fusion.1), calls=%async_computation | async-start | bytes 23592960 | tf_op jit(solution)/shard_map/all_to_all | solution.py:253
  388.2 16.4 copy-start.51
  388.3 42.0 %copy-start.75 = (pred[384,8]{0,1:T(8,128)(4,1)}, pred[384,8]{0,1:T(8,128)(4,1)S(1)}, u32[]{:S(2)}) copy-start(pred[384,8]{0,1:T(8,128)(4,1)S(1)} %copy.169) | copy-start | bytes 9220
  388.3 16.3 copy-start.5
  430.9 23.2 %copy-start.81 = (f32[384]{0:T(512)}, f32[384]{0:T(512)S(1)}, u32[]{:S(2)}) copy-start(f32[384]{0:T(512)S(1)} %fusion.117) | copy-start | bytes 4612
  431.0 23.1 %copy-start.30 = (f32[384,8]{1,0:T(8,128)}, f32[384,8]{1,0:T(8,128)S(1)}, u32[]{:S(2)}) copy-start(f32[384,8]{1,0:T(8,128)S(1)} %copy.170) | copy-start | bytes 36868
  517.7 135.9 %all-to-all-start.2 = ((bf16[8,2,240,1536]{3,2,1,0:T(8,128)(2,1)}), bf16[8,2,240,1536]{3,2,1,0:T(8,128)(2,1)}, u32[]{:S(2)}, u32[]{:S(2)}) async-start(bf16[8,2,240,1536]{3,2,1,0:T(8,128)(2,1)} %bitcast.386), calls=%async_computation.2 | async-start | bytes 23592960 | tf_op jit(solution)/shard_map/all_to_all | solution.py:287
  684.7 136.0 %all-to-all-start.1 = ((bf16[8,2,240,1536]{3,2,1,0:T(8,128)(2,1)}), bf16[8,2,240,1536]{3,2,1,0:T(8,128)(2,1)}, u32[]{:S(2)}, u32[]{:S(2)}) async-start(bf16[8,2,240,1536]{3,2,1,0:T(8,128)(2,1)} %copy.173), calls=%async_computation.1 | async-start | bytes 23592960 | tf_op jit(solution)/shard_map/all_to_all | solution.py:261
  719.3 106.8 %copy-start.52 = (pred[384,8]{1,0:T(8,128)(4,1)S(1)}, pred[384,8]{1,0:T(8,128)(4,1)}, u32[]{:S(2)}) copy-start(pred[384,8]{1,0:T(8,128)(4,1)} %copy-done.51) | copy-start | bytes 9220
  719.3 106.8 %copy-start.4 = (s32[3072]{0:T(1024)S(1)}, s32[3072]{0:T(1024)}, u32[]{:S(2)}) copy-start(s32[3072]{0:T(1024)} %copy-done.2) | copy-start | bytes 36868
  719.3 106.8 %copy-start.63 = (s32[3072]{0:T(1024)S(1)}, s32[3072]{0:T(1024)}, u32[]{:S(2)}) copy-start(s32[3072]{0:T(1024)} %copy-done.61) | copy-start | bytes 36868
  820.7 135.9 %all-to-all-start.3 = ((bf16[8,2,240,1536]{3,2,1,0:T(8,128)(2,1)}), bf16[8,2,240,1536]{3,2,1,0:T(8,128)(2,1)}, u32[]{:S(2)}, u32[]{:S(2)}) async-start(bf16[8,2,240,1536]{3,2,1,0:T(8,128)(2,1)} %copy.178), calls=%async_computation.3 | async-start | bytes 23592960 | tf_op jit(solution)/shard_map/all_to_all | solution.py:310
  826.0 355.7 %reduce-scatter.24.cloned.1.call-start = ((), (), s32[]{:S(2)}) async-start(), calls=%async_computation.22 | async-start | bytes 1179648
  826.2 25.6 %copy-start.13 = (f32[384,1536]{1,0:T(8,128)S(1)}, f32[384,1536]{1,0:T(8,128)}, u32[]{:S(2)}) copy-start(f32[384,1536]{1,0:T(8,128)} %convert_multiply_fusion.5) | copy-start | bytes 7077892
  826.2 25.6 %copy-start.85 = (pred[3072]{0:T(1024)(128)(4,1)S(1)}, pred[3072]{0:T(1024)(128)(4,1)}, u32[]{:S(2)}) copy-start(pred[3072]{0:T(1024)(128)(4,1)} %get-tuple-element.536) | copy-start | bytes 9220
  858.7 161.0 %copy-start.66 = (bf16[384,16]{0,1:T(8,128)(2,1)}, bf16[384,16]{0,1:T(8,128)(2,1)S(1)}, u32[]{:S(2)}) copy-start(bf16[384,16]{0,1:T(8,128)(2,1)S(1)} %select_reduce_fusion) | copy-start | bytes 36868
  956.6 25.2 %copy-start.31 = (f32[384,8]{1,0:T(8,128)S(1)}, f32[384,8]{1,0:T(8,128)}, u32[]{:S(2)}) copy-start(f32[384,8]{1,0:T(8,128)} %copy-done.30) | copy-start | bytes 36868
  981.7 37.9 %copy-start.15 = (f32[384,1536]{1,0:T(8,128)S(1)}, f32[384,1536]{1,0:T(8,128)}, u32[]{:S(2)}) copy-start(f32[384,1536]{1,0:T(8,128)} %copy-done.14) | copy-start | bytes 7077892
  981.8 38.0 %copy-start.50 = (bf16[1536,16]{0,1:T(8,128)(2,1)S(1)}, bf16[1536,16]{0,1:T(8,128)(2,1)}, u32[]{:S(2)}) copy-start(bf16[1536,16]{0,1:T(8,128)(2,1)} %copy-done.49) | copy-start | bytes 147460
  981.8 38.0 %copy-start.65 = (f32[1536]{0:T(1024)S(1)}, f32[1536]{0:T(1024)}, u32[]{:S(2)}) copy-start(f32[1536]{0:T(1024)} %copy-done.64) | copy-start | bytes 18436
  981.8 38.0 %copy-start.84 = (f32[384]{0:T(512)S(1)}, f32[384]{0:T(512)}, u32[]{:S(2)}) copy-start(f32[384]{0:T(512)} %copy-done.83) | copy-start | bytes 4612
  1031.9 9.4 copy-start.24
  1077.5 9.4 copy-start.24
  1127.4 78.1 %reduce-scatter.22.cloned.1.call-start = ((), (), s32[]{:S(2)}) async-start(), calls=%async_computation.21 | async-start | bytes 1179648
  1133.2 395.4 %all-reduce.11.cloned.1.call-start = ((), (), s32[]{:S(2)}) async-start(), calls=%async_computation.25 | async-start | bytes 18874368 | tf_op jit(solution)/shard_map/psum | solution.py:312
  1166.7 11.7 copy-start.6
  1166.7 11.7 copy-start.67
  1166.8 383.6 %reduce-scatter.26.cloned.1.call-start = ((), (), s32[]{:S(2)}) async-start(), calls=%async_computation.23 | async-start | bytes 491520
  1177.0 3.7 collective-permute-start.3
  1179.7 406.7 %reduce-scatter.18.cloned.1.call-start = ((), (), s32[]{:S(2)}) async-start(), calls=%async_computation.19 | async-start | bytes 1966080 | tf_op jit(solution)/shard_map/reduce_scatter | solution.py:442
  1185.2 10.1 copy-start.20
  1185.2 437.7 %reduce-scatter.16.cloned.1.call-start = ((), (), s32[]{:S(2)}) async-start(), calls=%async_computation.18 | async-start | bytes 1966080 | tf_op jit(solution)/shard_map/reduce_scatter | solution.py:439
  1185.3 10.0 copy-start.22
  1199.1 6.4 collective-permute-start.2
  1209.2 500.4 %reduce-scatter.20.cloned.1.call-start = ((), (), s32[]{:S(2)}) async-start(), calls=%async_computation.20 | async-start | bytes 5898240 | tf_op jit(solution)/shard_map/reduce_scatter | solution.py:445
  1215.2 582.5 %reduce-scatter.14.cloned.1.call-start = ((), (), s32[]{:S(2)}) async-start(), calls=%async_computation.17 | async-start | bytes 5898240 | tf_op jit(solution)/shard_map/reduce_scatter | solution.py:436
  1229.1 643.4 %all-reduce.9.cloned.1.call-start = ((), (), s32[]{:S(2)}) async-start(), calls=%async_computation.24 | async-start | bytes 6291456 | tf_op jit(solution)/shard_map/psum | solution.py:457
  1528.6 9.3 copy-start.27
  (65 other events, 223.8 us)
Sparse Core Ops, SparseCore 0:
  9.6 39.7 all-gather.12
  51.0 35.9 all-gather.8
  89.4 22.3 all-gather.14
  114.2 23.4 all-gather.10
  139.1 89.4 all-gather.16
  230.0 87.8 all-gather.18
  1127.5 32.7 reduce-scatter.23
  1164.0 35.9 reduce-scatter.21
  1203.2 325.3 all-reduce.10
  1530.7 19.5 reduce-scatter.25
  1552.8 33.5 reduce-scatter.17
  1588.6 34.2 reduce-scatter.15
  1625.4 84.2 reduce-scatter.19
  1711.9 85.7 reduce-scatter.13
  1801.6 70.8 all-reduce.8
where the time goes:
time: 1900 us; the launch traced here: 1890 us
  waiting for transfers between devices  1020 us (54%)
  matrix products  311 us (16%)
  local copies, waits for them, and re-layouts  263 us (14%)
  other arithmetic  173 us (9%)
  blocking collectives  72.6 us (4%)
  starting transfers between devices  31.2 us (2%)
    psum x1, waiting for transfers between devices, on_device(): lax.psum(gateup_local.astype(jnp.bfloat16), 'dp').astype(jnp.float32)  298 us
    all_to_all x1, waiting for transfers between devices, on_device(): lax.all_to_all(grad_send, 'expert', split_axis=0, concat_axis=0, tiled=True)  112 us
    all_to_all x1, waiting for transfers between devices, on_device(): lax.all_to_all(produced, 'expert', split_axis=0, concat_axis=0, tiled=True)  101 us
    all_to_all x1, waiting for transfers between devices, on_device(): lax.all_to_all(input_rows, 'expert', split_axis=0, concat_axis=0, tiled=T...  97.9 us
    reduce_scatter x1, waiting for transfers between devices, on_device(): lax.psum_scatter(dense_local[1].astype(jnp.bfloat16), 'dp', scatter_dimen...  88.1 us
    reduce_scatter x1, waiting for transfers between devices, on_device(): lax.psum_scatter(dense_local[4].astype(jnp.bfloat16), 'dp', scatter_dimen...  86.7 us
    all_to_all x1, waiting for transfers between devices, on_device(): lax.all_to_all(send_rows, 'expert', split_axis=0, concat_axis=0, tiled=True)  53.6 us
    dot_general x5, matrix products, score_block(): jnp.einsum('tkgd,skd->kgts', query_grouped, keyed, preferred_element_type...  42.9 us
  transfers between devices with their start and end apart: 23, of which 16 were waited for; matrix products, arithmetic and copies ran while one was open for 26% of the time, Pallas kernels for 0%

commit v1 on v0

v1 whole, which is shorter than its diff:
```python
import functools

import jax
import jax.numpy as jnp
from jax import lax
from jax.experimental import pallas as pl
from jax.experimental.pallas import tpu as pltpu
from jax.sharding import PartitionSpec as P

HEADS = 24
KV_HEADS = 8
HEAD = 64
PROMPT_DEV = 128


EPSILON = 1e-06
ATTN_SCALE = 0.015625
RESIDUAL = 0.22
ROPE_BASE = 10000.0
MASKED = -1e30
LOG2E = 1.4426950408889634


def norm_forward(inputs, gain_vec):
    inverse = lax.rsqrt(jnp.mean(inputs * inputs, axis=-1, keepdims=True) + EPSILON)
    return (inputs * inverse * gain_vec, inverse)


def norm_backward(inputs, inverse, gain_vec, upstream):
    scaled = upstream * gain_vec
    middle = jnp.mean(inputs * scaled, axis=-1, keepdims=True)
    row_grad = inverse * scaled - inputs * inverse * inverse * inverse * middle
    return (row_grad, jnp.sum(upstream * inputs * inverse, axis=0))


def rotary_tables(position, head_size):
    half_size = head_size // 2
    frequency = ROPE_BASE ** (-jnp.arange(half_size, dtype=jnp.float32) * 2.0 / head_size)
    angles = position.astype(jnp.float32)[:, None] * frequency[None, :]
    return (jnp.cos(angles)[:, None, :], jnp.sin(angles)[:, None, :])


def unrotate(values, cosine, sine_part):
    half_size = values.shape[-1] // 2
    lower_half = values[..., :half_size]
    upper_half = values[..., half_size:]
    return jnp.concatenate(
        [
            lower_half * cosine + upper_half * sine_part,
            upper_half * cosine - lower_half * sine_part,
        ],
        axis=-1,
    )


def slot_codes(routes, ranks, experts, capacity):
    ids = jnp.arange(experts, dtype=jnp.int32)
    hit = routes[:, :, None] == ids[None, None, :]
    far = jnp.int32(routes.shape[0] * routes.shape[1])
    pair_rank = jnp.min(jnp.where(hit, ranks[:, :, None], far), axis=1)
    by_expert = pair_rank.T
    slot = jnp.sum((by_expert[:, :, None] < by_expert[:, None, :]).astype(jnp.int32), axis=1).T
    chosen = pair_rank < far
    return jnp.where(chosen, jnp.where(slot < capacity, 2.0, 1.0), 0.0)


def gates_of(logits, codes):
    chosen = codes > 0.5
    top = jnp.max(jnp.where(chosen, logits, MASKED), axis=-1, keepdims=True)
    raised = jnp.where(chosen, jnp.exp(jnp.minimum(logits - top, 0.0)), 0.0)
    return raised / jnp.sum(raised, axis=-1, keepdims=True)


NT = (((1,), (1,)), ((), ()))
VMEM_GRANT = 50 * 1024 * 1024


def matmul(left, right):
    return jnp.dot(left, right, preferred_element_type=jnp.float32)


def matmul_nt(left, right):
    return lax.dot_general(left, right, NT, preferred_element_type=jnp.float32)


def low_lanes(shape):
    return lax.broadcasted_iota(jnp.int32, shape, 1) % 128 < 64


def spread_pair(pair):
    swapped = pltpu.roll(pair, 64, 1)
    low = low_lanes(pair.shape)
    return jnp.where(low, pair, swapped), jnp.where(low, swapped, pair)


def fold_halves(both, low_out):
    total = both + pltpu.roll(both, 64, 1)
    low = low_lanes(both.shape)
    return jnp.where(low, total, 0.0) if low_out else jnp.where(low, 0.0, total)


def one_half(block, low_half):
    low = low_lanes(block.shape)
    wide = block.astype(jnp.float32)
    wide = jnp.where(low, wide, 0.0) if low_half else jnp.where(low, 0.0, wide)
    return wide.astype(jnp.bfloat16)


def stage_pairs(prompt_ref, tail_ref, spread_ref):
    prompt_total = prompt_ref.shape[0]
    tail_total = tail_ref.shape[0]
    first, second = spread_pair(prompt_ref[...].astype(jnp.float32))
    spread_ref[0, :prompt_total, :] = first.astype(jnp.bfloat16)
    spread_ref[1, :prompt_total, :] = second.astype(jnp.bfloat16)
    first, second = spread_pair(tail_ref[...].astype(jnp.float32))
    spread_ref[0, prompt_total : prompt_total + tail_total, :] = first.astype(jnp.bfloat16)
    spread_ref[1, prompt_total : prompt_total + tail_total, :] = second.astype(jnp.bfloat16)


def attend_kernel(place_ref, q_ref, pk_ref, pv_ref, tk_ref, tv_ref, o_ref, lse_ref, keys, values):
    rows = q_ref.shape[0]
    prompt_rows = PROMPT_DEV
    cont = rows - prompt_rows
    prompt_total = pk_ref.shape[0]
    stage_pairs(pk_ref, tk_ref, keys)
    stage_pairs(pv_ref, tv_ref, values)
    first_position = place_ref[0]
    odd = place_ref[1]
    factor = ATTN_SCALE * LOG2E
    key_at = lax.broadcasted_iota(jnp.int32, (prompt_rows, prompt_total), 1)
    row_at = lax.broadcasted_iota(jnp.int32, (prompt_rows, prompt_total), 0)
    prompt_ok = key_at <= row_at + first_position
    tail_at = lax.broadcasted_iota(jnp.int32, (cont, 2 * cont), 1)
    cont_at = lax.broadcasted_iota(jnp.int32, (cont, 2 * cont), 0)
    tail_ok = ((tail_at < cont) & (odd == 1)) | ((tail_at >= cont) & (tail_at - cont <= cont_at))
    lane = lax.broadcasted_iota(jnp.int32, (rows, 128), 1)
    stats = jnp.zeros((rows, 128), jnp.float32)
    for block in range(3):
        q_block = q_ref[:, block * 128 : block * 128 + 128]
        halves = []
        for half in range(2):
            head = 2 * block + half
            own = head // 3
            q_own = one_half(q_block, half == 0)
            score = matmul_nt(q_own[:prompt_rows], keys[own, :prompt_total, :])
            score = jnp.where(prompt_ok, score, MASKED)
            top = jnp.max(score, axis=1, keepdims=True)
            raised = jnp.exp2((score - top) * factor)
            total = jnp.sum(raised, axis=1, keepdims=True)
            first_out = matmul(raised.astype(jnp.bfloat16), values[own, :prompt_total, :]) / total
            first_log = top * factor + jnp.log(total) * LOG2E
            q_cont = q_own[prompt_rows:]
            score = matmul_nt(q_cont, keys[own, :prompt_total, :])
            tail_score = matmul_nt(q_cont, keys[own, prompt_total:, :])
            tail_score = jnp.where(tail_ok, tail_score, MASKED)
            top = jnp.maximum(
                jnp.max(score, axis=1, keepdims=True), jnp.max(tail_score, axis=1, keepdims=True)
            )
            raised = jnp.exp2((score - top) * factor)
            tail_raised = jnp.exp2((tail_score - top) * factor)
            total = jnp.sum(raised, axis=1, keepdims=True) + jnp.sum(
                tail_raised, axis=1, keepdims=True
            )
            second_out = matmul(raised.astype(jnp.bfloat16), values[own, :prompt_total, :])
            second_out += matmul(tail_raised.astype(jnp.bfloat16), values[own, prompt_total:, :])
            second_out = second_out / total
            second_log = top * factor + jnp.log(total) * LOG2E
            halves.append(jnp.concatenate([first_out, second_out], axis=0))
            stats = jnp.where(
                lane == head, jnp.concatenate([first_log, second_log], axis=0), stats
            )
        o_ref[:, block * 128 : block * 128 + 128] = jnp.where(
            low_lanes((rows, 128)), halves[0], halves[1]
        ).astype(jnp.bfloat16)
    lse_ref[0] = stats


def attend(place, projected, prompt_pairs, tail_pairs):
    rows = projected.shape[0]
    width = HEADS * HEAD
    prompt_total = prompt_pairs.shape[0]
    tail_total = tail_pairs.shape[0]
    pairs = KV_HEADS // 2
    per_pair = width // pairs
    key_total = prompt_total + tail_total
    cost = 4 * HEADS * rows * key_total * 64
    return pl.pallas_call(
        attend_kernel,
        grid=(pairs,),
        in_specs=[
            pl.BlockSpec(memory_space=pltpu.SMEM),
            pl.BlockSpec((rows, per_pair), lambda p: (0, p)),
            pl.BlockSpec((prompt_total, 128), lambda p: (0, p)),
            pl.BlockSpec((prompt_total, 128), lambda p: (0, p + pairs)),
            pl.BlockSpec((tail_total, 128), lambda p: (0, p)),
            pl.BlockSpec((tail_total, 128), lambda p: (0, p + pairs)),
        ],
        out_specs=[
            pl.BlockSpec((rows, per_pair), lambda p: (0, p)),
            pl.BlockSpec((1, rows, 128), lambda p: (p, 0, 0)),
        ],
        out_shape=[
            jax.ShapeDtypeStruct((rows, width), jnp.bfloat16),
            jax.ShapeDtypeStruct((pairs, rows, 128), jnp.float32),
        ],
        scratch_shapes=[
            pltpu.VMEM((2, key_total, 128), jnp.bfloat16),
            pltpu.VMEM((2, key_total, 128), jnp.bfloat16),
        ],
        compiler_params=pltpu.CompilerParams(vmem_limit_bytes=VMEM_GRANT),
        cost_estimate=pl.CostEstimate(
            flops=cost, bytes_accessed=6 * rows * width, transcendentals=HEADS * rows * key_total
        ),
        name="attend",
    )(place, projected, prompt_pairs, prompt_pairs, tail_pairs, tail_pairs)


def attend_back_kernel(
    place_ref,
    q_ref,
    do_ref,
    pk_ref,
    pv_ref,
    tk_ref,
    tv_ref,
    lse_ref,
    cos_ref,
    sin_ref,
    dq_ref,
    dpk_ref,
    dpv_ref,
    dtk_ref,
    dtv_ref,
    keys,
    values,
    keys_across,
    key_sums,
    value_sums,
):
    rows = q_ref.shape[0]
    prompt_rows = PROMPT_DEV
    cont = rows - prompt_rows
    prompt_total = pk_ref.shape[0]
    key_total = prompt_total + tk_ref.shape[0]
    stage_pairs(pk_ref, tk_ref, keys)
    stage_pairs(pv_ref, tv_ref, values)
    first_position = place_ref[0]
    odd = place_ref[1]
    factor = ATTN_SCALE * LOG2E
    keys_across[:, :prompt_total] = pk_ref[...].astype(jnp.float32).T.astype(jnp.bfloat16)
    keys_across[:, prompt_total:] = tk_ref[...].astype(jnp.float32).T.astype(jnp.bfloat16)
    key_at = lax.broadcasted_iota(jnp.int32, (prompt_total, prompt_rows), 0)
    row_at = lax.broadcasted_iota(jnp.int32, (prompt_total, prompt_rows), 1)
    prompt_ok = key_at <= row_at + first_position
    tail_at = lax.broadcasted_iota(jnp.int32, (2 * cont, cont), 0)
    cont_at = lax.broadcasted_iota(jnp.int32, (2 * cont, cont), 1)
    tail_ok = ((tail_at < cont) & (odd == 1)) | ((tail_at >= cont) & (tail_at - cont <= cont_at))
    stats = lse_ref[0]
    query_parts = {}
    for own in range(2):
        across = keys_across[64 * own : 64 * own + 64, :]
        for member in range(3):
            head = 3 * own + member
            block, half = head // 2, head % 2
            lanes = slice(block * 128, block * 128 + 128)
            q_own = one_half(q_ref[:, lanes], half == 0)
            do_own = one_half(do_ref[:, lanes], half == 0)
            log_row = stats[head : head + 1, :]
            q_cont, do_cont = q_own[prompt_rows:], do_own[prompt_rows:]
            log_cont = log_row[:, prompt_rows:]
            score = matmul_nt(keys[own], q_cont)
            weight_prompt = jnp.exp2(score[:prompt_total] * factor - log_cont)
            weight_tail = jnp.where(
                tail_ok, jnp.exp2(jnp.minimum(score[prompt_total:] * factor - log_cont, 0.0)), 0.0
            )
            weight = jnp.concatenate([weight_prompt, weight_tail], axis=0)
            change = matmul_nt(values[own], do_cont)
            delta = jnp.sum(weight * change, axis=0, keepdims=True)
            score_grad = (weight * (change - delta)).astype(jnp.bfloat16)
            key_part = matmul(score_grad, q_cont)
            value_part = matmul(weight.astype(jnp.bfloat16), do_cont)
            query_cont = matmul(across, score_grad)
            if member == 0:
                key_sums[own] = key_part
                value_sums[own] = value_part
            else:
                key_sums[own] += key_part
                value_sums[own] += value_part
            q_first, do_first = q_own[:prompt_rows], do_own[:prompt_rows]
            log_first = log_row[:, :prompt_rows]
            score = matmul_nt(keys[own, :prompt_total, :], q_first)
            weight = jnp.where(
                prompt_ok, jnp.exp2(jnp.minimum(score * factor - log_first, 0.0)), 0.0
            )
            change = matmul_nt(values[own, :prompt_total, :], do_first)
            delta = jnp.sum(weight * change, axis=0, keepdims=True)
            score_grad = (weight * (change - delta)).astype(jnp.bfloat16)
            key_sums[own, :prompt_total, :] += matmul(score_grad, q_first)
            value_sums[own, :prompt_total, :] += matmul(weight.astype(jnp.bfloat16), do_first)
            query_first = matmul(across[:, :prompt_total], score_grad)
            query_parts[head] = jnp.concatenate([query_first, query_cont], axis=1)
    for block in range(3):
        lanes = slice(block * 128, block * 128 + 128)
        turned = jnp.concatenate([query_parts[2 * block], query_parts[2 * block + 1]], axis=0)
        flat = turned.T * ATTN_SCALE
        dq_ref[:, lanes] = turn(flat, cos_ref[...], sin_ref[...]).astype(jnp.bfloat16)
    key_pair = fold_halves(key_sums[0], True) + fold_halves(key_sums[1], False)
    key_pair = key_pair * ATTN_SCALE
    value_pair = fold_halves(value_sums[0], True) + fold_halves(value_sums[1], False)
    dpk_ref[...] = key_pair[:prompt_total].astype(jnp.bfloat16)
    dtk_ref[...] = key_pair[prompt_total:]
    dpv_ref[...] = value_pair[:prompt_total].astype(jnp.bfloat16)
    dtv_ref[...] = value_pair[prompt_total:]


def attend_back(place, projected, upstream, prompt_pairs, tail_pairs, stats, cosines, sines):
    rows, width = upstream.shape
    prompt_total = prompt_pairs.shape[0]
    kv_width = KV_HEADS * HEAD
    tail_total = tail_pairs.shape[0]
    pairs = KV_HEADS // 2
    per_pair = width // pairs
    key_total = prompt_total + tail_total
    across = stats[:, :, :8].transpose(0, 2, 1)
    own_rows = pl.BlockSpec((rows, per_pair), lambda p: (0, p))
    prompt_spec = pl.BlockSpec((prompt_total, 128), lambda p: (0, p))
    tail_spec = pl.BlockSpec((tail_total, 128), lambda p: (0, p))
    table = pl.BlockSpec((rows, 128), lambda p: (0, 0))
    return pl.pallas_call(
        attend_back_kernel,
        grid=(pairs,),
        in_specs=[
            pl.BlockSpec(memory_space=pltpu.SMEM),
            own_rows,
            own_rows,
            prompt_spec,
            pl.BlockSpec((prompt_total, 128), lambda p: (0, p + pairs)),
            tail_spec,
            pl.BlockSpec((tail_total, 128), lambda p: (0, p + pairs)),
            pl.BlockSpec((1, 8, rows), lambda p: (p, 0, 0)),
            table,
            table,
        ],
        out_specs=[own_rows, prompt_spec, prompt_spec, tail_spec, tail_spec],
        out_shape=[
            jax.ShapeDtypeStruct((rows, width), jnp.bfloat16),
            jax.ShapeDtypeStruct((prompt_total, kv_width), jnp.bfloat16),
            jax.ShapeDtypeStruct((prompt_total, kv_width), jnp.bfloat16),
            jax.ShapeDtypeStruct((tail_total, kv_width), jnp.float32),
            jax.ShapeDtypeStruct((tail_total, kv_width), jnp.float32),
        ],
        scratch_shapes=[
            pltpu.VMEM((2, key_total, 128), jnp.bfloat16),
            pltpu.VMEM((2, key_total, 128), jnp.bfloat16),
            pltpu.VMEM((128, key_total), jnp.bfloat16),
            pltpu.VMEM((2, key_total, 128), jnp.float32),
            pltpu.VMEM((2, key_total, 128), jnp.float32),
        ],
        compiler_params=pltpu.CompilerParams(vmem_limit_bytes=VMEM_GRANT),
        cost_estimate=pl.CostEstimate(
            flops=10 * HEADS * rows * key_total * 64,
            bytes_accessed=12 * rows * width,
            transcendentals=HEADS * rows * key_total,
        ),
        name="attend_back",
    )(
        place,
        projected,
        upstream,
        prompt_pairs,
        prompt_pairs,
        tail_pairs,
        tail_pairs,
        across,
        cosines,
        sines,
    )


def pair_tables(position):
    frequency = ROPE_BASE ** (-jnp.arange(HEAD // 2, dtype=jnp.float32) * 2.0 / HEAD)
    angles = position.astype(jnp.float32)[:, None] * frequency[None, :]
    cosine, sine = jnp.cos(angles), jnp.sin(angles)
    return (
        jnp.concatenate([cosine, cosine, cosine, cosine], axis=1),
        jnp.concatenate([sine, -sine, sine, -sine], axis=1),
    )


def turn(flat, cosines, sines):
    front = lax.broadcasted_iota(jnp.int32, flat.shape, 1) % 64 < 32
    partner = jnp.where(front, pltpu.roll(flat, 96, 1), pltpu.roll(flat, 32, 1))
    return flat * cosines + partner * sines


def project_kernel(turned_blocks, x_ref, w_ref, cos_ref, sin_ref, o_ref):
    made = matmul(x_ref[...], w_ref[...])
    rotates = pl.program_id(0) < turned_blocks
    for lanes in (slice(0, 128), slice(128, 256)):
        part = made[:, lanes]
        o_ref[:, lanes] = jnp.where(
            rotates, turn(part, cos_ref[...], -sin_ref[...]), part
        ).astype(jnp.bfloat16)


def project(normed, weights, cosines, sines):
    rows, width = normed.shape
    columns = (HEADS + 2 * KV_HEADS) * HEAD
    table = pl.BlockSpec((rows, 128), lambda j: (0, 0))
    return pl.pallas_call(
        functools.partial(project_kernel, (HEADS + KV_HEADS) * HEAD // 256),
        grid=(columns // 256,),
        in_specs=[
            pl.BlockSpec((rows, width), lambda j: (0, 0)),
            pl.BlockSpec((width, 256), lambda j: (0, j)),
            table,
            table,
        ],
        out_specs=pl.BlockSpec((rows, 256), lambda j: (0, j)),
        out_shape=jax.ShapeDtypeStruct((rows, columns), jnp.bfloat16),
        compiler_params=pltpu.CompilerParams(vmem_limit_bytes=VMEM_GRANT),
        cost_estimate=pl.CostEstimate(
            flops=2 * rows * width * columns, bytes_accessed=2 * width * columns, transcendentals=0
        ),
        name="project",
    )(normed, weights, cosines, sines)


def experts_kernel(
    place_ref, x_ref, g_ref, up_ref, down_ref, router_ref, codes_ref, dx_ref, dgu_ref, act_ref
):
    local_experts, hidden = down_ref.shape[0], down_ref.shape[1]
    width = x_ref.shape[1]
    x, g = x_ref[...], g_ref[...]
    logits = matmul(x, router_ref[...])
    codes = codes_ref[...].astype(jnp.float32)
    gates = gates_of(logits, codes)
    kept = codes > 1.5
    lane = lax.broadcasted_iota(jnp.int32, logits.shape, 1)
    placed = jnp.zeros(logits.shape, jnp.float32)
    total = None
    for local in range(local_experts):
        number = place_ref[2] + local
        mine = (lane == number) & kept
        weight = jnp.sum(jnp.where(mine, gates, 0.0), axis=1, keepdims=True)
        made = matmul(x, up_ref[local])
        act_grad = matmul_nt(g, down_ref[local])
        gate_part, up_part = made[:, :hidden], made[:, hidden:]
        sigma = jax.nn.sigmoid(gate_part)
        silu = gate_part * sigma
        acted = (silu * up_part).astype(jnp.bfloat16).astype(jnp.float32)
        act_ref[local] = (weight * acted).astype(jnp.bfloat16)
        pair_grad = RESIDUAL * jnp.sum(acted * act_grad, axis=1, keepdims=True)
        placed = jnp.where(mine, pair_grad, placed)
        scaled = (RESIDUAL * weight) * act_grad
        gate_grad = scaled * up_part * sigma * (1.0 + gate_part * (1.0 - sigma))
        both = jnp.concatenate([gate_grad, scaled * silu], axis=1).astype(jnp.bfloat16)
        dgu_ref[local] = both
        part = matmul_nt(both, up_ref[local])
        total = part if total is None else total + part
    dx_ref[:, :width] = total.astype(jnp.bfloat16)
    high = placed.astype(jnp.bfloat16).astype(jnp.float32)
    rest = pltpu.roll(placed - high, 64, 1)
    dx_ref[:, width:] = (high + rest).astype(jnp.bfloat16)


def experts(place, rows_in, rows_grad, gate_up, down, weights, codes):
    total, width = rows_in.shape
    local_experts, hidden = down.shape[0], down.shape[1]
    step = 256
    whole = pl.Buffered(1)
    return pl.pallas_call(
        experts_kernel,
        grid=(total // step,),
        in_specs=[
            pl.BlockSpec(memory_space=pltpu.SMEM),
            pl.BlockSpec((step, width), lambda i: (i, 0)),
            pl.BlockSpec((step, width), lambda i: (i, 0)),
            pl.BlockSpec(gate_up.shape, lambda i: (0, 0, 0), pipeline_mode=whole),
            pl.BlockSpec(down.shape, lambda i: (0, 0, 0), pipeline_mode=whole),
            pl.BlockSpec((width, 128), lambda i: (0, 0), pipeline_mode=whole),
            pl.BlockSpec((step, 128), lambda i: (i, 0)),
        ],
        out_specs=[
            pl.BlockSpec((step, width + 128), lambda i: (i, 0)),
            pl.BlockSpec((local_experts, step, 2 * hidden), lambda i: (0, i, 0)),
            pl.BlockSpec((local_experts, step, hidden), lambda i: (0, i, 0)),
        ],
        out_shape=[
            jax.ShapeDtypeStruct((total, width + 128), jnp.bfloat16),
            jax.ShapeDtypeStruct((local_experts, total, 2 * hidden), jnp.bfloat16),
            jax.ShapeDtypeStruct((local_experts, total, hidden), jnp.bfloat16),
        ],
        compiler_params=pltpu.CompilerParams(vmem_limit_bytes=VMEM_GRANT),
        cost_estimate=pl.CostEstimate(
            flops=10 * total * width * local_experts * hidden,
            bytes_accessed=16 * total * width,
            transcendentals=total * local_experts * hidden,
        ),
        name="experts",
    )(place, rows_in, rows_grad, gate_up, down, weights, codes)


def dense_grads_kernel(
    normed_ref, ffn_ref, att_ref, right_ref, out_right_ref, extra_ref, o_ref, *, mixed
):
    block = pl.program_id(0)

    @pl.when(block < mixed)
    def _():
        o_ref[...] = matmul(normed_ref[...], right_ref[...]).astype(jnp.bfloat16)

    @pl.when(block == mixed)
    def _():
        o_ref[:, :256] = matmul(normed_ref[...], right_ref[:, :256]).astype(jnp.bfloat16)
        o_ref[:, 256:] = (matmul(ffn_ref[...], right_ref[:, 256:]) + extra_ref[...]).astype(
            jnp.bfloat16
        )

    @pl.when(block > mixed)
    def _():
        o_ref[...] = matmul(att_ref[...], out_right_ref[...]).astype(jnp.bfloat16)


def dense_weight_grads(normed, ffn_in, attended, right, out_right, extra):
    features, rows = normed.shape
    mixed = right.shape[1] // 384 - 1
    columns = right.shape[1] + out_right.shape[1]
    whole = pl.BlockSpec((features, rows), lambda j: (0, 0))
    return pl.pallas_call(
        functools.partial(dense_grads_kernel, mixed=mixed),
        grid=(columns // 384,),
        in_specs=[
            whole,
            whole,
            whole,
            pl.BlockSpec((rows, 384), lambda j: (0, jnp.minimum(j, mixed))),
            pl.BlockSpec((rows, 384), lambda j: (0, jnp.maximum(j - mixed - 1, 0))),
            pl.BlockSpec((features, 128), lambda j: (0, 0)),
        ],
        out_specs=pl.BlockSpec((features, 384), lambda j: (0, j)),
        out_shape=jax.ShapeDtypeStruct((features, columns), jnp.bfloat16),
        compiler_params=pltpu.CompilerParams(vmem_limit_bytes=VMEM_GRANT),
        cost_estimate=pl.CostEstimate(
            flops=2 * features * rows * columns,
            bytes_accessed=2 * features * columns,
            transcendentals=0,
        ),
        name="dense_weight_grads",
    )(normed, ffn_in, attended, right, out_right, extra)


def on_device(
    layer_in,
    grad_out,
    attn_gain,
    query_proj,
    key_proj,
    value_proj,
    out_proj,
    ffn_gain,
    router_proj,
    gate_up,
    down_proj,
    routes,
    drop_rank,
):
    tok_rows, width = layer_in.shape
    local_experts = gate_up.shape[0]
    hidden_units = down_proj.shape[1]
    top_count = routes.shape[1]
    owner_count = lax.axis_size("expert")
    owner_index = lax.axis_index("expert")
    expert_total = local_experts * owner_count
    capacity = 5 * tok_rows * top_count // (4 * expert_total)
    prompt_rows = PROMPT_DEV
    half_rows = tok_rows - prompt_rows
    prompt_total = prompt_rows * owner_count
    head_size = HEAD
    kv_heads = KV_HEADS
    kv_width = kv_heads * head_size
    dp_count = lax.axis_size("dp")
    shard_rows = query_proj.shape[0]
    piece_rows = shard_rows // owner_count

    def whole_of(shard):
        columns = shard.shape[1]
        piece = lax.dynamic_slice_in_dim(shard, owner_index * piece_rows, piece_rows, 0)
        piece = lax.all_gather(piece, "dp", axis=0, tiled=True)
        piece = lax.all_gather(piece, "expert", axis=0, tiled=True)
        piece = piece.reshape(owner_count, dp_count, piece_rows, columns)
        return piece.transpose(1, 0, 2, 3).reshape(dp_count * shard_rows, columns)

    extras = jnp.concatenate(
        [
            router_proj,
            attn_gain[:, None],
            ffn_gain[:, None],
            jnp.zeros((shard_rows, 126 - router_proj.shape[1]), jnp.bfloat16),
        ],
        axis=1,
    )
    fused = whole_of(jnp.concatenate([query_proj, key_proj, value_proj], axis=1))
    spread = lax.dynamic_update_slice(
        jnp.zeros((dp_count * shard_rows, 128), jnp.bfloat16),
        extras,
        (lax.axis_index("dp") * shard_rows, 0),
    )
    extra_full = lax.psum(spread, "dp")
    full_out = whole_of(out_proj)
    codes = slot_codes(routes, drop_rank.reshape(tok_rows, top_count), expert_total, capacity)
    codes_all = lax.all_gather(
        jnp.pad(codes, ((0, 0), (0, 128 - expert_total))).astype(jnp.bfloat16),
        "expert",
        axis=0,
        tiled=True,
    )
    fused, codes_all = lax.optimization_barrier((fused, codes_all))
    q_width = query_proj.shape[1]
    extra_at = q_width + 2 * kv_width
    full_router = extra_full[:, :expert_total]
    gain_one = extra_full[:, expert_total]
    gain_two = extra_full[:, expert_total + 1]
    grad_all = lax.all_gather(grad_out, "expert", axis=0, tiled=True)
    gain_one = gain_one.astype(jnp.float32)
    gain_two = gain_two.astype(jnp.float32)
    inputs = layer_in.astype(jnp.float32)
    normed_full, inverse_one = norm_forward(inputs, gain_one)
    normed = normed_full.astype(jnp.bfloat16)
    row_index = jnp.arange(tok_rows, dtype=jnp.int32)
    parity = owner_index % 2
    position = jnp.where(
        row_index < prompt_rows,
        owner_index * prompt_rows + row_index,
        prompt_total + parity * half_rows + row_index - prompt_rows,
    )
    place = jnp.stack(
        [owner_index * prompt_rows, parity, owner_index * local_experts]
    ).astype(jnp.int32)
    cosines, sines = pair_tables(position)
    projected = project(normed, fused, cosines, sines)
    own_pairs = projected[:, q_width:]
    prompt_pairs = lax.all_gather(own_pairs[:prompt_rows], "expert", axis=0, tiled=True)
    ahead = [(source, source + 1) for source in range(0, owner_count, 2)]
    partner_pairs = lax.ppermute(own_pairs[prompt_rows:], "expert", ahead)
    tail_pairs = jnp.concatenate([partner_pairs, own_pairs[prompt_rows:]], axis=0)
    att_low, stats = attend(place, projected, prompt_pairs, tail_pairs)
    attn_proj = jnp.dot(att_low, full_out, preferred_element_type=jnp.float32)
    mixed_rows = inputs + RESIDUAL * attn_proj
    ffn_full, inverse_two = norm_forward(mixed_rows, gain_two)
    ffn_low = ffn_full.astype(jnp.bfloat16)
    ffn_low, grad_all = lax.optimization_barrier((ffn_low, grad_all))
    ffn_all = lax.all_gather(ffn_low, "expert", axis=0, tiled=True)
    gates = gates_of(
        jnp.dot(ffn_low, full_router, preferred_element_type=jnp.float32), codes
    )
    input_rows, mixed_grad, acted_low = experts(
        place, ffn_all, grad_all, gate_up, down_proj, extra_full, codes_all
    )
    back_rows = lax.psum_scatter(
        input_rows, "expert", scatter_dimension=0, tiled=True
    ).astype(jnp.float32)
    gateup_local = jnp.einsum(
        "td,etf->edf", ffn_all, mixed_grad, preferred_element_type=jnp.float32
    )
    down_local = RESIDUAL * jnp.einsum(
        "etf,td->efd", acted_low, grad_all, preferred_element_type=jnp.float32
    )
    upstream = grad_out.astype(jnp.float32)
    gate_grad = (
        back_rows[:, width : width + expert_total]
        + back_rows[:, width + 64 : width + 64 + expert_total]
    )
    logit_grad = (
        gates * (gate_grad - jnp.sum(gates * gate_grad, axis=1, keepdims=True))
    ).astype(jnp.bfloat16)
    ffn_grad = jnp.einsum("te,de->td", logit_grad, full_router, preferred_element_type=jnp.float32)
    ffn_grad = ffn_grad + back_rows[:, :width]
    norm_part, gain_two_local = norm_backward(mixed_rows, inverse_two, gain_two, ffn_grad)
    mixed_grad_total = upstream + norm_part
    attn_grad_low = (RESIDUAL * mixed_grad_total).astype(jnp.bfloat16)
    moe_part = jnp.einsum(
        "etf,efd->td", acted_low, down_proj, preferred_element_type=jnp.float32
    ).astype(jnp.bfloat16)
    gateup_low = gateup_local.astype(jnp.bfloat16).reshape(-1, 2 * hidden_units)
    down_low = down_local.astype(jnp.bfloat16).reshape(-1, width)
    unit = gateup_low.shape[0] // 192
    down_cut = down_low.shape[0] // 64 * 43
    parts = [
        (gateup_low[: 40 * unit],),
        (gateup_low[40 * unit : 112 * unit],),
        (gateup_low[112 * unit : 183 * unit],),
        (gateup_low[183 * unit :], down_low[:down_cut]),
        (down_low[down_cut:],),
    ]
    attended_grad = jnp.einsum(
        "td,cd->tc", attn_grad_low, full_out, preferred_element_type=jnp.float32
    ).astype(jnp.bfloat16)
    sums = [lax.psum(parts[0], "dp")]
    attended_grad, moe_part, sums, parts = lax.optimization_barrier(
        (attended_grad, moe_part, sums, parts)
    )
    for part in parts[1:]:
        part, sums[-1] = lax.optimization_barrier((part, sums[-1]))
        sums.append(lax.psum(part, "dp"))
    gateup_grad = jnp.concatenate([sums[0][0], sums[1][0], sums[2][0], sums[3][0]], axis=0)
    gateup_grad = gateup_grad.astype(jnp.float32).reshape(gate_up.shape)
    down_grad = jnp.concatenate([sums[3][1], sums[4][0]], axis=0)
    down_grad = down_grad.astype(jnp.float32).reshape(down_proj.shape)

    def by_piece(values):
        turned = values.T.reshape(dp_count, owner_count, piece_rows, tok_rows)
        return turned.transpose(1, 0, 2, 3).reshape(width, tok_rows)

    query_grad_low, prompt_key_part, prompt_value_part, tail_key_part, tail_value_part = (
        attend_back(
            place, projected, attended_grad, prompt_pairs, tail_pairs, stats, cosines, sines
        )
    )
    moe_rows = lax.psum_scatter(moe_part, "expert", scatter_dimension=0, tiled=True)
    moe_rows, prompt_key_part = lax.optimization_barrier((moe_rows, prompt_key_part))
    prompt_grad = lax.psum_scatter(
        jnp.concatenate([prompt_key_part, prompt_value_part], axis=1),
        "expert",
        scatter_dimension=0,
        tiled=True,
    )
    layer_out = (mixed_rows + RESIDUAL * moe_rows.astype(jnp.float32)).astype(jnp.bfloat16)
    prompt_grad = prompt_grad.astype(jnp.float32)
    tail_part = jnp.concatenate([tail_key_part, tail_value_part], axis=1)
    behind = [(source + 1, source) for source in range(0, owner_count, 2)]
    tail_grad = tail_part[half_rows:] + lax.ppermute(
        tail_part[:half_rows].astype(jnp.bfloat16), "expert", behind
    ).astype(jnp.float32)
    pair_grad = jnp.concatenate([prompt_grad, tail_grad], axis=0)
    cosine, sine_part = rotary_tables(position, head_size)
    key_grad_low = (
        unrotate(pair_grad[:, :kv_width].reshape(tok_rows, kv_heads, head_size), cosine, sine_part)
        .reshape(tok_rows, kv_width)
        .astype(jnp.bfloat16)
    )
    value_grad_low = pair_grad[:, kv_width:].astype(jnp.bfloat16)
    all_grad = jnp.concatenate(
        [
            query_grad_low,
            key_grad_low,
            value_grad_low,
            jnp.pad(logit_grad, ((0, 0), (0, 128 - expert_total))),
        ],
        axis=1,
    )
    normed_grad = jnp.einsum(
        "tc,dc->td",
        all_grad[:, :extra_at],
        fused,
        preferred_element_type=jnp.float32,
    )
    input_part, gain_one_local = norm_backward(inputs, inverse_one, gain_one, normed_grad)
    input_grad = (mixed_grad_total + input_part).astype(jnp.bfloat16)

    def summed(pieces):
        pieces = lax.psum_scatter(pieces, "expert", scatter_dimension=0, tiled=True)
        pieces = lax.psum_scatter(pieces, "dp", scatter_dimension=0, tiled=True)
        return lax.all_gather(pieces, "expert", axis=0, tiled=True).astype(jnp.float32)

    extra = jnp.stack([gain_one_local, gain_two_local], axis=1)
    extra = extra.reshape(dp_count, owner_count, piece_rows, 2).transpose(1, 0, 2, 3)
    extra = jnp.pad(
        extra.reshape(width, 2), ((0, 0), (expert_total, 126 - expert_total))
    )
    late = summed(
        dense_weight_grads(
            by_piece(normed), by_piece(ffn_low), by_piece(att_low), all_grad, attn_grad_low, extra
        )
    )
    dense_grads = (
        late[:, extra_at + expert_total],
        late[:, :q_width],
        late[:, q_width : q_width + kv_width],
        late[:, q_width + kv_width : extra_at],
        late[:, extra_at + 128 :],
        late[:, extra_at + expert_total + 1],
        late[:, extra_at : extra_at + expert_total],
    )
    return (
        layer_out,
        input_grad,
        dense_grads[0],
        dense_grads[1],
        dense_grads[2],
        dense_grads[3],
        dense_grads[4],
        dense_grads[5],
        dense_grads[6],
        gateup_grad,
        down_grad,
    )


def solution(mesh):
    placed = (
        P(("dp", "expert"), None),
        P(("dp", "expert"), None),
        P("dp"),
        P("dp", None),
        P("dp", None),
        P("dp", None),
        P("dp", None),
        P("dp"),
        P("dp", None),
        P("expert", None, None),
        P("expert", None, None),
        P(("dp", "expert"), None),
        P(("dp", "expert"), None),
    )
    return jax.shard_map(
        on_device,
        mesh=mesh,
        in_specs=placed,
        out_specs=(
            P(("dp", "expert"), None),
            P(("dp", "expert"), None),
            P("dp"),
            P("dp", None),
            P("dp", None),
            P("dp", None),
            P("dp", None),
            P("dp"),
            P("dp", None),
            P("expert", None, None),
            P("expert", None, None),
        ),
        check_vma=False,
    )
```

time: 1900 us -> 920 us (0.48)
  waiting for transfers between devices: 1020 us -> 466 us
  matrix products: 311 us -> 74.1 us
  local copies, waits for them, and re-layouts: 263 us -> 81.2 us
  Pallas kernels: 0 us -> 158 us
  other arithmetic: 173 us -> 45.8 us
  starting transfers between devices: 31.2 us -> 5.38 us
    all_to_all x4 -> x0, waiting for transfers between devices: 364 us -> none  [the longest x1 112 us: on_device(): lax.all_to_all(grad_send, 'expert', split_axis=0, concat_axis=0, tiled=True)]
    dot_general x38 -> x5, matrix products: 302 us -> 67.5 us  [the longest x1 26.2 us: on_device(): jnp.einsum('td,etf->edf', ffn_all, mixed_grad, preferred_element_type=jnp...]
    psum x2 -> x6, waiting for transfers between devices: 327 us -> 167 us  [the longest x4 117 us: on_device(): sums.append(lax.psum(part, 'dp'))]
    pallas_call x0 -> x5, Pallas kernels: none -> 158 us  [the longest x1 65 us: experts(): pl.pallas_call(experts_kernel, grid=(total // step,), in_specs=[pl.BlockS...]
    gather x10 -> x0, local copies, waits for them, and re-layouts: 136 us -> none  [the longest x1 25.5 us: on_device(): jnp.take(produced_flat, picked, axis=0).reshape(tok_rows, top_count, width)]
    reduce_scatter x4 -> x5, waiting for transfers between devices: 246 us -> 151 us  [the longest x1 61 us: summed(): pieces = lax.psum_scatter(pieces, 'expert', scatter_dimension=0, tiled=True)]
    all_gather x6, waiting for transfers between devices: 69.7 us -> 146 us  [the longest x1 61.2 us: on_device(): ffn_all = lax.all_gather(ffn_low, 'expert', axis=0, tiled=True)]
    reduce_sum x9 -> x3, other arithmetic: 75.3 us -> 1.84 us  [the longest x1 1.29 us: slot_codes(): jnp.sum((by_expert[:, :, None] < by_expert[:, None, :]).astype(jnp.int32)...]
  transfers between devices with their start and end apart: 23 -> 19, of which waited for: 16 -> 14; matrix products, arithmetic and copies ran while one was open for 26% -> 19% of each run, Pallas kernels for 0% -> 10%
where the time goes in v1:
time: 920 us; the launch traced here: 914 us
  waiting for transfers between devices  466 us (51%)
  Pallas kernels  158 us (17%)
  local copies, waits for them, and re-layouts  81.2 us (9%)
  matrix products  74.1 us (8%)
  blocking collectives  65.9 us (7%)
  other arithmetic  45.8 us (5%)
  between operations  16.8 us (2%)
    psum x4, waiting for transfers between devices, on_device(): sums.append(lax.psum(part, 'dp'))  117 us
    pallas_call x1, Pallas kernels, experts(): pl.pallas_call(experts_kernel, grid=(total // step,), in_specs=[pl.BlockS...  65 us
    all_gather x1, waiting for transfers between devices, on_device(): ffn_all = lax.all_gather(ffn_low, 'expert', axis=0, tiled=True)  61.2 us
    reduce_scatter x1, waiting for transfers between devices, summed(): pieces = lax.psum_scatter(pieces, 'expert', scatter_dimension=0, tiled=True)  61 us
    all_gather x2, blocking collectives, whole_of(): piece = lax.all_gather(piece, 'dp', axis=0, tiled=True)  50.5 us
    psum x1, waiting for transfers between devices, on_device(): sums = [lax.psum(parts[0], 'dp')]  49.7 us
    pallas_call x1, Pallas kernels, attend_back(): pl.pallas_call(attend_back_kernel, grid=(pairs,), in_specs=[pl.BlockSpec(...  42.3 us
    reduce_scatter x1, waiting for transfers between devices, summed(): pieces = lax.psum_scatter(pieces, 'dp', scatter_dimension=0, tiled=True)  37.2 us
  transfers between devices with their start and end apart: 19, of which 14 were waited for; matrix products, arithmetic and copies ran while one was open for 19% of the time, Pallas kernels for 10%

profile of v1, /device:TPU:0, one launch (start us, length us, event | category | flops | bytes accessed | tf_op | source)
XLA Modules:
  0.0 913.7 jit_solution(15278541948439739706)
XLA Ops:
  12.7 30.2 %all_gather.27 = bf16[192,2560]{1,0:T(8,128)(2,1)} all-gather(bf16[48,2560]{1,0:T(8,128)(2,1)S(1)} %fusion.34), channel_id=1, replica_groups=mesh['dp'=4,'expert'=8] {'dp'}, dimensions={0}, use_global_device_ids=true | all-gather | bytes 1228800 | tf_op jit(solution)/shard_map/all_gather | solution.py:589
  43.1 20.2 %all_gather.31 = bf16[192,1536]{1,0:T(8,128)(2,1)} all-gather(bf16[48,1536]{1,0:T(8,128)(2,1)S(1)} %constant_dynamic-slice_fusion), channel_id=1, replica_groups=mesh['dp'=4,'expert'=8] {'dp'}, dimensions={0}, use_global_device_ids=true | all-gather | bytes 737280 | tf_op jit(solution)/shard_map/all_gather | solution.py:589
  68.4 15.4 %all_gather.29.codes_ref = bf16[3072,128]{1,0:T(8,128)(2,1)} all-gather(bf16[384,128]{1,0:T(8,128)(2,1)S(1)} %pad.13), channel_id=1, replica_groups=mesh['dp'=4,'expert'=8] {'expert'}, dimensions={0}, use_global_device_ids=true | all-gather | bytes 884736 | tf_op jit(solution)/shard_map/all_gather | solution.py:612
  84.2 1.7 convert_reduce_fusion.1
  86.3 11.7 %all-gather.7.cloned.1.call-done = bf16[1536,2560]{1,0:T(8,128)(2,1)} async-done(((bf16[192,2560]{1,0:T(8,128)(2,1)}), bf16[1536,2560]{1,0:T(8,128)(2,1)}) %all-gather.7.cloned.1.call-update) | async-done | bytes 7864336 | tf_op jit(solution)/shard_map/all_gather | solution.py:590
  97.9 7.1 copy.125
  105.1 10.0 %project.1.q_ref = bf16[384,2560]{1,0:T(8,128)(2,1)S(1)} custom-call(bf16[384,1536]{1,0:T(8,128)(2,1)S(1)} %fusion.11.x_ref, bf16[1536,2560]{1,0:T(8,128)(2,1)} %bitcast.76, f32[384,128]{1,0:T(8,128)S(1)} %get-tuple-element.162.cos_ref, f32[384,128]{1,0:T(8,128)S(1)} %copy-done.7), custom_call_target="tpu_custom_call" | custom-call | flops 3019898880 | bytes 7864320 | tf_op jit(solution)/shard_map/project/pallas_call | solution.py:410
  116.7 2.4 collective-permute-start
  119.1 19.5 %all-gather.11.cloned.1.call-done = bf16[1536,1536]{1,0:T(8,128)(2,1)} async-done(((bf16[192,1536]{1,0:T(8,128)(2,1)}), bf16[1536,1536]{1,0:T(8,128)(2,1)}) %all-gather.11.cloned.1.call-update) | async-done | bytes 4718608 | tf_op jit(solution)/shard_map/all_gather | solution.py:590
  138.6 4.9 copy.130
  143.6 25.3 %all-gather.9.cloned.1.call-done.pk_ref.pv_ref = bf16[1024,1024]{1,0:T(8,128)(2,1)} async-done(((bf16[128,1024]{1,0:T(8,128)(2,1)}), bf16[1024,1024]{1,0:T(8,128)(2,1)}) %all-gather.9.cloned.1.call-update) | async-done | bytes 2097168 | tf_op jit(solution)/shard_map/all_gather | solution.py:643
  168.9 27.1 %attend.1 = (bf16[384,1536]{1,0:T(8,128)(2,1)S(1)}, f32[4,384,128]{2,1,0:T(8,128)S(1)}) custom-call(s32[3]{0:T(128)S(1)} %pad_add_fusion.place_ref, bf16[384,2560]{1,0:T(8,128)(2,1)} %copy-done.2, bf16[1024,1024]{1,0:T(8,128)(2,1)} %all-gather.9.cloned.1.call-done.pk_ref.pv_ref, bf16[1024,1024]{1,0:T(8,128)(2,1)} %all-gather.9.cloned.1.call-done.pk_ref.pv_ref, ...), custom_call_target="tpu_custom_call" | custom-call | flops 3623878656 | bytes 3538944 | tf_op jit(solution)/shard_map/attend/pallas_call | solution.py:187
  196.0 2.1 multiply_reduce_fusion.2
  198.1 1.4 copy-done.9
  200.8 28.8 %all-gather.13.cloned.1.call-done.g_ref = bf16[3072,1536]{1,0:T(8,128)(2,1)} async-done(((bf16[384,1536]{1,0:T(8,128)(2,1)}), bf16[3072,1536]{1,0:T(8,128)(2,1)}) %all-gather.13.cloned.1.call-update) | async-done | bytes 9437200 | tf_op jit(solution)/shard_map/all_gather | solution.py:624
  229.7 61.2 %all-gather.15.cloned.1.call-done.x_ref = bf16[3072,1536]{1,0:T(8,128)(2,1)} async-done(((bf16[384,1536]{1,0:T(8,128)(2,1)}), bf16[3072,1536]{1,0:T(8,128)(2,1)}) %all-gather.15.cloned.1.call-update) | async-done | bytes 9437200 | tf_op jit(solution)/shard_map/all_gather | solution.py:653
  292.1 65.0 %experts.1 = (bf16[3072,1664]{1,0:T(8,128)(2,1)}, bf16[2,3072,1024]{2,1,0:T(8,128)(2,1)}, bf16[2,3072,512]{2,1,0:T(8,128)(2,1)}) custom-call(s32[3]{0:T(128)S(1)} %pad_add_fusion.place_ref, bf16[3072,1536]{1,0:T(8,128)(2,1)} %all-gather.15.cloned.1.call-done.x_ref, bf16[3072,1536]{1,0:T(8,128)(2,1)} %all-gather.13.cloned.1.call-done.g_ref, ...), custom_call_target="tpu_custom_call" | custom-call | flops 48318382080 | bytes 75497472 | tf_op jit(solution)/shard_map/experts/pallas_call | solution.py:472
  358.0 1.8 select_reduce_fusion
  360.1 15.0 %multiply_convert_fusion = bf16[2,512,1536]{2,1,0:T(8,128)(2,1)S(1)} fusion(bf16[2,3072,512]{2,1,0:T(8,128)(2,1)} %get-tuple-element.51, bf16[3072,1536]{1,0:T(8,128)(2,1)} %all-gather.13.cloned.1.call-done.g_ref), kind=kOutput, calls=%fused_computation.7 | convolution fusion | flops 9666822144 | bytes 18874368 | tf_op jit(solution)/shard_map/etf,td->efd/dot_general | solution.py:666
  375.1 1.5 slice.132
  377.6 26.2 %convert_bitcast_fusion = bf16[2,1536,1024]{1,2,0:T(8,128)(2,1)} fusion(bf16[2,3072,1024]{2,1,0:T(8,128)(2,1)} %get-tuple-element.52, bf16[3072,1536]{1,0:T(8,128)(2,1)} %all-gather.15.cloned.1.call-done.x_ref), kind=kOutput, calls=%fused_computation.8 | convolution fusion | flops 19330498560 | bytes 28311552 | tf_op jit(solution)/shard_map/td,etf->edf/dot_general | solution.py:663
  403.8 8.7 copy.134
  412.5 2.5 slice.128
  415.0 3.3 slice.129
  418.3 3.3 slice.130
  421.5 1.7 slice.131
  423.2 15.2 %bitcast_convert_fusion = bf16[3072,1536]{1,0:T(8,128)(2,1)} fusion(bf16[2,3072,512]{2,1,0:T(8,128)(2,1)} %get-tuple-element.51, bf16[2,512,1536]{2,1,0:T(8,128)(2,1)} %down_ref.1), kind=kOutput, calls=%fused_computation | convolution fusion | flops 9668395008 | bytes 18874368 | tf_op jit(solution)/shard_map/etf,efd->td/dot_general | solution.py:682
  438.7 1.6 convert_element_type.122
  441.0 1.4 multiply_reduce_fusion
  445.7 3.0 convolution_convert_fusion.do_ref
  448.8 49.7 %all-reduce.13.cloned.1.call-done = bf16[640,1024]{1,0:T(8,128)(2,1)} async-done(((bf16[640,1024]{1,0:T(8,128)(2,1)}), bf16[640,1024]{1,0:T(8,128)(2,1)}) %all-reduce.13.cloned.1.call-update) | async-done | bytes 1310736 | tf_op jit(solution)/shard_map/psum | solution.py:699
  500.5 42.3 %attend_back.1 = (bf16[384,1536]{1,0:T(8,128)(2,1)}, bf16[1024,512]{1,0:T(8,128)(2,1)S(1)}, bf16[1024,512]{1,0:T(8,128)(2,1)S(1)}, f32[512,512]{1,0:T(8,128)S(1)}, f32[512,512]{1,0:T(8,128)}) custom-call(s32[3]{0:T(128)S(1)} %pad_add_fusion.place_ref, bf16[384,2560]{1,0:T(8,128)(2,1)} %copy-done.2, bf16[384,1536]{1,0:T(8,128)(2,1)} %convolution_convert_fusion.do_ref, ...), custom_call_target="tpu_custom_call" | custom-call | flops 9059696640 | bytes 7077888 | tf_op jit(solution)/shard_map/attend_back/pallas_call | solution.py:329
  543.8 30.8 %reduce-scatter.8.cloned.1.call-done = bf16[384,1536]{1,0:T(8,128)(2,1)} async-done(((bf16[3072,1536]{1,0:T(8,128)(2,1)}), bf16[384,1536]{1,0:T(8,128)(2,1)}) %reduce-scatter.8.cloned.1.call-update) | async-done | bytes 1179664 | tf_op jit(solution)/shard_map/reduce_scatter | solution.py:720
  574.6 2.8 pad_maximum_fusion.2
  577.5 1.7 copy.138
  581.7 1.5 collective-permute-start.1
  583.6 1.4 copy.141
  585.0 1.5 copy.142
  586.5 1.4 copy.143
  587.9 1.4 copy.144
  589.3 1.4 copy.145
  590.7 2.5 copy.146
  593.9 1.5 slice_add_fusion
  595.4 2.3 all-reduce.15.cloned.1.call-done
  597.8 22.1 %reduce-scatter.10.cloned.1.call-done = bf16[128,1024]{1,0:T(8,128)(2,1)} async-done(((bf16[1024,1024]{1,0:T(8,128)(2,1)}), bf16[128,1024]{1,0:T(8,128)(2,1)}) %reduce-scatter.10.cloned.1.call-update) | async-done | bytes 262160 | tf_op jit(solution)/shard_map/reduce_scatter | solution.py:722
  622.7 2.3 copy.137
  627.1 1.9 copy.140
  630.2 9.3 %fusion.20 = (f32[1536]{0:T(1024)}, f32[384]{0:T(512)}, f32[384,1536]{1,0:T(8,128)}) fusion(bf16[384,1536]{1,0:T(8,128)(2,1)S(1)} %copy-done.17, f32[384]{0:T(512)} %copy-done.47, f32[1536]{0:T(1024)S(1)} %copy-done.43, bf16[1536,2560]{1,0:T(8,128)(2,1)} %bitcast.77, bf16[384,512]{1,0:T(8,128)(2,1)S(1)} %fusion.29, bf16[384,512]{1,0:T(8,128)(2,1)} %copy.140, ...), kind=kOutput, calls=%fused_computation.31 | convolution fusion | flops 3029923840 | bytes 13384704 | tf_op jit(solution)/shard_map/tc,dc->td/dot_general | solution.py:752
  642.3 1.5 pad.15.extra_ref
  643.8 2.5 fusion.21.right_ref
  646.3 14.1 %dense_weight_grads.1 = bf16[1536,4224]{1,0:T(8,128)(2,1)} custom-call(bf16[1536,384]{1,0:T(8,128)(2,1)S(1)} %bitcast.73, bf16[1536,384]{1,0:T(8,128)(2,1)S(1)} %bitcast.74, bf16[1536,384]{1,0:T(8,128)(2,1)} %bitcast.86, bf16[384,2688]{1,0:T(8,128)(2,1)} %fusion.21.right_ref, bf16[384,1536]{1,0:T(8,128)(2,1)} %copy-done.24, f32[1536,128]{1,0:T(8,128)S(1)} %pad.15.extra_ref), custom_call_target="tpu_custom_call" | custom-call | flops 4982833152 | bytes 12976128 | tf_op jit(solution)/shard_map/dense_weight_grads/pallas_call | solution.py:530
  660.4 33.4 %all-reduce.17.cloned.1.call-done = bf16[1136,1024]{1,0:T(8,128)(2,1)} async-done(((bf16[1136,1024]{1,0:T(8,128)(2,1)}), bf16[1136,1024]{1,0:T(8,128)(2,1)}) %all-reduce.17.cloned.1.call-update) | async-done | bytes 2326544 | tf_op jit(solution)/shard_map/psum | solution.py:705
  693.9 61.0 %reduce-scatter.12.cloned.1.call-done = bf16[192,4224]{1,0:T(8,128)(2,1)} async-done(((bf16[1536,4224]{1,0:T(8,128)(2,1)}), bf16[192,4224]{1,0:T(8,128)(2,1)}) %reduce-scatter.12.cloned.1.call-update) | async-done | bytes 1622032 | tf_op jit(solution)/shard_map/reduce_scatter | solution.py:762
  754.9 38.0 %all-reduce.21.cloned.1.call-done = (bf16[144,1024]{1,0:T(8,128)(2,1)}, bf16[688,1536]{1,0:T(8,128)(2,1)}) async-done(((bf16[144,1024]{1,0:T(8,128)(2,1)}, bf16[688,1536]{1,0:T(8,128)(2,1)}), (bf16[144,1024]{1,0:T(8,128)(2,1)}, bf16[688,1536]{1,0:T(8,128)(2,1)})) %all-reduce.21.cloned.1.call-update) | async-done | bytes 2408464 | tf_op jit(solution)/shard_map/psum | solution.py:705
  793.2 37.2 %reduce-scatter.14.cloned.1.call-done = bf16[48,4224]{1,0:T(8,128)(2,1)} async-done(((bf16[192,4224]{1,0:T(8,128)(2,1)}), bf16[48,4224]{1,0:T(8,128)(2,1)}) %reduce-scatter.14.cloned.1.call-update) | async-done | bytes 405520 | tf_op jit(solution)/shard_map/reduce_scatter | solution.py:763
  830.5 3.2 pad_maximum_fusion
  833.7 6.3 convert.25
  840.0 43.4 %all-reduce.19.cloned.1.call-done = bf16[336,1536]{1,0:T(8,128)(2,1)} async-done(((bf16[336,1536]{1,0:T(8,128)(2,1)}), bf16[336,1536]{1,0:T(8,128)(2,1)}) %all-reduce.19.cloned.1.call-update) | async-done | bytes 1032208 | tf_op jit(solution)/shard_map/psum | solution.py:705
  883.5 1.5 pad_maximum_fusion.1
  885.1 4.1 convert.26
  891.0 3.1 fusion.16
  894.1 2.3 convert_element_type.136
  898.9 4.6 fusion.42
  903.5 2.5 fusion.43
  (213 shorter events, 41.2 us)
Async XLA Ops:
  8.0 35.1 %copy-start = (bf16[384,1536]{1,0:T(8,128)(2,1)S(1)}, bf16[384,1536]{1,0:T(8,128)(2,1)}, u32[]{:S(2)}) copy-start(bf16[384,1536]{1,0:T(8,128)(2,1)} %param.19) | copy-start | bytes 3538948
  8.0 76.2 %all-reduce.11.cloned.1.call-start = ((), (), s32[]{:S(2)}) async-start(), calls=%async_computation.5 | async-start | bytes 786432 | tf_op jit(solution)/shard_map/psum | solution.py:609
  11.7 86.3 %all-gather.7.cloned.1.call-start = ((), (), s32[]{:S(2)}) async-start(), calls=%async_computation.6 | async-start | bytes 8847360 | tf_op jit(solution)/shard_map/all_gather | solution.py:590
  12.7 51.2 %copy-start.52 = (s32[1,3072]{1,0:T(1,128)S(1)}, s32[1,3072]{1,0:T(1,128)}, u32[]{:S(2)}) copy-start(s32[1,3072]{1,0:T(1,128)} %param.25) | copy-start | bytes 36868
  12.7 52.1 %copy-start.53 = (s32[384,8]{0,1:T(8,128)S(1)}, s32[384,8]{0,1:T(8,128)}, u32[]{:S(2)}) copy-start(s32[384,8]{0,1:T(8,128)} %param.24) | copy-start | bytes 36868
  43.0 95.6 %all-gather.11.cloned.1.call-start = ((), (), s32[]{:S(2)}) async-start(), calls=%async_computation.8 | async-start | bytes 5308416 | tf_op jit(solution)/shard_map/all_gather | solution.py:590
  63.3 20.5 %copy-start.14 = (bf16[384,1536]{1,0:T(8,128)(2,1)S(1)}, bf16[384,1536]{1,0:T(8,128)(2,1)}, u32[]{:S(2)}) copy-start(bf16[384,1536]{1,0:T(8,128)(2,1)} %param.13) | copy-start | bytes 3538948
  63.3 105.5 %all-gather.9.cloned.1.call-start = ((), (), s32[]{:S(2)}) async-start(), calls=%async_computation.7 | async-start | bytes 2359296 | tf_op jit(solution)/shard_map/all_gather | solution.py:643
  66.3 19.5 %copy-start.40 = (f32[16,384]{0,1:T(8,128)}, f32[16,384]{0,1:T(8,128)S(1)}, u32[]{:S(2)}) copy-start(f32[16,384]{0,1:T(8,128)S(1)} %copy.127) | copy-start | bytes 73732
  67.4 18.9 %copy-start.30 = (f32[384,32]{1,0:T(8,128)}, f32[384,32]{1,0:T(8,128)S(1)}, u32[]{:S(2)}) copy-start(f32[384,32]{1,0:T(8,128)S(1)} %get-tuple-element.154) | copy-start | bytes 147460
  67.4 18.9 %copy-start.32 = (f32[384,32]{1,0:T(8,128)}, f32[384,32]{1,0:T(8,128)S(1)}, u32[]{:S(2)}) copy-start(f32[384,32]{1,0:T(8,128)S(1)} %get-tuple-element.156) | copy-start | bytes 147460
  84.2 20.9 %copy-start.47 = (f32[384]{0:T(512)}, f32[384]{0:T(512)S(1)}, u32[]{:S(2)}) copy-start(f32[384]{0:T(512)S(1)} %add_rsqrt_fusion.1) | copy-start | bytes 4612
  85.9 19.2 %copy-start.42 = (f32[1536]{0:T(1024)}, f32[1536]{0:T(1024)S(1)}, u32[]{:S(2)}) copy-start(f32[1536]{0:T(1024)S(1)} %get-tuple-element.141) | copy-start | bytes 18436
  97.9 7.1 copy-start.7
  115.0 28.5 %copy-start.2 = (bf16[384,2560]{1,0:T(8,128)(2,1)}, bf16[384,2560]{1,0:T(8,128)(2,1)S(1)}, u32[]{:S(2)}) copy-start(bf16[384,2560]{1,0:T(8,128)(2,1)S(1)} %project.1.q_ref) | copy-start | bytes 5898244
  115.8 113.8 %all-gather.13.cloned.1.call-start = ((), (), s32[]{:S(2)}) async-start(), calls=%async_computation.9 | async-start | bytes 10616832 | tf_op jit(solution)/shard_map/all_gather | solution.py:624
  116.6 174.4 %all-gather.15.cloned.1.call-start = ((), (), s32[]{:S(2)}) async-start(), calls=%async_computation.10 | async-start | bytes 10616832 | tf_op jit(solution)/shard_map/all_gather | solution.py:653
  116.7 26.8 %collective-permute-start = (bf16[256,1024]{1,0:T(8,128)(2,1)S(1)}, bf16[256,1024]{1,0:T(8,128)(2,1)S(1)}, u32[]{:S(2)}, u32[]{:S(2)}) collective-permute-start(bf16[256,1024]{1,0:T(8,128)(2,1)S(1)} %slice.122), channel_id=1, source_target_pairs={{0,1},{2,3},{4,5},{6,7},{8,9},{10,11},{12,13},{14,15},{16,17},{18,... | collective-permute-start | bytes 1572872 | tf_op jit(solution)/shard_map/ppermute | solution.py:645
  143.6 52.3 %copy-start.4 = (bf16[512,1024]{1,0:T(8,128)(2,1)}, bf16[512,1024]{1,0:T(8,128)(2,1)S(1)}, u32[]{:S(2)}) copy-start(bf16[512,1024]{1,0:T(8,128)(2,1)S(1)} %pad_maximum_fusion.3.tk_ref.tv_ref) | copy-start | bytes 3145732
  168.9 27.1 %copy-start.15 = (bf16[384,1536]{1,0:T(8,128)(2,1)S(1)}, bf16[384,1536]{1,0:T(8,128)(2,1)}, u32[]{:S(2)}) copy-start(bf16[384,1536]{1,0:T(8,128)(2,1)} %param.13) | copy-start | bytes 3538948
  168.9 27.1 %copy-start.23 = (bf16[4,8,48,1536]{3,2,1,0:T(8,128)(2,1)S(1)}, bf16[4,8,48,1536]{3,2,1,0:T(8,128)(2,1)}, u32[]{:S(2)}) copy-start(bf16[4,8,48,1536]{3,2,1,0:T(8,128)(2,1)} %copy.130) | copy-start | bytes 14155780
  198.1 244.3 %copy-start.44 = (f32[384]{0:T(512)}, f32[384]{0:T(512)S(1)}, u32[]{:S(2)}) copy-start(f32[384]{0:T(512)S(1)} %add_rsqrt_fusion) | copy-start | bytes 4612
  199.5 91.4 %copy-start.3 = (bf16[1536,128]{1,0:T(8,128)(2,1)S(1)}, bf16[1536,128]{1,0:T(8,128)(2,1)}, u32[]{:S(2)}) copy-start(bf16[1536,128]{1,0:T(8,128)(2,1)} %all-reduce.11.cloned.1.call-done.router_ref) | copy-start | bytes 1179652
  229.6 209.1 %reduce-scatter.6.cloned.1.call-start = ((), (), s32[]{:S(2)}) async-start(), calls=%async_computation.11 | async-start | bytes 11501568 | tf_op jit(solution)/shard_map/reduce_scatter | solution.py:660
  357.1 141.4 %all-reduce.13.cloned.1.call-start = ((), (), s32[]{:S(2)}) async-start(), calls=%async_computation.12 | async-start | bytes 2621440 | tf_op jit(solution)/shard_map/psum | solution.py:699
  438.4 136.2 %reduce-scatter.8.cloned.1.call-start = ((), (), s32[]{:S(2)}) async-start(), calls=%async_computation.13 | async-start | bytes 10616832 | tf_op jit(solution)/shard_map/reduce_scatter | solution.py:720
  438.7 2.2 copy-start.10
  438.7 7.0 slice-start
  441.0 2.8 copy-start.20
  441.0 4.8 slice-start.1
  442.4 2.3 copy-start.50
  498.5 99.2 %all-reduce.15.cloned.1.call-start = ((), (), s32[]{:S(2)}) async-start(), calls=%async_computation.18 | async-start | bytes 4718592 | tf_op jit(solution)/shard_map/psum | solution.py:705
  499.3 120.7 %reduce-scatter.10.cloned.1.call-start = ((), (), s32[]{:S(2)}) async-start(), calls=%async_computation.14 | async-start | bytes 2359296 | tf_op jit(solution)/shard_map/reduce_scatter | solution.py:722
  574.6 4.7 copy-start.31
  577.5 2.6 copy-start.38
  577.5 116.3 %all-reduce.17.cloned.1.call-start = ((), (), s32[]{:S(2)}) async-start(), calls=%async_computation.19 | async-start | bytes 4653056 | tf_op jit(solution)/shard_map/psum | solution.py:705
  580.0 3.2 copy-start.16
  580.0 3.2 copy-start.43
  580.0 3.2 copy-start.48
  581.7 12.2 %collective-permute-start.1 = (bf16[256,1024]{1,0:T(8,128)(2,1)}, bf16[256,1024]{1,0:T(8,128)(2,1)}, u32[]{:S(2)}, u32[]{:S(2)}) collective-permute-start(bf16[256,1024]{1,0:T(8,128)(2,1)} %slice.180), channel_id=1, source_target_pairs={{1,0},{3,2},{5,4},{7,6},{9,8},{11,10},{13,12},{15,14},{17,16},{19,... | collective-permute-start | bytes 1572872 | tf_op jit(solution)/shard_map/ppermute | solution.py:732
  583.6 2.9 copy-start.19
  590.7 2.5 copy-start.46
  595.4 27.3 %copy-start.22 = (f32[256,1024]{1,0:T(8,128)}, f32[256,1024]{1,0:T(8,128)S(1)}, u32[]{:S(2)}) copy-start(f32[256,1024]{1,0:T(8,128)S(1)} %slice_add_fusion) | copy-start | bytes 3145732
  597.8 157.0 %reduce-scatter.12.cloned.1.call-start = ((), (), s32[]{:S(2)}) async-start(), calls=%async_computation.15 | async-start | bytes 14598144 | tf_op jit(solution)/shard_map/reduce_scatter | solution.py:762
  625.0 5.2 copy-start.17
  630.2 9.3 %copy-start.35 = (bf16[384,512]{1,0:T(8,128)(2,1)}, bf16[384,512]{1,0:T(8,128)(2,1)S(1)}, u32[]{:S(2)}) copy-start(bf16[384,512]{1,0:T(8,128)(2,1)S(1)} %fusion.29) | copy-start | bytes 1179652
  639.5 4.3 copy-start.34
  660.4 170.1 %copy-start.27 = (bf16[1152,1024]{1,0:T(8,128)(2,1)S(1)}, bf16[1152,1024]{1,0:T(8,128)(2,1)}, u32[]{:S(2)}) copy-start(bf16[1152,1024]{1,0:T(8,128)(2,1)} %all-reduce.15.cloned.1.call-done) | copy-start | bytes 7077892
  660.4 132.5 %all-reduce.21.cloned.1.call-start = ((), (), s32[]{:S(2)}) async-start(), calls=%async_computation.21 | async-start | bytes 4816896 | tf_op jit(solution)/shard_map/psum | solution.py:705
  693.8 136.6 %reduce-scatter.14.cloned.1.call-start = ((), (), s32[]{:S(2)}) async-start(), calls=%async_computation.16 | async-start | bytes 2027520 | tf_op jit(solution)/shard_map/reduce_scatter | solution.py:763
  754.8 128.6 %all-reduce.19.cloned.1.call-start = ((), (), s32[]{:S(2)}) async-start(), calls=%async_computation.20 | async-start | bytes 2064384 | tf_op jit(solution)/shard_map/psum | solution.py:705
  792.9 101.2 %all-gather.17.cloned.1.call-start = ((), (), s32[]{:S(2)}) async-start(), calls=%async_computation.17 | async-start | bytes 3649536 | tf_op jit(solution)/shard_map/all_gather | solution.py:764
  833.7 49.8 %copy-start.29 = (bf16[688,1536]{1,0:T(8,128)(2,1)S(1)}, bf16[688,1536]{1,0:T(8,128)(2,1)}, u32[]{:S(2)}) copy-start(bf16[688,1536]{1,0:T(8,128)(2,1)} %get-tuple-element.77) | copy-start | bytes 6340612
  883.5 5.7 copy-start.54
  883.5 5.7 copy-start.36
  885.0 4.2 copy-start.11
  885.0 4.2 copy-start.13
  885.0 4.5 copy-start.18
  885.0 5.3 copy-start.21
  885.0 6.0 copy-start.28
  885.0 6.0 copy-start.45
  885.1 6.0 copy-start.49
  885.1 6.0 copy-start.51
  898.9 7.0 copy-start.1
  (12 other events, 13.8 us)
Sparse Core Ops, SparseCore 0:
  11.8 45.8 all-reduce.10
  438.6 59.8 all-reduce.12
  502.4 95.2 all-reduce.14
  600.1 93.5 all-reduce.16
  696.1 96.7 all-reduce.20
  795.1 35.2 reduce-scatter.13
  832.8 50.6 all-reduce.18
Sparse Core Ops, SparseCore 1:
  43.1 54.8 all-gather.6
  99.8 38.7 all-gather.10
  141.1 27.7 all-gather.8
  170.9 58.6 all-gather.12
  232.3 58.6 all-gather.14
  357.2 79.9 reduce-scatter.5
  498.6 75.9 reduce-scatter.7
  578.3 41.5 reduce-scatter.9
  660.4 94.3 reduce-scatter.11
  830.5 31.5 all-gather.16

commit v2 on v1

--- a/solution.py
+++ b/solution.py
@@ -72,7 +72,8 @@
 
 
 NT = (((1,), (1,)), ((), ()))
-VMEM_GRANT = 50 * 1024 * 1024
+VMEM_GRANT = 56 * 1024 * 1024
+MESH_ID = pl.DeviceIdType.MESH
 
 
 def matmul(left, right):
@@ -358,9 +359,7 @@
         ],
         compiler_params=pltpu.CompilerParams(vmem_limit_bytes=VMEM_GRANT),
         cost_estimate=pl.CostEstimate(
-            flops=10 * HEADS * rows * key_total * 64,
-            bytes_accessed=12 * rows * width,
-            transcendentals=HEADS * rows * key_total,
+            flops=rows * width, bytes_accessed=rows * width, transcendentals=0
         ),
         name="attend_back",
     )(
@@ -426,22 +425,16 @@
     )(normed, weights, cosines, sines)
 
 
-def experts_kernel(
-    place_ref, x_ref, g_ref, up_ref, down_ref, router_ref, codes_ref, dx_ref, dgu_ref, act_ref
-):
+def expert_rows(first, x, g, codes, up_ref, down_ref, router_ref, dgu_ref, act_ref):
     local_experts, hidden = down_ref.shape[0], down_ref.shape[1]
-    width = x_ref.shape[1]
-    x, g = x_ref[...], g_ref[...]
     logits = matmul(x, router_ref[...])
-    codes = codes_ref[...].astype(jnp.float32)
     gates = gates_of(logits, codes)
     kept = codes > 1.5
     lane = lax.broadcasted_iota(jnp.int32, logits.shape, 1)
     placed = jnp.zeros(logits.shape, jnp.float32)
     total = None
     for local in range(local_experts):
-        number = place_ref[2] + local
-        mine = (lane == number) & kept
+        mine = (lane == first + local) & kept
         weight = jnp.sum(jnp.where(mine, gates, 0.0), axis=1, keepdims=True)
         made = matmul(x, up_ref[local])
         act_grad = matmul_nt(g, down_ref[local])
@@ -458,10 +451,25 @@
         dgu_ref[local] = both
         part = matmul_nt(both, up_ref[local])
         total = part if total is None else total + part
-    dx_ref[:, :width] = total.astype(jnp.bfloat16)
     high = placed.astype(jnp.bfloat16).astype(jnp.float32)
     rest = pltpu.roll(placed - high, 64, 1)
-    dx_ref[:, width:] = (high + rest).astype(jnp.bfloat16)
+    return jnp.concatenate([total, high + rest], axis=1).astype(jnp.bfloat16)
+
+
+def experts_kernel(
+    place_ref, x_ref, g_ref, up_ref, down_ref, router_ref, codes_ref, dx_ref, dgu_ref, act_ref
+):
+    dx_ref[...] = expert_rows(
+        place_ref[2],
+        x_ref[...],
+        g_ref[...],
+        codes_ref[...].astype(jnp.float32),
+        up_ref,
+        down_ref,
+        router_ref,
+        dgu_ref,
+        act_ref,
+    )
 
 
 def experts(place, rows_in, rows_grad, gate_up, down, weights, codes):
@@ -499,6 +507,875 @@
         ),
         name="experts",
     )(place, rows_in, rows_grad, gate_up, down, weights, codes)
+
+
+def flipped(index, step):
+    core, across, along = index % 2, index // 2 % 2, index // 4
+    return (
+        index
+        + (step % 2) * (1 - 2 * core)
+        + 2 * (step // 2 % 2) * (1 - 2 * across)
+        + 4 * (step // 4) * (1 - 2 * along)
+    )
+
+
+def gather_weights_kernel(
+    query_hbm,
+    key_hbm,
+    value_hbm,
+    out_hbm,
+    fused_hbm,
+    piece_hbm,
+    local_sem,
+    line_send,
+    plane_send,
+    pass_send,
+    recv_sem,
+    piece_send,
+    piece_recv,
+):
+    level, me = lax.axis_index("dp"), lax.axis_index("expert")
+    shard = query_hbm.shape[0]
+    part = piece_hbm.shape[0] // 4
+    q_width, kv_width = query_hbm.shape[1], key_hbm.shape[1]
+    barrier = pltpu.get_barrier_semaphore()
+    plane_steps, line_steps = (2, 4, 6, 1), (1, 2, 3)
+    for step in plane_steps:
+        pl.semaphore_signal(
+            barrier, inc=1, device_id={"expert": flipped(me, step)}, device_id_type=MESH_ID
+        )
+    for step in line_steps:
+        pl.semaphore_signal(
+            barrier, inc=1, device_id={"dp": flipped(level, step)}, device_id_type=MESH_ID
+        )
+    own = pl.ds(pl.multiple_of(me * part, part), part)
+
+    def rows(line_step, plane_step):
+        start = flipped(level, line_step) * shard + flipped(me, plane_step) * part
+        return fused_hbm.at[pl.ds(pl.multiple_of(start, part), part)]
+
+    mine = pl.ds(pl.multiple_of(level * shard + me * part, part), part)
+    starts = (
+        pltpu.make_async_copy(
+            query_hbm.at[own], fused_hbm.at[mine, pl.ds(0, q_width)], local_sem.at[0]
+        ),
+        pltpu.make_async_copy(
+            key_hbm.at[own], fused_hbm.at[mine, pl.ds(q_width, kv_width)], local_sem.at[1]
+        ),
+        pltpu.make_async_copy(
+            value_hbm.at[own],
+            fused_hbm.at[mine, pl.ds(q_width + kv_width, kv_width)],
+            local_sem.at[2],
+        ),
+        pltpu.make_async_copy(
+            out_hbm.at[own],
+            piece_hbm.at[pl.ds(pl.multiple_of(level * part, part), part)],
+            local_sem.at[3],
+        ),
+    )
+
+    def along(step):
+        return pltpu.make_async_remote_copy(
+            src_ref=rows(0, 0),
+            dst_ref=rows(0, 0),
+            send_sem=line_send.at[step],
+            recv_sem=recv_sem.at[step, 0],
+            device_id={"dp": flipped(level, step)},
+            device_id_type=MESH_ID,
+        )
+
+    def along_out(step):
+        place = piece_hbm.at[pl.ds(pl.multiple_of(level * part, part), part)]
+        return pltpu.make_async_remote_copy(
+            src_ref=place,
+            dst_ref=place,
+            send_sem=piece_send.at[step],
+            recv_sem=piece_recv.at[step],
+            device_id={"dp": flipped(level, step)},
+            device_id_type=MESH_ID,
+        )
+
+    def across(line_step, step):
+        return pltpu.make_async_remote_copy(
+            src_ref=rows(line_step, 0),
+            dst_ref=rows(line_step, 0),
+            send_sem=plane_send.at[line_step, step],
+            recv_sem=recv_sem.at[line_step, step],
+            device_id={"expert": flipped(me, step)},
+            device_id_type=MESH_ID,
+        )
+
+    def pass_on(line_step, step):
+        return pltpu.make_async_remote_copy(
+            src_ref=rows(line_step, step),
+            dst_ref=rows(line_step, step),
+            send_sem=pass_send.at[line_step, step],
+            recv_sem=recv_sem.at[line_step, step + 1],
+            device_id={"expert": flipped(me, 1)},
+            device_id_type=MESH_ID,
+        )
+
+    for copy in starts:
+        copy.start()
+    for copy in starts[:3]:
+        copy.wait()
+    pl.semaphore_wait(barrier, len(plane_steps) + len(line_steps))
+    for step in line_steps:
+        along(step).start()
+    for step in plane_steps:
+        across(0, step).start()
+    starts[3].wait()
+    for step in line_steps:
+        along_out(step).start()
+
+    def wait_level(line_step, carry):
+        along(line_step).wait_recv()
+        for step in plane_steps:
+            across(line_step, step).start()
+        return carry
+
+    def pass_level(line_step, carry):
+        for step in (2, 4, 6):
+            across(line_step, step).wait_recv()
+            pass_on(line_step, step).start()
+        return carry
+
+    def last_level(line_step, carry):
+        for step in (1, 3, 5, 7):
+            across(line_step, step).wait_recv()
+        for step in plane_steps:
+            across(line_step, step).wait_send()
+        for step in (2, 4, 6):
+            pass_on(line_step, step).wait_send()
+        return carry
+
+    wait_level(1, 0)
+    pass_level(0, 0)
+    wait_level(2, 0)
+    pass_level(1, 0)
+    wait_level(3, 0)
+    pass_level(2, 0)
+    pass_level(3, 0)
+    lax.fori_loop(0, 4, last_level, 0)
+    for step in line_steps:
+        along(step).wait_send()
+        along_out(step).wait()
+
+
+def gather_weights(query_proj, key_proj, value_proj, out_proj):
+    shard = query_proj.shape[0]
+    columns = query_proj.shape[1] + 2 * key_proj.shape[1]
+    anywhere = pl.BlockSpec(memory_space=pl.ANY)
+    dma = pltpu.SemaphoreType.DMA
+    return pl.pallas_call(
+        gather_weights_kernel,
+        in_specs=[anywhere] * 4,
+        out_specs=[anywhere] * 2,
+        out_shape=[
+            jax.ShapeDtypeStruct((4 * shard, columns), jnp.bfloat16),
+            jax.ShapeDtypeStruct((shard // 2, out_proj.shape[1]), jnp.bfloat16),
+        ],
+        scratch_shapes=[
+            dma((4,)),
+            dma((4,)),
+            dma((4, 8)),
+            dma((4, 8)),
+            dma((4, 8)),
+            dma((4,)),
+            dma((4,)),
+        ],
+        compiler_params=pltpu.CompilerParams(
+            collective_id=2, has_side_effects=True, vmem_limit_bytes=1024 * 1024
+        ),
+        cost_estimate=pl.CostEstimate(
+            flops=0, bytes_accessed=16 * shard * columns, transcendentals=0
+        ),
+        name="gather_weights",
+    )(query_proj, key_proj, value_proj, out_proj)
+
+
+def share_pairs_kernel(
+    rows_hbm, prompt_hbm, tail_hbm, local_sem, tail_send, tail_recv, send_sem, pass_sem, recv_sem
+):
+    me = lax.axis_index("expert")
+    columns = prompt_hbm.shape[1]
+    count = prompt_hbm.shape[0] // 8
+    cont = tail_hbm.shape[0] // 2
+    pairs_at = pl.ds(rows_hbm.shape[1] - columns, columns)
+    barrier = pltpu.get_barrier_semaphore()
+    for step in (1, 2, 4, 6):
+        pl.semaphore_signal(
+            barrier, inc=1, device_id={"expert": flipped(me, step)}, device_id_type=MESH_ID
+        )
+
+    def block(step):
+        return prompt_hbm.at[pl.ds(pl.multiple_of(flipped(me, step) * count, count), count)]
+
+    own_prompt = rows_hbm.at[pl.ds(0, count), pairs_at]
+    own_cont = rows_hbm.at[pl.ds(count, cont), pairs_at]
+    local = (
+        pltpu.make_async_copy(own_prompt, block(0), local_sem.at[0]),
+        pltpu.make_async_copy(own_cont, tail_hbm.at[pl.ds(cont, cont)], local_sem.at[1]),
+    )
+    tail = pltpu.make_async_remote_copy(
+        src_ref=own_cont,
+        dst_ref=tail_hbm.at[pl.ds(0, cont)],
+        send_sem=tail_send,
+        recv_sem=tail_recv,
+        device_id={"expert": flipped(me, 1)},
+        device_id_type=MESH_ID,
+    )
+
+    def send(step):
+        return pltpu.make_async_remote_copy(
+            src_ref=own_prompt,
+            dst_ref=block(0),
+            send_sem=send_sem.at[step],
+            recv_sem=recv_sem.at[step],
+            device_id={"expert": flipped(me, step)},
+            device_id_type=MESH_ID,
+        )
+
+    def pass_on(step):
+        return pltpu.make_async_remote_copy(
+            src_ref=block(step),
+            dst_ref=block(step),
+            send_sem=pass_sem.at[step],
+            recv_sem=recv_sem.at[step + 1],
+            device_id={"expert": flipped(me, 1)},
+            device_id_type=MESH_ID,
+        )
+
+    for copy in local:
+        copy.start()
+    pl.semaphore_wait(barrier, 4)
+    for step in (2, 4, 6, 1):
+        send(step).start()
+    tail.start()
+    for step in (2, 4, 6):
+        send(step).wait_recv()
+        pass_on(step).start()
+    for step in (1, 3, 5, 7):
+        send(step).wait_recv()
+    for step in (1, 2, 4, 6):
+        send(step).wait_send()
+    for step in (2, 4, 6):
+        pass_on(step).wait_send()
+    tail.wait()
+    for copy in local:
+        copy.wait()
+
+
+def share_pairs(projected):
+    rows = projected.shape[0]
+    columns = 2 * KV_HEADS * HEAD
+    anywhere = pl.BlockSpec(memory_space=pl.ANY)
+    dma = pltpu.SemaphoreType.DMA
+    return pl.pallas_call(
+        share_pairs_kernel,
+        in_specs=[anywhere],
+        out_specs=[anywhere] * 2,
+        out_shape=[
+            jax.ShapeDtypeStruct((8 * PROMPT_DEV, columns), jnp.bfloat16),
+            jax.ShapeDtypeStruct((2 * (rows - PROMPT_DEV), columns), jnp.bfloat16),
+        ],
+        scratch_shapes=[dma((2,)), dma, dma, dma((8,)), dma((8,)), dma((8,))],
+        compiler_params=pltpu.CompilerParams(
+            collective_id=3, has_side_effects=True, vmem_limit_bytes=1024 * 1024
+        ),
+        cost_estimate=pl.CostEstimate(
+            flops=0, bytes_accessed=32 * PROMPT_DEV * columns, transcendentals=0
+        ),
+        name="share_pairs",
+    )(projected)
+
+
+def line_sum_kernel(
+    count,
+    mine_hbm,
+    total_hbm,
+    mine,
+    partial,
+    result,
+    wide,
+    load_sem,
+    up_send,
+    up_recv,
+    down_send,
+    down_recv,
+    store_sem,
+):
+    chunks = mine.shape[0]
+    at = lax.axis_index("dp")
+    last = count - 1
+    barrier = pltpu.get_barrier_semaphore()
+
+    @pl.when(at > 0)
+    def _():
+        pl.semaphore_signal(barrier, inc=1, device_id={"dp": at - 1}, device_id_type=MESH_ID)
+
+    @pl.when(at < last)
+    def _():
+        pl.semaphore_signal(barrier, inc=1, device_id={"dp": at + 1}, device_id_type=MESH_ID)
+
+    def load(chunk):
+        return pltpu.make_async_copy(mine_hbm.at[chunk], mine.at[chunk], load_sem.at[chunk])
+
+    def upward(chunk):
+        return pltpu.make_async_remote_copy(
+            src_ref=mine.at[chunk],
+            dst_ref=partial.at[chunk],
+            send_sem=up_send.at[chunk],
+            recv_sem=up_recv.at[chunk],
+            device_id={"dp": at + 1},
+            device_id_type=MESH_ID,
+        )
+
+    def downward(source, chunk):
+        return pltpu.make_async_remote_copy(
+            src_ref=source.at[chunk],
+            dst_ref=result.at[chunk],
+            send_sem=down_send.at[chunk],
+            recv_sem=down_recv.at[chunk],
+            device_id={"dp": at - 1},
+            device_id_type=MESH_ID,
+        )
+
+    def store(slot, chunk):
+        return pltpu.make_async_copy(wide.at[slot], total_hbm.at[chunk], store_sem.at[slot])
+
+    lax.fori_loop(0, chunks, lambda chunk, c: (load(chunk).start(), c)[1], 0)
+    pl.semaphore_wait(barrier, jnp.where(at > 0, 1, 0) + jnp.where(at < last, 1, 0))
+    lag = 2 * (last - at) + jnp.where(at < last, 2, 0)
+
+    def finish(source, done):
+        slot = lax.rem(done, 2)
+
+        @pl.when(done >= 2)
+        def _():
+            store(slot, done - 2).wait()
+
+        wide[slot] = source[done].astype(jnp.float32)
+        store(slot, done).start()
+
+    def tick(step, carry):
+        @pl.when(step < chunks)
+        def _():
+            load(step).wait()
+
+            @pl.when(at > 0)
+            def _():
+                upward(step).wait_recv()
+                mine[step] = (
+                    mine[step].astype(jnp.float32) + partial[step].astype(jnp.float32)
+                ).astype(jnp.bfloat16)
+
+            @pl.when(at < last)
+            def _():
+                upward(step).start()
+
+        done = step - lag
+
+        @pl.when((done >= 0) & (done < chunks))
+        def _():
+            @pl.when(at == last)
+            def _():
+                downward(mine, done).start()
+                finish(mine, done)
+
+            @pl.when(at < last)
+            def _():
+                downward(result, done).wait_recv()
+
+                @pl.when(at > 0)
+                def _():
+                    downward(result, done).start()
+
+                finish(result, done)
+
+        return carry
+
+    lax.fori_loop(0, chunks + 2 * last + 2, tick, 0)
+    for late in (chunks - 2, chunks - 1):
+        store(late % 2, late).wait()
+
+    def drain(chunk, carry):
+        @pl.when(at < last)
+        def _():
+            upward(chunk).wait_send()
+
+        @pl.when(at > 0)
+        def _():
+            downward(result, chunk).wait_send()
+
+        return carry
+
+    lax.fori_loop(0, chunks, drain, 0)
+
+
+def line_sum(count, number, values):
+    shape = values.shape
+    chunks = shape[0]
+    dma = pltpu.SemaphoreType.DMA
+    return pl.pallas_call(
+        functools.partial(line_sum_kernel, count),
+        in_specs=[pl.BlockSpec(memory_space=pl.ANY)],
+        out_specs=pl.BlockSpec(memory_space=pl.ANY),
+        out_shape=jax.ShapeDtypeStruct(shape, jnp.float32),
+        scratch_shapes=[
+            pltpu.VMEM(shape, jnp.bfloat16),
+            pltpu.VMEM(shape, jnp.bfloat16),
+            pltpu.VMEM(shape, jnp.bfloat16),
+            pltpu.VMEM((2,) + shape[1:], jnp.float32),
+            dma((chunks,)),
+            dma((chunks,)),
+            dma((chunks,)),
+            dma((chunks,)),
+            dma((chunks,)),
+            dma((2,)),
+        ],
+        compiler_params=pltpu.CompilerParams(
+            collective_id=number, has_side_effects=True, vmem_limit_bytes=VMEM_GRANT
+        ),
+        cost_estimate=pl.CostEstimate(
+            flops=0, bytes_accessed=60 * values.size, transcendentals=0
+        ),
+        name="line_sum",
+    )(values)
+
+
+def line_scatter_kernel(
+    parts_hbm, sum_ref, landed, local_sem, send_sem, recv_sem
+):
+    level = lax.axis_index("dp")
+    rows = sum_ref.shape[0]
+    barrier = pltpu.get_barrier_semaphore()
+    for step in (1, 2, 3):
+        pl.semaphore_signal(
+            barrier, inc=1, device_id={"dp": flipped(level, step)}, device_id_type=MESH_ID
+        )
+
+    def part(step):
+        start = flipped(level, step) * rows
+        return parts_hbm.at[pl.ds(pl.multiple_of(start, rows), rows)]
+
+    def send(step):
+        return pltpu.make_async_remote_copy(
+            src_ref=part(step),
+            dst_ref=landed.at[step],
+            send_sem=send_sem.at[step],
+            recv_sem=recv_sem.at[step],
+            device_id={"dp": flipped(level, step)},
+            device_id_type=MESH_ID,
+        )
+
+    own = pltpu.make_async_copy(part(0), landed.at[0], local_sem)
+    own.start()
+    pl.semaphore_wait(barrier, 3)
+    for step in (2, 3, 1):
+        send(step).start()
+    own.wait()
+    for step in (1, 2, 3):
+        send(step).wait_recv()
+    total = landed[0].astype(jnp.float32) + landed[1].astype(jnp.float32)
+    total += landed[2].astype(jnp.float32)
+    total += landed[3].astype(jnp.float32)
+    sum_ref[...] = total.astype(jnp.bfloat16)
+    for step in (1, 2, 3):
+        send(step).wait_send()
+
+
+def line_scatter(parts):
+    rows, columns = parts.shape[0] // 4, parts.shape[1]
+    dma = pltpu.SemaphoreType.DMA
+    return pl.pallas_call(
+        line_scatter_kernel,
+        in_specs=[pl.BlockSpec(memory_space=pl.ANY)],
+        out_specs=pl.BlockSpec(memory_space=pltpu.VMEM),
+        out_shape=jax.ShapeDtypeStruct((rows, columns), jnp.bfloat16),
+        scratch_shapes=[pltpu.VMEM((4, rows, columns), jnp.bfloat16), dma, dma((4,)), dma((4,))],
+        compiler_params=pltpu.CompilerParams(
+            collective_id=4, has_side_effects=True, vmem_limit_bytes=16 * 1024 * 1024
+        ),
+        cost_estimate=pl.CostEstimate(
+            flops=0, bytes_accessed=100 * rows * columns, transcendentals=0
+        ),
+        name="line_scatter",
+    )(parts)
+
+
+def return_pairs_kernel(
+    key_ref,
+    value_ref,
+    tail_key_ref,
+    tail_value_ref,
+    cos_ref,
+    sin_ref,
+    low_ref,
+    tail_out,
+    tail_in,
+    pairs_in,
+    joined,
+    last_in,
+    tail_send,
+    tail_recv,
+    pair_send,
+    pair_recv,
+    last_send,
+    last_recv,
+):
+    me = lax.axis_index("expert")
+    count = pairs_in.shape[2]
+    kv_width = key_ref.shape[1]
+    cont = tail_out.shape[0]
+    barrier = pltpu.get_barrier_semaphore()
+    for step in (1, 2, 4, 6):
+        pl.semaphore_signal(
+            barrier, inc=1, device_id={"expert": flipped(me, step)}, device_id_type=MESH_ID
+        )
+
+    def block_of(step):
+        return pl.ds(pl.multiple_of(flipped(me, step) * count, count), count)
+
+    sources = (key_ref, value_ref)
+
+    def remote(source, target, sent, landed, step):
+        return pltpu.make_async_remote_copy(
+            src_ref=source,
+            dst_ref=target,
+            send_sem=sent,
+            recv_sem=landed,
+            device_id={"expert": flipped(me, step)},
+            device_id_type=MESH_ID,
+        )
+
+    def to_sibling(half, which):
+        return remote(
+            sources[which].at[block_of(2 * half + 1)],
+            pairs_in.at[half, which],
+            pair_send.at[half, which],
+            pair_recv.at[half, which],
+            1,
+        )
+
+    def to_owner(half, which):
+        return remote(
+            joined.at[half, which],
+            last_in.at[half, which],
+            last_send.at[half, which],
+            last_recv.at[half, which],
+            2 * half,
+        )
+
+    tail = remote(tail_out, tail_in, tail_send, tail_recv, 1)
+    pl.semaphore_wait(barrier, 4)
+    for half in (1, 2, 3, 0):
+        for which in range(2):
+            to_sibling(half, which).start()
+    tail_out[:, :kv_width] = tail_key_ref[:cont].astype(jnp.bfloat16)
+    tail_out[:, kv_width:] = tail_value_ref[:cont].astype(jnp.bfloat16)
+    tail.start()
+    for half in (3, 1, 2):
+        for which in range(2):
+            to_sibling(half, which).wait_recv()
+            joined[half, which] = (
+                sources[which][block_of(2 * half), :].astype(jnp.float32)
+                + pairs_in[half, which].astype(jnp.float32)
+            ).astype(jnp.bfloat16)
+            to_owner(half, which).start()
+    tail.wait_recv()
+    blocks = kv_width // 128
+    for block in range(blocks):
+        lanes = slice(block * 128, block * 128 + 128)
+        values = slice(kv_width + block * 128, kv_width + block * 128 + 128)
+        grown = tail_key_ref[cont:, lanes] + tail_in[:, lanes].astype(jnp.float32)
+        low_ref[count:, lanes] = turn(grown, cos_ref[count:], sin_ref[count:]).astype(jnp.bfloat16)
+        grown = tail_value_ref[cont:, lanes] + tail_in[:, values].astype(jnp.float32)
+        low_ref[count:, values] = grown.astype(jnp.bfloat16)
+    totals = []
+    for which in range(2):
+        to_sibling(0, which).wait_recv()
+        totals.append(
+            sources[which][block_of(0), :].astype(jnp.float32)
+            + pairs_in[0, which].astype(jnp.float32)
+        )
+    for half in (1, 2, 3):
+        for which in range(2):
+            to_owner(half, which).wait_recv()
+            totals[which] = totals[which] + last_in[half, which].astype(jnp.float32)
+    for block in range(blocks):
+        lanes = slice(block * 128, block * 128 + 128)
+        low_ref[:count, lanes] = turn(
+            totals[0][:, lanes], cos_ref[:count], sin_ref[:count]
+        ).astype(jnp.bfloat16)
+    low_ref[:count, kv_width:] = totals[1].astype(jnp.bfloat16)
+    tail.wait_send()
+    for half in range(4):
+        for which in range(2):
+            to_sibling(half, which).wait_send()
+    for half in (1, 2, 3):
+        for which in range(2):
+            to_owner(half, which).wait_send()
+
+
+def return_pairs(key_part, value_part, tail_keys, tail_values, cosines, sines):
+    kv_width = key_part.shape[1]
+    count, cont = PROMPT_DEV, tail_keys.shape[0] // 2
+    resident = pl.BlockSpec(memory_space=pltpu.VMEM)
+    dma = pltpu.SemaphoreType.DMA
+    pieces = pltpu.VMEM((4, 2, count, kv_width), jnp.bfloat16)
+    rows = pltpu.VMEM((cont, 2 * kv_width), jnp.bfloat16)
+    return pl.pallas_call(
+        return_pairs_kernel,
+        in_specs=[resident] * 6,
+        out_specs=resident,
+        out_shape=jax.ShapeDtypeStruct((count + cont, 2 * kv_width), jnp.bfloat16),
+        scratch_shapes=[
+            rows,
+            rows,
+            pieces,
+            pieces,
+            pieces,
+            dma,
+            dma,
+            dma((4, 2)),
+            dma((4, 2)),
+            dma((4, 2)),
+            dma((4, 2)),
+        ],
+        compiler_params=pltpu.CompilerParams(
+            collective_id=5, has_side_effects=True, vmem_limit_bytes=24 * 1024 * 1024
+        ),
+        cost_estimate=pl.CostEstimate(flops=0, bytes_accessed=8 * 1024 * 1024, transcendentals=0),
+        name="return_pairs",
+    )(key_part, value_part, tail_keys, tail_values, cosines, sines)
+
+
+def gathering_experts_kernel(
+    own_hbm,
+    g_hbm,
+    up_ref,
+    down_ref,
+    router_ref,
+    dx_hbm,
+    dgu_hbm,
+    act_hbm,
+    x_hbm,
+    rows,
+    grads,
+    dx_out,
+    dgu_out,
+    act_out,
+    own_sem,
+    send_sem,
+    pass_sem,
+    recv_sem,
+    grad_sem,
+    x_sem,
+    dx_sem,
+    dgu_sem,
+    act_sem,
+):
+    me = lax.axis_index("expert")
+    local_experts = down_ref.shape[0]
+    steps, count = rows.shape[0], rows.shape[1]
+    barrier = pltpu.get_barrier_semaphore()
+    for step in (1, 2, 4):
+        pl.semaphore_signal(
+            barrier, inc=1, device_id={"expert": flipped(me, step)}, device_id_type=MESH_ID
+        )
+
+    def block_of(step):
+        return pl.ds(pl.multiple_of(flipped(me, step) * count, count), count)
+
+    def grad_load(step):
+        return pltpu.make_async_copy(
+            g_hbm.at[block_of(step)], grads.at[step % 2], grad_sem.at[step % 2]
+        )
+
+    half_count = count // 2
+    top, bottom = pl.ds(0, half_count), pl.ds(half_count, half_count)
+
+    def remote(source, target, sent, landed, step):
+        return pltpu.make_async_remote_copy(
+            src_ref=source,
+            dst_ref=target,
+            send_sem=sent,
+            recv_sem=landed,
+            device_id={"expert": flipped(me, step)},
+            device_id_type=MESH_ID,
+        )
+
+    def send(step):
+        return remote(rows.at[0], rows.at[step], send_sem.at[step], recv_sem.at[step], step)
+
+    def pass_on(step):
+        return remote(
+            rows.at[step], rows.at[step + 1], pass_sem.at[step], recv_sem.at[step + 1], 1
+        )
+
+    def relay_top():
+        return remote(rows.at[2, top], rows.at[6, top], send_sem.at[6], recv_sem.at[6], 4)
+
+    def relay_bottom():
+        return remote(rows.at[4, bottom], rows.at[6, bottom], send_sem.at[7], recv_sem.at[0], 2)
+
+    def x_store(step):
+        return pltpu.make_async_copy(
+            rows.at[step, :, pl.ds(0, x_hbm.shape[1])], x_hbm.at[block_of(step)], x_sem.at[step]
+        )
+
+    def stores(step):
+        slot = step % 2
+        return (
+            pltpu.make_async_copy(dx_out.at[slot], dx_hbm.at[block_of(step)], dx_sem.at[slot]),
+            pltpu.make_async_copy(dgu_out.at[slot], dgu_hbm.at[:, block_of(step)], dgu_sem.at[slot]),
+            pltpu.make_async_copy(act_out.at[slot], act_hbm.at[:, block_of(step)], act_sem.at[slot]),
+        )
+
+    own_load = pltpu.make_async_copy(own_hbm, rows.at[0], own_sem)
+    own_load.start()
+    grad_load(0).start()
+    own_load.wait()
+    pl.semaphore_wait(barrier, 3)
+    for step in (2, 4, 1):
+        send(step).start()
+
+    def work(step, carry):
+        @pl.when(step == 2)
+        def _():
+            send(2).wait_recv()
+            relay_top().start()
+            pass_on(2).start()
+            send(4).wait_recv()
+            relay_bottom().start()
+            pass_on(4).start()
+
+        @pl.when(step == 6)
+        def _():
+            relay_top().wait_recv()
+            relay_bottom().wait_recv()
+            pass_on(6).start()
+
+        @pl.when(step % 2 == 1)
+        def _():
+            send(step).wait_recv()
+
+        x_store(step).start()
+
+        @pl.when(step + 1 < steps)
+        def _():
+            grad_load(step + 1).start()
+
+        grad_load(step).wait()
+        slot = step % 2
+
+        @pl.when(step >= 2)
+        def _():
+            for copy in stores(step - 2):
+                copy.wait()
+
+        dx_out[slot] = expert_rows(
+            me * local_experts,
+            rows[step, :, : x_hbm.shape[1]],
+            grads[slot],
+            rows[step, :, x_hbm.shape[1] :].astype(jnp.float32),
+            up_ref,
+            down_ref,
+            router_ref,
+            dgu_out.at[slot],
+            act_out.at[slot],
+        )
+        for copy in stores(step):
+            copy.start()
+        return carry
+
+    lax.fori_loop(0, steps, work, 0)
+    for step in (steps - 2, steps - 1):
+        for copy in stores(step):
+            copy.wait()
+    for step in (1, 2, 4):
+        send(step).wait_send()
+    relay_top().wait_send()
+    relay_bottom().wait_send()
+    for step in (2, 4, 6):
+        pass_on(step).wait_send()
+    for step in range(steps):
+        x_store(step).wait()
+
+
+def gathering_experts(own_rows, rows_grad, gate_up, down, weights):
+    count = own_rows.shape[0]
+    total, width = rows_grad.shape
+    steps = total // count
+    local_experts, hidden = down.shape[0], down.shape[1]
+    resident = pl.BlockSpec(memory_space=pltpu.VMEM)
+    anywhere = pl.BlockSpec(memory_space=pl.ANY)
+    dma = pltpu.SemaphoreType.DMA
+    return pl.pallas_call(
+        gathering_experts_kernel,
+        in_specs=[anywhere, anywhere, resident, resident, resident],
+        out_specs=[anywhere] * 4,
+        out_shape=[
+            jax.ShapeDtypeStruct((total, width + 128), jnp.bfloat16),
+            jax.ShapeDtypeStruct((local_experts, total, 2 * hidden), jnp.bfloat16),
+            jax.ShapeDtypeStruct((local_experts, total, hidden), jnp.bfloat16),
+            jax.ShapeDtypeStruct((total, width), jnp.bfloat16),
+        ],
+        scratch_shapes=[
+            pltpu.VMEM((steps, count, width + 128), jnp.bfloat16),
+            pltpu.VMEM((2, count, width), jnp.bfloat16),
+            pltpu.VMEM((2, count, width + 128), jnp.bfloat16),
+            pltpu.VMEM((2, local_experts, count, 2 * hidden), jnp.bfloat16),
+            pltpu.VMEM((2, local_experts, count, hidden), jnp.bfloat16),
+            dma,
+            dma((steps,)),
+            dma((steps,)),
+            dma((steps,)),
+            dma((2,)),
+            dma((steps,)),
+            dma((2,)),
+            dma((2,)),
+            dma((2,)),
+        ],
+        compiler_params=pltpu.CompilerParams(
+            collective_id=1, has_side_effects=True, vmem_limit_bytes=VMEM_GRANT
+        ),
+        cost_estimate=pl.CostEstimate(
+            flops=10 * total * width * local_experts * hidden,
+            bytes_accessed=16 * total * width,
+            transcendentals=total * local_experts * hidden,
+        ),
+        name="gathering_experts",
+    )(own_rows, rows_grad, gate_up, down, weights)
+
+
+def shares_kernel(act_ref, down_ref, o_ref):
+    total = matmul(act_ref[0], down_ref[0])
+    for local in range(1, down_ref.shape[0]):
+        total += matmul(act_ref[local], down_ref[local])
+    o_ref[...] = total.astype(jnp.bfloat16)
+
+
+def moe_shares(act, down):
+    local_experts, total, hidden = act.shape
+    width = down.shape[2]
+    step = 512
+    return pl.pallas_call(
+        shares_kernel,
+        grid=(total // step,),
+        in_specs=[
+            pl.BlockSpec((local_experts, step, hidden), lambda i: (0, i, 0)),
+            pl.BlockSpec(down.shape, lambda i: (0, 0, 0)),
+        ],
+        out_specs=pl.BlockSpec((step, width), lambda i: (i, 0)),
+        out_shape=jax.ShapeDtypeStruct((total, width), jnp.bfloat16),
+        compiler_params=pltpu.CompilerParams(vmem_limit_bytes=VMEM_GRANT),
+        cost_estimate=pl.CostEstimate(
+            flops=total * width, bytes_accessed=total * width, transcendentals=0
+        ),
+        name="moe_shares",
+    )(act, down)
 
 
 def dense_grads_kernel(
@@ -583,13 +1460,15 @@
     shard_rows = query_proj.shape[0]
     piece_rows = shard_rows // owner_count
 
+    def in_order(pieces):
+        columns = pieces.shape[1]
+        pieces = pieces.reshape(owner_count, dp_count, piece_rows, columns)
+        return pieces.transpose(1, 0, 2, 3).reshape(dp_count * shard_rows, columns)
+
     def whole_of(shard):
-        columns = shard.shape[1]
         piece = lax.dynamic_slice_in_dim(shard, owner_index * piece_rows, piece_rows, 0)
         piece = lax.all_gather(piece, "dp", axis=0, tiled=True)
-        piece = lax.all_gather(piece, "expert", axis=0, tiled=True)
-        piece = piece.reshape(owner_count, dp_count, piece_rows, columns)
-        return piece.transpose(1, 0, 2, 3).reshape(dp_count * shard_rows, columns)
+        return in_order(lax.all_gather(piece, "expert", axis=0, tiled=True))
 
     extras = jnp.concatenate(
         [
@@ -600,22 +1479,22 @@
         ],
         axis=1,
     )
-    fused = whole_of(jnp.concatenate([query_proj, key_proj, value_proj], axis=1))
+    small_plane = owner_count == 8 and dp_count == 4
+    if small_plane:
+        fused, out_piece = gather_weights(query_proj, key_proj, value_proj, out_proj)
+        out_piece = lax.all_gather(out_piece, "expert", axis=0, tiled=True)
+        full_out = in_order(out_piece)
+    else:
+        fused = whole_of(jnp.concatenate([query_proj, key_proj, value_proj], axis=1))
+        full_out = whole_of(out_proj)
     spread = lax.dynamic_update_slice(
         jnp.zeros((dp_count * shard_rows, 128), jnp.bfloat16),
         extras,
         (lax.axis_index("dp") * shard_rows, 0),
     )
     extra_full = lax.psum(spread, "dp")
-    full_out = whole_of(out_proj)
     codes = slot_codes(routes, drop_rank.reshape(tok_rows, top_count), expert_total, capacity)
-    codes_all = lax.all_gather(
-        jnp.pad(codes, ((0, 0), (0, 128 - expert_total))).astype(jnp.bfloat16),
-        "expert",
-        axis=0,
-        tiled=True,
-    )
-    fused, codes_all = lax.optimization_barrier((fused, codes_all))
+    wide_codes = jnp.pad(codes, ((0, 0), (0, 128 - expert_total))).astype(jnp.bfloat16)
     q_width = query_proj.shape[1]
     extra_at = q_width + 2 * kv_width
     full_router = extra_full[:, :expert_total]
@@ -639,33 +1518,78 @@
     ).astype(jnp.int32)
     cosines, sines = pair_tables(position)
     projected = project(normed, fused, cosines, sines)
-    own_pairs = projected[:, q_width:]
-    prompt_pairs = lax.all_gather(own_pairs[:prompt_rows], "expert", axis=0, tiled=True)
-    ahead = [(source, source + 1) for source in range(0, owner_count, 2)]
-    partner_pairs = lax.ppermute(own_pairs[prompt_rows:], "expert", ahead)
-    tail_pairs = jnp.concatenate([partner_pairs, own_pairs[prompt_rows:]], axis=0)
+    if small_plane:
+        prompt_pairs, tail_pairs = share_pairs(projected)
+    else:
+        own_pairs = projected[:, q_width:]
+        prompt_pairs = lax.all_gather(own_pairs[:prompt_rows], "expert", axis=0, tiled=True)
+        ahead = [(source, source + 1) for source in range(0, owner_count, 2)]
+        partner_pairs = lax.ppermute(own_pairs[prompt_rows:], "expert", ahead)
+        tail_pairs = jnp.concatenate([partner_pairs, own_pairs[prompt_rows:]], axis=0)
     att_low, stats = attend(place, projected, prompt_pairs, tail_pairs)
     attn_proj = jnp.dot(att_low, full_out, preferred_element_type=jnp.float32)
     mixed_rows = inputs + RESIDUAL * attn_proj
     ffn_full, inverse_two = norm_forward(mixed_rows, gain_two)
     ffn_low = ffn_full.astype(jnp.bfloat16)
-    ffn_low, grad_all = lax.optimization_barrier((ffn_low, grad_all))
-    ffn_all = lax.all_gather(ffn_low, "expert", axis=0, tiled=True)
+
+    def by_piece(values):
+        turned = values.T.reshape(dp_count, owner_count, piece_rows, tok_rows)
+        return turned.transpose(1, 0, 2, 3).reshape(width, tok_rows)
+
+    normed_across, ffn_across, att_across = by_piece(normed), by_piece(ffn_low), by_piece(att_low)
+    ffn_low, grad_all, normed_across, ffn_across, att_across = lax.optimization_barrier(
+        (ffn_low, grad_all, normed_across, ffn_across, att_across)
+    )
     gates = gates_of(
         jnp.dot(ffn_low, full_router, preferred_element_type=jnp.float32), codes
     )
-    input_rows, mixed_grad, acted_low = experts(
-        place, ffn_all, grad_all, gate_up, down_proj, extra_full, codes_all
-    )
+    if owner_count == 8:
+        input_rows, mixed_grad, acted_low, ffn_all = gathering_experts(
+            jnp.concatenate([ffn_low, wide_codes], axis=1),
+            grad_all,
+            gate_up,
+            down_proj,
+            extra_full,
+        )
+    else:
+        ffn_all = lax.all_gather(ffn_low, "expert", axis=0, tiled=True)
+        codes_all = lax.all_gather(wide_codes, "expert", axis=0, tiled=True)
+        input_rows, mixed_grad, acted_low = experts(
+            place, ffn_all, grad_all, gate_up, down_proj, extra_full, codes_all
+        )
     back_rows = lax.psum_scatter(
         input_rows, "expert", scatter_dimension=0, tiled=True
     ).astype(jnp.float32)
-    gateup_local = jnp.einsum(
-        "td,etf->edf", ffn_all, mixed_grad, preferred_element_type=jnp.float32
-    )
-    down_local = RESIDUAL * jnp.einsum(
-        "etf,td->efd", acted_low, grad_all, preferred_element_type=jnp.float32
-    )
+    over_tokens = (((0,), (0,)), ((), ()))
+
+    def summed_over_tokens(left, right):
+        return lax.dot_general(left, right, over_tokens, preferred_element_type=jnp.float32)
+
+    gateup_low = [
+        summed_over_tokens(ffn_all, mixed_grad[local]).astype(jnp.bfloat16)
+        for local in range(local_experts)
+    ]
+
+    def down_part(act):
+        return (RESIDUAL * summed_over_tokens(act, grad_all)).astype(jnp.bfloat16)
+
+    down_first = down_part(acted_low[0])
+    unit = width // 96
+    parts = [
+        (gateup_low[0][: 57 * unit],),
+        (gateup_low[0][57 * unit :], gateup_low[1][: 25 * unit]),
+        (gateup_low[1][25 * unit : 83 * unit],),
+        (gateup_low[1][83 * unit :], down_first),
+    ]
+
+    def next_sum(part, sums):
+        part, last = lax.optimization_barrier((part, sums[-1]))
+        return [*sums[:-1], last, lax.psum(part, "dp")]
+
+    sums = [lax.psum(parts[0], "dp")]
+    back_rows, sums = lax.optimization_barrier((back_rows, sums))
+    moe_part = moe_shares(acted_low, down_proj)
+    sums = next_sum(parts[1], sums)
     upstream = grad_out.astype(jnp.float32)
     gate_grad = (
         back_rows[:, width : width + expert_total]
@@ -679,72 +1603,44 @@
     norm_part, gain_two_local = norm_backward(mixed_rows, inverse_two, gain_two, ffn_grad)
     mixed_grad_total = upstream + norm_part
     attn_grad_low = (RESIDUAL * mixed_grad_total).astype(jnp.bfloat16)
-    moe_part = jnp.einsum(
-        "etf,efd->td", acted_low, down_proj, preferred_element_type=jnp.float32
-    ).astype(jnp.bfloat16)
-    gateup_low = gateup_local.astype(jnp.bfloat16).reshape(-1, 2 * hidden_units)
-    down_low = down_local.astype(jnp.bfloat16).reshape(-1, width)
-    unit = gateup_low.shape[0] // 192
-    down_cut = down_low.shape[0] // 64 * 43
-    parts = [
-        (gateup_low[: 40 * unit],),
-        (gateup_low[40 * unit : 112 * unit],),
-        (gateup_low[112 * unit : 183 * unit],),
-        (gateup_low[183 * unit :], down_low[:down_cut]),
-        (down_low[down_cut:],),
-    ]
     attended_grad = jnp.einsum(
         "td,cd->tc", attn_grad_low, full_out, preferred_element_type=jnp.float32
     ).astype(jnp.bfloat16)
-    sums = [lax.psum(parts[0], "dp")]
-    attended_grad, moe_part, sums, parts = lax.optimization_barrier(
-        (attended_grad, moe_part, sums, parts)
-    )
-    for part in parts[1:]:
-        part, sums[-1] = lax.optimization_barrier((part, sums[-1]))
-        sums.append(lax.psum(part, "dp"))
-    gateup_grad = jnp.concatenate([sums[0][0], sums[1][0], sums[2][0], sums[3][0]], axis=0)
-    gateup_grad = gateup_grad.astype(jnp.float32).reshape(gate_up.shape)
-    down_grad = jnp.concatenate([sums[3][1], sums[4][0]], axis=0)
-    down_grad = down_grad.astype(jnp.float32).reshape(down_proj.shape)
-
-    def by_piece(values):
-        turned = values.T.reshape(dp_count, owner_count, piece_rows, tok_rows)
-        return turned.transpose(1, 0, 2, 3).reshape(width, tok_rows)
-
+    attended_grad, moe_part, parts = lax.optimization_barrier((attended_grad, moe_part, parts))
+    moe_rows = lax.psum_scatter(moe_part, "expert", scatter_dimension=0, tiled=True)
     query_grad_low, prompt_key_part, prompt_value_part, tail_key_part, tail_value_part = (
         attend_back(
             place, projected, attended_grad, prompt_pairs, tail_pairs, stats, cosines, sines
         )
     )
-    moe_rows = lax.psum_scatter(moe_part, "expert", scatter_dimension=0, tiled=True)
-    moe_rows, prompt_key_part = lax.optimization_barrier((moe_rows, prompt_key_part))
-    prompt_grad = lax.psum_scatter(
-        jnp.concatenate([prompt_key_part, prompt_value_part], axis=1),
-        "expert",
-        scatter_dimension=0,
-        tiled=True,
-    )
-    layer_out = (mixed_rows + RESIDUAL * moe_rows.astype(jnp.float32)).astype(jnp.bfloat16)
-    prompt_grad = prompt_grad.astype(jnp.float32)
-    tail_part = jnp.concatenate([tail_key_part, tail_value_part], axis=1)
-    behind = [(source + 1, source) for source in range(0, owner_count, 2)]
-    tail_grad = tail_part[half_rows:] + lax.ppermute(
-        tail_part[:half_rows].astype(jnp.bfloat16), "expert", behind
-    ).astype(jnp.float32)
-    pair_grad = jnp.concatenate([prompt_grad, tail_grad], axis=0)
-    cosine, sine_part = rotary_tables(position, head_size)
-    key_grad_low = (
-        unrotate(pair_grad[:, :kv_width].reshape(tok_rows, kv_heads, head_size), cosine, sine_part)
-        .reshape(tok_rows, kv_width)
-        .astype(jnp.bfloat16)
-    )
-    value_grad_low = pair_grad[:, kv_width:].astype(jnp.bfloat16)
+    if small_plane:
+        pair_grad_low = return_pairs(
+            prompt_key_part, prompt_value_part, tail_key_part, tail_value_part, cosines, sines
+        )
+    else:
+        prompt_grad = lax.psum_scatter(
+            jnp.concatenate([prompt_key_part, prompt_value_part], axis=1),
+            "expert",
+            scatter_dimension=0,
+            tiled=True,
+        ).astype(jnp.float32)
+        tail_part = jnp.concatenate([tail_key_part, tail_value_part], axis=1)
+        behind = [(source + 1, source) for source in range(0, owner_count, 2)]
+        tail_grad = tail_part[half_rows:] + lax.ppermute(
+            tail_part[:half_rows].astype(jnp.bfloat16), "expert", behind
+        ).astype(jnp.float32)
+        pair_grad = jnp.concatenate([prompt_grad, tail_grad], axis=0)
+        cosine, sine_part = rotary_tables(position, head_size)
+        key_grad = unrotate(
+            pair_grad[:, :kv_width].reshape(tok_rows, kv_heads, head_size), cosine, sine_part
+        ).reshape(tok_rows, kv_width)
+        pair_grad_low = jnp.concatenate(
+            [key_grad, pair_grad[:, kv_width:]], axis=1
+        ).astype(jnp.bfloat16)
     all_grad = jnp.concatenate(
         [
             query_grad_low,
-            key_grad_low,
-            value_grad_low,
+            pair_grad_low,
             jnp.pad(logit_grad, ((0, 0), (0, 128 - expert_total))),
         ],
         axis=1,
@@ -758,21 +1654,39 @@
     input_part, gain_one_local = norm_backward(inputs, inverse_one, gain_one, normed_grad)
     input_grad = (mixed_grad_total + input_part).astype(jnp.bfloat16)
 
-    def summed(pieces):
-        pieces = lax.psum_scatter(pieces, "expert", scatter_dimension=0, tiled=True)
-        pieces = lax.psum_scatter(pieces, "dp", scatter_dimension=0, tiled=True)
-        return lax.all_gather(pieces, "expert", axis=0, tiled=True).astype(jnp.float32)
-
     extra = jnp.stack([gain_one_local, gain_two_local], axis=1)
     extra = extra.reshape(dp_count, owner_count, piece_rows, 2).transpose(1, 0, 2, 3)
     extra = jnp.pad(
         extra.reshape(width, 2), ((0, 0), (expert_total, 126 - expert_total))
     )
-    late = summed(
-        dense_weight_grads(
-            by_piece(normed), by_piece(ffn_low), by_piece(att_low), all_grad, attn_grad_low, extra
-        )
-    )
+    extra, moe_rows, sums = lax.optimization_barrier((extra, moe_rows, sums))
+    sums = next_sum(parts[2], sums)
+    layer_out = (mixed_rows + RESIDUAL * moe_rows.astype(jnp.float32)).astype(jnp.bfloat16)
+    late_local = dense_weight_grads(
+        normed_across, ffn_across, att_across, all_grad, attn_grad_low, extra
+    )
+    act_second, late_local = lax.optimization_barrier((acted_low[1], late_local))
+    late = lax.psum_scatter(late_local, "expert", scatter_dimension=0, tiled=True)
+    second_low = down_part(act_second)
+    if small_plane:
+        chunks = second_low.reshape(8, hidden_units // 8, width)
+        second_sum = line_sum(dp_count, 6, chunks).reshape(hidden_units, width)
+    else:
+        second_sum = lax.psum(second_low, "dp").astype(jnp.float32)
+    late, sums, second_sum = lax.optimization_barrier((late, sums, second_sum))
+    sums = next_sum(parts[3], sums)
+    if small_plane:
+        late = line_scatter(late)
+    else:
+        late = lax.psum_scatter(late, "dp", scatter_dimension=0, tiled=True)
+    late = lax.all_gather(late, "expert", axis=0, tiled=True).astype(jnp.float32)
+    gateup_grad = jnp.stack(
+        [
+            jnp.concatenate([sums[0][0], sums[1][0]], axis=0),
+            jnp.concatenate([sums[1][1], sums[2][0], sums[3][0]], axis=0),
+        ]
+    ).astype(jnp.float32)
+    down_grad = jnp.stack([sums[3][1].astype(jnp.float32), second_sum])
     dense_grads = (
         late[:, extra_at + expert_total],
         late[:, :q_width],

time: 920 us -> 767 us (0.83)
  waiting for transfers between devices: 466 us -> 107 us
  Pallas kernels: 158 us -> 458 us
  blocking collectives: 65.9 us -> 0 us
  local copies, waits for them, and re-layouts: 81.2 us -> 62.3 us
    pallas_call x1 -> x7, Pallas kernels: 65 us -> 361 us  [the longest x1 107 us: line_sum(): pl.pallas_call(functools.partial(line_sum_kernel, count), in_specs=[pl.Bl...]
    reduce_scatter x3 -> x1, waiting for transfers between devices: 120 us -> 0.03 us  [on_device(): lax.psum_scatter(late_local, 'expert', scatter_dimension=0, tiled=True)]
    all_gather x5 -> x2, waiting for transfers between devices: 118 us -> 0.01 us  [the longest x1 0.01 us: on_device(): out_piece = lax.all_gather(out_piece, 'expert', axis=0, tiled=True)]
    all_gather x3 -> x0, blocking collectives: 65.9 us -> none  [the longest x2 50.5 us: whole_of(): piece = lax.all_gather(piece, 'dp', axis=0, tiled=True)]
    psum x4 -> x3, waiting for transfers between devices: 117 us -> 62.3 us  [next_sum(): return [*sums[:-1], last, lax.psum(part, 'dp')]]
    psum x1, waiting for transfers between devices: 49.7 us -> 13.2 us  [on_device(): sums = [lax.psum(parts[0], 'dp')]]
    reduce_scatter x1, waiting for transfers between devices: 30.8 us -> 3.48 us  [on_device(): lax.psum_scatter(moe_part, 'expert', scatter_dimension=0, tiled=True)]
    all_gather x1, waiting for transfers between devices: 28.8 us -> 12.1 us  [on_device(): grad_all = lax.all_gather(grad_out, 'expert', axis=0, tiled=True)]
  transfers between devices with their start and end apart: 19 -> 11, of which waited for: 14 -> 6; matrix products, arithmetic and copies ran while one was open for 19% -> 16% of each run, Pallas kernels for 10% -> 49%
where the time goes in v2:
time: 767 us; the launch traced here: 757 us
  Pallas kernels  458 us (60%)
  waiting for transfers between devices  107 us (14%)
  matrix products  70 us (9%)
  local copies, waits for them, and re-layouts  62.3 us (8%)
  other arithmetic  42.7 us (6%)
  between operations  16.5 us (2%)
    pallas_call x1, Pallas kernels, line_sum(): pl.pallas_call(functools.partial(line_sum_kernel, count), in_specs=[pl.Bl...  107 us
    pallas_call x1, Pallas kernels, gathering_experts(): pl.pallas_call(gathering_experts_kernel, in_specs=[anywhere, anywhere, re...  87.8 us
    psum x3, waiting for transfers between devices, next_sum(): return [*sums[:-1], last, lax.psum(part, 'dp')]  62.3 us
    pallas_call x1, Pallas kernels, gather_weights(): pl.pallas_call(gather_weights_kernel, in_specs=[anywhere] * 4, out_specs=...  59.3 us
    pallas_call x1, Pallas kernels, line_scatter(): pl.pallas_call(line_scatter_kernel, in_specs=[pl.BlockSpec(memory_space=p...  50.1 us
    dot_general x4, matrix products, summed_over_tokens(): lax.dot_general(left, right, over_tokens, preferred_element_type=jnp.floa...  49.1 us
    pallas_call x1, Pallas kernels, attend_back(): pl.pallas_call(attend_back_kernel, grid=(pairs,), in_specs=[pl.BlockSpec(...  42.9 us
    unnamed x109, local copies, waits for them, and re-layouts  28.3 us
  transfers between devices with their start and end apart: 11, of which 6 were waited for; matrix products, arithmetic and copies ran while one was open for 16% of the time, Pallas kernels for 49%

profile of v2, /device:TPU:0, one launch (start us, length us, event | category | flops | bytes accessed | tf_op | source)
XLA Modules:
  0.0 756.9 jit_solution(7630518076065230595)
XLA Ops:
  11.6 1.3 copy-done.7
  12.9 1.3 copy-done.8
  16.2 59.3 %gather_weights.1 = (bf16[1536,2560]{1,0:T(8,128)(2,1)S(1)}, bf16[192,1536]{1,0:T(8,128)(2,1)}) custom-call(bf16[384,1536]{1,0:T(8,128)(2,1)S(1)} %copy-done.7, bf16[384,512]{1,0:T(8,128)(2,1)S(1)} %copy-done.13, bf16[384,512]{1,0:T(8,128)(2,1)S(1)} %copy-done.14, bf16[384,1536]{1,0:T(8,128)(2,1)S(1)} %copy-done.8), custom_call_target="tpu_custom_call" | custom-call | bytes 15728640 | tf_op jit(solution)/shard_map/gather_weights/pallas_call | solution.py:670
  75.5 3.1 copy-done.2
  80.8 1.3 convert_reduce_fusion
  85.9 1.7 convert_reduce_fusion.1
  89.9 1.4 fusion.22.x_ref
  91.3 11.4 %project.1.rows_hbm.q_ref = bf16[384,2560]{1,0:T(8,128)(2,1)} custom-call(bf16[384,1536]{1,0:T(8,128)(2,1)} %fusion.22.x_ref, bf16[1536,2560]{1,0:T(8,128)(2,1)} %copy-done.2, f32[384,128]{1,0:T(8,128)} %get-tuple-element.181.cos_ref, f32[384,128]{1,0:T(8,128)} %get-tuple-element.182.sin_ref), custom_call_target="tpu_custom_call" | custom-call | flops 3019898880 | bytes 7864320 | tf_op jit(solution)/shard_map/project/pallas_call | solution.py:409
  102.6 1.5 copy-done
  104.2 23.9 %share_pairs.1 = (bf16[1024,1024]{1,0:T(8,128)(2,1)S(1)}, bf16[512,1024]{1,0:T(8,128)(2,1)S(1)}) custom-call(bf16[384,2560]{1,0:T(8,128)(2,1)S(1)} %copy-done), custom_call_target="tpu_custom_call" | custom-call | bytes 4194304 | tf_op jit(solution)/shard_map/share_pairs/pallas_call | solution.py:774
  128.1 1.3 copy-done.1
  130.4 27.6 %attend.1 = (bf16[384,1536]{1,0:T(8,128)(2,1)}, f32[4,384,128]{2,1,0:T(8,128)}) custom-call(s32[3]{0:T(128)} %pad_add_fusion.place_ref, bf16[384,2560]{1,0:T(8,128)(2,1)} %project.1.rows_hbm.q_ref, bf16[1024,1024]{1,0:T(8,128)(2,1)} %copy-done.1, bf16[1024,1024]{1,0:T(8,128)(2,1)} %copy-done.1, bf16[512,1024]{1,0:T(8,128)(2,1)} %copy-done.3, ...), custom_call_target="tpu_custom_call" | custom-call | flops 3623878656 | bytes 3538944 | tf_op jit(solution)/shard_map/attend/pallas_call | solution.py:188
  158.0 1.9 copy.87
  161.1 2.7 copy.79
  163.8 2.2 multiply_reduce_fusion.2
  166.7 1.3 fusion.62
  167.9 2.4 copy.85
  170.3 2.5 copy.86
  172.8 1.3 multiply_convert_fusion.1
  174.1 12.1 %all-gather.6.cloned.1.call-done.g_hbm = bf16[3072,1536]{1,0:T(8,128)(2,1)} async-done(((bf16[384,1536]{1,0:T(8,128)(2,1)}), bf16[3072,1536]{1,0:T(8,128)(2,1)}) %all-gather.6.cloned.1.call-update) | async-done | bytes 9437200 | tf_op jit(solution)/shard_map/all_gather | solution.py:1503
  186.2 2.5 fusion.37.own_hbm
  188.6 87.8 %gathering_experts.1 = (bf16[3072,1664]{1,0:T(8,128)(2,1)}, bf16[2,3072,1024]{2,1,0:T(8,128)(2,1)}, bf16[2,3072,512]{2,1,0:T(8,128)(2,1)}, bf16[3072,1536]{1,0:T(8,128)(2,1)}) custom-call(bf16[384,1664]{1,0:T(8,128)(2,1)} %fusion.37.own_hbm, bf16[3072,1536]{1,0:T(8,128)(2,1)} %all-gather.6.cloned.1.call-done.g_hbm, bf16[2,1536,1024]{2,1,0:T(8,128)(2,1)} %up_ref.1, ...), custom_call_target="tpu_custom_call" | custom-call | flops 48318382080 | bytes 75497472 | tf_op jit(solution)/shard_map/gathering_experts/pallas_call | solution.py:1315
  276.5 14.1 %fusion.7 = bf16[1536,1024]{1,0:T(8,128)(2,1)S(1)} fusion(bf16[3072,1536]{1,0:T(8,128)(2,1)} %get-tuple-element.68, bf16[2,3072,1024]{2,1,0:T(8,128)(2,1)} %get-tuple-element.69), kind=kOutput, calls=%fused_computation.16 | convolution fusion | flops 9665249280 | bytes 18874368 | tf_op jit(solution)/shard_map/dot_general | solution.py:1566
  290.6 1.8 copy-done.23
  292.4 1.4 slice.97
  294.2 14.2 %fusion.10 = bf16[1536,1024]{1,0:T(8,128)(2,1)S(1)} fusion(bf16[3072,1536]{1,0:T(8,128)(2,1)} %get-tuple-element.68, bf16[2,3072,1024]{2,1,0:T(8,128)(2,1)} %get-tuple-element.69), kind=kOutput, calls=%fused_computation.17 | convolution fusion | flops 9665249280 | bytes 18874368 | tf_op jit(solution)/shard_map/dot_general | solution.py:1566
  310.1 1.4 slice.100
  311.5 2.4 slice.98
  313.9 14.3 %moe_shares.1 = bf16[3072,1536]{1,0:T(8,128)(2,1)} custom-call(bf16[2,3072,512]{2,1,0:T(8,128)(2,1)} %get-tuple-element.71.act_ref, bf16[2,512,1536]{2,1,0:T(8,128)(2,1)} %down_ref.3), custom_call_target="tpu_custom_call" | custom-call | flops 4718592 | bytes 4718592 | tf_op jit(solution)/shard_map/moe_shares/pallas_call | solution.py:1364
  328.2 2.0 select_reduce_fusion
  331.7 10.5 %fusion.15 = bf16[512,1536]{1,0:T(8,128)(2,1)} fusion(bf16[3072,1536]{1,0:T(8,128)(2,1)} %all-gather.6.cloned.1.call-done.g_hbm, bf16[2,3072,512]{2,1,0:T(8,128)(2,1)} %get-tuple-element.71.act_ref), kind=kOutput, calls=%fused_computation.27 | convolution fusion | flops 4833411072 | bytes 14155776 | tf_op jit(solution)/shard_map/dot_general | solution.py:1566
  342.1 14.3 %reduce-scatter.4.cloned.1.call-done = bf16[384,1664]{1,0:T(8,128)(2,1)} async-done(((bf16[3072,1664]{1,0:T(8,128)(2,1)}), bf16[384,1664]{1,0:T(8,128)(2,1)}) %reduce-scatter.4.cloned.1.call-update) | async-done | bytes 1277968 | tf_op jit(solution)/shard_map/reduce_scatter | solution.py:1560
  356.4 2.9 convert_element_type.99
  359.4 13.2 %all-reduce.13.cloned.1.call-done = bf16[912,1024]{1,0:T(8,128)(2,1)} async-done(((bf16[912,1024]{1,0:T(8,128)(2,1)}), bf16[912,1024]{1,0:T(8,128)(2,1)}) %all-reduce.13.cloned.1.call-update) | async-done | bytes 1867792 | tf_op jit(solution)/shard_map/psum | solution.py:1589
  372.6 1.5 multiply_reduce_fusion.3
  374.1 1.4 multiply_convert_fusion.2
  375.6 3.3 multiply_reduce_fusion.1
  378.9 1.4 copy-done.17
  382.2 5.4 convolution_convert_fusion.do_ref
  389.8 42.9 %attend_back.1 = (bf16[384,1536]{1,0:T(8,128)(2,1)}, bf16[1024,512]{1,0:T(8,128)(2,1)}, bf16[1024,512]{1,0:T(8,128)(2,1)}, f32[512,512]{1,0:T(8,128)}, f32[512,512]{1,0:T(8,128)}) custom-call(s32[3]{0:T(128)} %pad_add_fusion.place_ref, bf16[384,2560]{1,0:T(8,128)(2,1)} %project.1.rows_hbm.q_ref, bf16[384,1536]{1,0:T(8,128)(2,1)} %convolution_convert_fusion.do_ref, ...), custom_call_target="tpu_custom_call" | custom-call | flops 589824 | bytes 589824 | tf_op jit(solution)/shard_map/attend_back/pallas_call | solution.py:330
  432.6 1.2 copy-done.9
  433.9 1.3 copy-done.10
  435.2 1.3 copy-done.11
  436.4 1.4 copy-done.12
  437.8 18.7 %return_pairs.1 = bf16[384,1024]{1,0:T(8,128)(2,1)S(1)} custom-call(bf16[1024,512]{1,0:T(8,128)(2,1)S(1)} %copy-done.9, bf16[1024,512]{1,0:T(8,128)(2,1)S(1)} %copy-done.10, f32[512,512]{1,0:T(8,128)S(1)} %copy-done.11, f32[512,512]{1,0:T(8,128)S(1)} %copy-done.12, f32[384,128]{1,0:T(8,128)S(1)} %copy-done.4, f32[384,128]{1,0:T(8,128)S(1)} %copy-done.5), custom_call_target="tpu_custom_call" | custom-call | bytes 8388608 | tf_op jit(solution)/shard_map/return_pairs/pallas_call | solution.py:1128
  456.5 8.1 %fusion.31 = (f32[384]{0:T(512)S(1)}, f32[1536]{0:T(1024)S(1)}, f32[384,1536]{1,0:T(8,128)}) fusion(bf16[384,1536]{1,0:T(8,128)(2,1)S(1)} %copy-done.18, f32[1536]{0:T(1024)S(1)} %get-tuple-element.160, f32[384]{0:T(512)S(1)} %copy-done.47, bf16[1536,2560]{1,0:T(8,128)(2,1)} %copy-done.2, bf16[384,1024]{1,0:T(8,128)(2,1)S(1)} %return_pairs.1, ...), kind=kOutput, calls=%fused_computation.43 | convolution fusion | flops 3027957760 | bytes 13384704 | tf_op jit(solution)/shard_map/tc,dc->td/dot_general | solution.py:1648
  466.2 7.7 %all-reduce.19.cloned.1.call-done = (bf16[624,1024]{1,0:T(8,128)(2,1)}, bf16[400,1024]{1,0:T(8,128)(2,1)}) async-done(((bf16[624,1024]{1,0:T(8,128)(2,1)}, bf16[400,1024]{1,0:T(8,128)(2,1)}), (bf16[624,1024]{1,0:T(8,128)(2,1)}, bf16[400,1024]{1,0:T(8,128)(2,1)})) %all-reduce.19.cloned.1.call-update) | async-done | bytes 2097168 | tf_op jit(solution)/shard_map/psum | solution.py:1587
  473.9 3.5 reduce-scatter.6.cloned.1.call-done
  477.5 3.8 slice_bitcast_fusion
  481.3 1.4 fusion.32.right_ref
  482.8 14.9 %dense_weight_grads.1 = bf16[1536,4224]{1,0:T(8,128)(2,1)} custom-call(bf16[1536,384]{1,0:T(8,128)(2,1)} %bitcast.75, bf16[1536,384]{1,0:T(8,128)(2,1)} %bitcast.77, bf16[1536,384]{1,0:T(8,128)(2,1)} %bitcast.76, bf16[384,2688]{1,0:T(8,128)(2,1)} %fusion.32.right_ref, bf16[384,1536]{1,0:T(8,128)(2,1)} %copy-done.22, f32[1536,128]{1,0:T(8,128)} %pad.14.extra_ref), custom_call_target="tpu_custom_call" | custom-call | flops 4982833152 | bytes 12976128 | tf_op jit(solution)/shard_map/dense_weight_grads/pallas_call | solution.py:1407
  497.8 10.3 %fusion.18 = bf16[512,1536]{1,0:T(8,128)(2,1)} fusion(bf16[3072,512]{1,0:T(8,128)(2,1)} %slice_bitcast_fusion, bf16[3072,1536]{1,0:T(8,128)(2,1)} %all-gather.6.cloned.1.call-done.g_hbm), kind=kOutput, calls=%fused_computation.28 | convolution fusion | flops 4833411072 | bytes 14155776 | tf_op jit(solution)/shard_map/dot_general | solution.py:1566
  508.1 106.8 %line_sum.1 = f32[8,64,1536]{2,1,0:T(8,128)} custom-call(bf16[8,64,1536]{2,1,0:T(8,128)(2,1)} %bitcast.86), custom_call_target="tpu_custom_call" | custom-call | bytes 47185920 | tf_op jit(solution)/shard_map/line_sum/pallas_call | solution.py:920
  615.1 1.3 copy-done.6
  616.5 50.1 %line_scatter.1 = bf16[48,4224]{1,0:T(8,128)(2,1)} custom-call(bf16[192,4224]{1,0:T(8,128)(2,1)S(1)} %copy-done.6), custom_call_target="tpu_custom_call" | custom-call | bytes 20275200 | tf_op jit(solution)/shard_map/line_scatter/pallas_call | solution.py:991
  666.7 5.7 fusion.27
  672.7 54.6 %all-reduce.17.cloned.1.call-done = (bf16[208,1024]{1,0:T(8,128)(2,1)}, bf16[1,512,1536]{2,1,0:T(8,128)(2,1)}) async-done(((bf16[208,1024]{1,0:T(8,128)(2,1)}, bf16[1,512,1536]{2,1,0:T(8,128)(2,1)}), (bf16[208,1024]{1,0:T(8,128)(2,1)}, bf16[1,512,1536]{2,1,0:T(8,128)(2,1)})) %all-reduce.17.cloned.1.call-update) | async-done | bytes 1998864 | tf_op jit(solution)/shard_map/psum | solution.py:1587
  727.3 2.0 stack.53
  730.0 1.5 copy-done.19
  731.5 3.1 pad_maximum_fusion
  734.6 5.6 maximum_convert_fusion
  741.8 2.5 convert_element_type.110
  745.2 1.3 fusion.49
  746.6 2.8 fusion.48
  (167 shorter events, 29.7 us)
Async XLA Ops:
  8.0 77.9 %all-reduce.11.cloned.1.call-start = ((), (), s32[]{:S(2)}) async-start(), calls=%async_computation.3 | async-start | bytes 786432 | tf_op jit(solution)/shard_map/psum | solution.py:1495
  10.8 0.7 copy-start.27
  11.6 149.5 %all-gather.4.cloned.1.call-start = ((), (), s32[]{:S(2)}) async-start(), calls=%async_computation.4 | async-start | bytes 5308416 | tf_op jit(solution)/shard_map/all_gather | solution.py:1485
  11.6 1.3 copy-start.7
  12.9 1.3 copy-start.8
  14.2 1.0 copy-start.13
  15.2 1.0 copy-start.14
  16.2 63.6 %copy-start.51 = (s32[1,3072]{1,0:T(1,128)S(1)}, s32[1,3072]{1,0:T(1,128)}, u32[]{:S(2)}) copy-start(s32[1,3072]{1,0:T(1,128)} %param.25) | copy-start | bytes 36868
  16.2 64.4 %copy-start.52 = (s32[384,8]{0,1:T(8,128)S(1)}, s32[384,8]{0,1:T(8,128)}, u32[]{:S(2)}) copy-start(s32[384,8]{0,1:T(8,128)} %param.24) | copy-start | bytes 36868
  75.5 3.1 copy-start.2
  78.5 6.4 copy-start.18
  78.5 107.6 %all-gather.6.cloned.1.call-start = ((), (), s32[]{:S(2)}) async-start(), calls=%async_computation.5 | async-start | bytes 10616832 | tf_op jit(solution)/shard_map/all_gather | solution.py:1503
  79.1 277.3 %reduce-scatter.4.cloned.1.call-start = ((), (), s32[]{:S(2)}) async-start(), calls=%async_computation.6 | async-start | bytes 11501568 | tf_op jit(solution)/shard_map/reduce_scatter | solution.py:1560
  80.8 6.7 copy-start.39
  82.3 5.3 copy-start.36
  85.2 2.4 copy-start.45
  88.7 1.2 copy-start.46
  102.6 1.5 copy-start
  128.1 1.3 copy-start.1
  129.4 1.0 copy-start.3
  161.1 2.8 copy-start.29
  163.8 2.2 copy-start.21
  166.0 212.9 %copy-start.15 = (f32[384,1536]{1,0:T(8,128)}, f32[384,1536]{1,0:T(8,128)S(1)}, u32[]{:S(2)}) copy-start(f32[384,1536]{1,0:T(8,128)S(1)} %get-tuple-element.177) | copy-start | bytes 7077892
  166.0 0.6 copy-start.40
  170.3 2.5 copy-start.41
  276.5 96.1 %all-reduce.13.cloned.1.call-start = ((), (), s32[]{:S(2)}) async-start(), calls=%async_computation.7 | async-start | bytes 3735552 | tf_op jit(solution)/shard_map/psum | solution.py:1589
  290.6 1.8 copy-start.23
  293.7 180.1 %all-reduce.19.cloned.1.call-start = ((), (), s32[]{:S(2)}) async-start(), calls=%async_computation.13 | async-start | bytes 4194304 | tf_op jit(solution)/shard_map/psum | solution.py:1587
  330.2 0.7 copy-start.26
  330.2 0.7 copy-start.37
  330.2 0.7 copy-start.48
  375.5 3.4 copy-start.32
  375.5 4.8 copy-start.20
  375.5 4.8 copy-start.42
  378.9 1.4 copy-start.17
  378.9 2.3 copy-start.49
  381.2 1.0 copy-start.22
  387.6 1.1 copy-start.35
  387.6 2.0 copy-start.44
  387.7 89.7 %reduce-scatter.6.cloned.1.call-start = ((), (), s32[]{:S(2)}) async-start(), calls=%async_computation.8 | async-start | bytes 10616832 | tf_op jit(solution)/shard_map/reduce_scatter | solution.py:1610
  388.4 226.6 %all-reduce.15.cloned.1.call-start = ((), (), s32[]{:S(2)}) async-start(), calls=%async_computation.10 | async-start | bytes 3801088 | tf_op jit(solution)/shard_map/psum | solution.py:1587
  389.7 42.9 %copy-start.4 = (f32[384,128]{1,0:T(8,128)S(1)}, f32[384,128]{1,0:T(8,128)}, u32[]{:S(2)}) copy-start(f32[384,128]{1,0:T(8,128)} %get-tuple-element.181.cos_ref) | copy-start | bytes 589828
  389.7 42.9 %copy-start.5 = (f32[384,128]{1,0:T(8,128)S(1)}, f32[384,128]{1,0:T(8,128)}, u32[]{:S(2)}) copy-start(f32[384,128]{1,0:T(8,128)} %get-tuple-element.182.sin_ref) | copy-start | bytes 589828
  432.6 1.2 copy-start.9
  433.9 1.3 copy-start.10
  435.2 1.3 copy-start.11
  436.4 1.4 copy-start.12
  437.8 18.7 %copy-start.30 = (bf16[384,1536]{1,0:T(8,128)(2,1)S(1)}, bf16[384,1536]{1,0:T(8,128)(2,1)}, u32[]{:S(2)}) copy-start(bf16[384,1536]{1,0:T(8,128)(2,1)} %get-tuple-element.74) | copy-start | bytes 3538948
  437.8 18.7 %copy-start.47 = (f32[384]{0:T(512)S(1)}, f32[384]{0:T(512)}, u32[]{:S(2)}) copy-start(f32[384]{0:T(512)} %copy-done.45) | copy-start | bytes 4612
  477.4 3.9 copy-start.31
  477.4 3.9 copy-start.33
  477.4 137.6 %reduce-scatter.8.cloned.1.call-start = ((), (), s32[]{:S(2)}) async-start(), calls=%async_computation.9 | async-start | bytes 14598144 | tf_op jit(solution)/shard_map/reduce_scatter | solution.py:1669
  497.7 229.6 %all-reduce.17.cloned.1.call-start = ((), (), s32[]{:S(2)}) async-start(), calls=%async_computation.12 | async-start | bytes 3997696 | tf_op jit(solution)/shard_map/psum | solution.py:1587
  615.0 51.7 %copy-start.43 = (f32[384]{0:T(512)S(1)}, f32[384]{0:T(512)}, u32[]{:S(2)}) copy-start(f32[384]{0:T(512)} %copy-done.40) | copy-start | bytes 4612
  615.0 51.7 %copy-start.50 = (f32[384]{0:T(512)S(1)}, f32[384]{0:T(512)}, u32[]{:S(2)}) copy-start(f32[384]{0:T(512)} %copy-done.49) | copy-start | bytes 4612
  615.0 1.4 copy-start.6
  615.1 125.1 %all-gather.8.cloned.1.call-start = ((), (), s32[]{:S(2)}) async-start(), calls=%async_computation.11 | async-start | bytes 3649536 | tf_op jit(solution)/shard_map/all_gather | solution.py:1682
  666.6 5.7 copy-start.25
  666.7 5.7 copy-start.28
  727.3 2.0 copy-start.24
  727.3 2.2 copy-start.34
  727.3 2.3 copy-start.38
  729.6 1.9 copy-start.19
  741.8 3.4 copy-start.16
Sparse Core Ops, SparseCore 0:
  11.8 54.4 all-reduce.10
  293.9 78.6 all-reduce.12
  387.8 86.0 all-reduce.18
  477.5 100.6 all-reduce.14
  615.2 112.0 all-reduce.16
Sparse Core Ops, SparseCore 1:
  78.6 44.7 all-gather.3
  125.3 60.8 all-gather.5
  276.5 79.8 reduce-scatter.3
  392.5 84.8 reduce-scatter.5
  497.8 94.6 reduce-scatter.7
  666.7 50.7 all-gather.7
